TPU v7x, 512 devices: a whole 4x8x8 slice. The times are simulated.
512 devices in a mesh: leaf: 64 (over y, z_lo, core), node: 8 (over z_hi, x).
Axes of the slice: x: 4, y: 8, z: 8 (z_hi: 2, z_lo: 4; z = z_hi * 4 + z_lo), core: 2. Of those that a mesh axis runs over, the one named last changes fastest.
Arguments:
- leaf_rhs: bfloat16 [64, 512, 128], P('leaf', 'node'), may hold values from -6 to 6
- leaf_inverse: bfloat16 [64, 512, 8192], P('leaf', 'node'), as said below
- leaf_update: bfloat16 [64, 1536, 512], P('leaf', None, 'node'), may hold values from -0.0625 to 0.0625
- root_tiles: int32 [4, 12], replicated, may hold values from 0 to 23, all different within a row
- leaf_dinv: float32 [64, 512], P('leaf', 'node'), may hold values from 0.5 to 2
- leaf_doff: float32 [64, 256], P('leaf', 'node'), may hold values from -0.5 to 0.5
- leaf_pairs: int32 [64, 256], P('leaf', 'node'), may hold values 0 or 1
- root_rhs: bfloat16 [3072, 128], P(('leaf', 'node')), may hold values from -6 to 6
- root_inverse: bfloat16 [3072, 3072], P(('leaf', 'node')), as said below
- root_dinv: float32 [3072], P(('leaf', 'node')), may hold values from 0.5 to 2
- root_doff: float32 [1536], P(('leaf', 'node')), may hold values from -0.5 to 0.5
- root_pairs: int32 [1536], P(('leaf', 'node')), may hold values 0 or 1
Outputs:
- leaf_solution: bfloat16 [64, 512, 128], P('leaf', 'node')
- root_solution: bfloat16 [3072, 128], P(('leaf', 'node'))
Inputs may be any that keep to these rules, and one draw needn't show every extreme that they name: `leaf_inverse`: the 16 row blocks of each leaf, stacked, form Q M transpose(Q) for a permutation matrix Q and a unit lower triangular matrix M. root_inverse is unit lower triangular. `root_tiles`: the 12 tiles of one leaf are distinct, and every root tile is named by some leaf.
All inputs are finite; a program needn't handle non-finite values. No bound on the sum of `leaf_pairs` or of `root_pairs` on one device may be relied on, other than what follows from the above.
Results may differ from a plain program's by a relative error of at most 0.013.
Values may be sent and summed in bfloat16 or wider, within the bound.
No kernel may reach another device: no remote copies, remote signals or barrier semaphores. Data moves between devices by JAX's collectives and lax.ppermute only.
A program may use at most 64 MiB of HBM per device.

v0:
```python
import jax
import jax.numpy as jnp
from jax import lax
from jax.sharding import PartitionSpec as P

LEAVES = 4
ROOT_TILES = 24


tile_rows = 128


def partner(value, axis, apart):
    mask = 2**apart
    pairs = [(source, source ^ mask) for source in range(lax.axis_size(axis))]
    return lax.ppermute(value, axis, pairs)


def pivot_solve(values, diagonal, coupling, pairs):
    length = values.shape[0]
    halves = values.reshape(length // 2, 2, values.shape[1])
    diag_two = diagonal.reshape(length // 2, 2)
    joined = (coupling * pairs.astype(jnp.float32))[:, None]
    first_row = diag_two[:, 0:1] * halves[:, 0, :] + joined * halves[:, 1, :]
    second_row = joined * halves[:, 0, :] + diag_two[:, 1:2] * halves[:, 1, :]
    return jnp.stack([first_row, second_row], axis=1).reshape(length, values.shape[1])


def transposed_product(matrix, vector):
    return lax.dot_general(
        matrix, vector, (((0,), (0,)), ((), ())), preferred_element_type=jnp.float32
    )


def on_device(
    leaf_rhs,
    leaf_inverse,
    leaf_update,
    root_tiles,
    leaf_dinv,
    leaf_doff,
    leaf_pairs,
    root_rhs,
    root_inverse,
    root_dinv,
    root_doff,
    root_pairs,
):
    factor_rows = leaf_inverse[0]
    local_rows = factor_rows.shape[0]
    rhs_count = leaf_rhs.shape[2]
    root_local = root_rhs.shape[0]
    group_size = lax.axis_size("leaf") // LEAVES
    node_count = lax.axis_size("node")
    bit_count = group_size.bit_length() - 1
    leaf_index = lax.axis_index("leaf")
    group_member = leaf_index % group_size
    leaf_owner = leaf_index // group_size
    block_rows = node_count * local_rows
    holding = lax.all_gather(leaf_rhs[0], "node", axis=0, tiled=True)
    block_start = group_member * block_rows
    own_columns = lax.dynamic_slice_in_dim(factor_rows, block_start, block_rows, 1)
    product_sum = jnp.dot(own_columns, holding, preferred_element_type=jnp.float32)
    for bit_number in range(bit_count):
        partner_rows = partner(holding, "leaf", bit_number)
        span_rows = holding.shape[0]
        partner_start = (group_member >> bit_number ^ 1) * span_rows
        columns = lax.dynamic_slice_in_dim(factor_rows, partner_start, span_rows, 1)
        product_sum = product_sum + jnp.dot(
            columns, partner_rows, preferred_element_type=jnp.float32
        )
        if bit_number + 1 < bit_count:
            low_side = group_member >> bit_number & 1 == 0
            holding = jnp.where(
                low_side,
                jnp.concatenate([holding, partner_rows], 0),
                jnp.concatenate([partner_rows, holding], 0),
            )
    leaf_forward = product_sum.astype(jnp.bfloat16)
    update_rows = leaf_update[0]
    tile_ids = lax.dynamic_index_in_dim(root_tiles, leaf_owner, 0, keepdims=False)
    tile_count = tile_ids.shape[0]
    onehot = (jnp.arange(ROOT_TILES, dtype=jnp.int32)[:, None] == tile_ids[None, :]).astype(
        jnp.float32
    )
    update_term = jnp.dot(update_rows, leaf_forward, preferred_element_type=jnp.float32)
    scattered = jnp.einsum(
        "tk,kar->tar",
        onehot,
        update_term.reshape(tile_count, tile_rows, rhs_count),
        precision=lax.Precision.HIGHEST,
    )
    scattered = scattered.reshape(ROOT_TILES * tile_rows, rhs_count)
    offset = lax.axis_index(("leaf", "node")) * root_local
    own_rows = lax.dynamic_update_slice_in_dim(
        jnp.zeros_like(scattered), root_rhs.astype(jnp.float32), offset, 0
    )
    merged = lax.psum(own_rows - scattered, ("leaf", "node")).astype(jnp.bfloat16)
    root_forward = jnp.dot(root_inverse, merged, preferred_element_type=jnp.float32)
    root_scaled = pivot_solve(root_forward, root_dinv, root_doff, root_pairs).astype(jnp.bfloat16)
    full_term = transposed_product(root_inverse, root_scaled)
    root_full = lax.psum(full_term, ("leaf", "node")).astype(jnp.bfloat16)
    own_offset = lax.axis_index(("leaf", "node")) * root_local
    root_own = lax.dynamic_slice_in_dim(root_full, own_offset, root_local, 0)
    tile_values = jnp.einsum(
        "tk,tar->kar",
        onehot.astype(jnp.bfloat16),
        root_full.reshape(ROOT_TILES, tile_rows, rhs_count),
        preferred_element_type=jnp.float32,
    )
    tile_values = tile_values.astype(jnp.bfloat16).reshape(tile_count * tile_rows, rhs_count)
    coupling_term = transposed_product(update_rows, tile_values)
    leaf_scaled = pivot_solve(
        leaf_forward.astype(jnp.float32), leaf_dinv[0], leaf_doff[0], leaf_pairs[0]
    )
    leaf_vector = (leaf_scaled - coupling_term).astype(jnp.bfloat16)
    back_term = transposed_product(factor_rows, leaf_vector)
    for bit_number in reversed(range(bit_count)):
        half_rows = back_term.shape[0] // 2
        lower_rows = back_term[:half_rows]
        upper_rows = back_term[half_rows:]
        high_side = group_member >> bit_number & 1 == 1
        outgoing = jnp.where(high_side, lower_rows, upper_rows)
        keeping = jnp.where(high_side, upper_rows, lower_rows)
        back_term = keeping + partner(outgoing.astype(jnp.bfloat16), "leaf", bit_number).astype(
            outgoing.dtype
        )
    leaf_solution = lax.psum_scatter(
        back_term.astype(jnp.bfloat16), "node", scatter_dimension=0, tiled=True
    )
    return (leaf_solution[None], root_own)


def solution(mesh):
    in_specs = (
        P("leaf", "node", None),
        P("leaf", "node", None),
        P("leaf", None, "node"),
        P(),
        P("leaf", "node"),
        P("leaf", "node"),
        P("leaf", "node"),
        P(("leaf", "node"), None),
        P(("leaf", "node"), None),
        P(("leaf", "node")),
        P(("leaf", "node")),
        P(("leaf", "node")),
    )
    out_specs = (P("leaf", "node", None), P(("leaf", "node"), None))
    return jax.shard_map(
        on_device, mesh=mesh, in_specs=in_specs, out_specs=out_specs, check_vma=False
    )
```

profile of v0, /device:TPU:1, one launch (start us, length us, event | category | flops | bytes accessed | tf_op | source)
XLA Modules:
  0.0 515.8 jit_solution(18070194130903692981)
XLA Ops:
  7.2 42.6 %all-gather = bf16[1,512,128]{2,1,0:T(8,128)(2,1)S(1)} all-gather(bf16[1,64,128]{2,1,0:T(8,128)(2,1)} %param.12), channel_id=2, replica_groups=mesh['leaf'=64,'node'=8] {'node'}, dimensions={1}, use_global_device_ids=true | all-gather | bytes 147456 | tf_op jit(solution)/shard_map/all_gather | solution.py:60
  49.8 10.3 %collective-permute-start = (bf16[512,128]{1,0:T(8,128)(2,1)S(1)}, bf16[512,128]{1,0:T(8,128)(2,1)S(1)}, u32[]{:S(2)}, u32[]{:S(2)}) collective-permute-start(bf16[512,128]{1,0:T(8,128)(2,1)S(1)} %bitcast.81), channel_id=1, source_target_pairs={{0,8},{8,0},{16,24},{24,16},{32,40},{40,32},{48,56},{56,48},{64,72... | collective-permute-start | bytes 393224 | tf_op jit(solution)/shard_map/ppermute | solution.py:16
  61.2 1.9 collective-permute-start.1
  63.1 7.5 %collective-permute-done.1 = bf16[1024,128]{1,0:T(8,128)(2,1)S(1)} collective-permute-done((bf16[1024,128]{1,0:T(8,128)(2,1)S(1)}, bf16[1024,128]{1,0:T(8,128)(2,1)S(1)}, u32[]{:S(2)}, u32[]{:S(2)}) %collective-permute-start.1) | collective-permute-done | bytes 262176 | tf_op jit(solution)/shard_map/ppermute | solution.py:16
  70.7 2.6 collective-permute-start.2
  74.9 1.2 multiply_bitcast_fusion
  76.1 22.4 %collective-permute-done.2 = bf16[2048,128]{1,0:T(8,128)(2,1)S(1)} collective-permute-done((bf16[2048,128]{1,0:T(8,128)(2,1)S(1)}, bf16[2048,128]{1,0:T(8,128)(2,1)S(1)}, u32[]{:S(2)}, u32[]{:S(2)}) %collective-permute-start.2) | collective-permute-done | bytes 524320 | tf_op jit(solution)/shard_map/ppermute | solution.py:16
  98.5 1.2 maximum_select_fusion
  99.8 1.9 collective-permute-start.3
  101.7 1.2 fusion.38
  107.7 18.5 %collective-permute-done.3 = bf16[4096,128]{1,0:T(8,128)(2,1)} collective-permute-done((bf16[4096,128]{1,0:T(8,128)(2,1)}, bf16[4096,128]{1,0:T(8,128)(2,1)}, u32[]{:S(2)}, u32[]{:S(2)}) %collective-permute-start.3) | collective-permute-done | bytes 1048608 | tf_op jit(solution)/shard_map/ppermute | solution.py:16
  126.2 1.5 fusion.10
  127.9 1.2 convolution_bitcast_fusion.2
  129.1 1.4 copy.25
  130.5 1.2 fusion.7
  132.1 1.3 bitcast_subtract_fusion
  133.4 106.1 %all-reduce.2 = bf16[3072,128]{1,0:T(8,128)(2,1)S(1)} all-reduce(f32[3072,128]{1,0:T(8,128)} %bitcast_subtract_fusion), channel_id=1, replica_groups=mesh['leaf'=64,'node'=8] {'leaf','node'}, use_global_device_ids=true, to_apply=%region_0.1 | all-reduce | flops 393216 | bytes 2359296 | tf_op jit(solution)/shard_map/psum | solution.py:98
  240.3 101.8 %all-reduce.3 = bf16[3072,128]{0,1:T(8,128)(2,1)S(1)} all-reduce(f32[3072,128]{0,1:T(8,128)S(1)} %convolution_bitcast_fusion.1), channel_id=1, replica_groups=mesh['leaf'=64,'node'=8] {'leaf','node'}, use_global_device_ids=true, to_apply=%region_1.2 | all-reduce | flops 393216 | bytes 2359296 | tf_op jit(solution)/shard_map/psum | solution.py:102
  343.9 2.9 convolution_bitcast_fusion
  346.8 2.4 select_convert_fusion
  349.2 3.4 collective-permute-start.4
  352.6 23.7 %collective-permute-done.4 = bf16[4096,128]{0,1:T(8,128)(2,1)} collective-permute-done((bf16[4096,128]{0,1:T(8,128)(2,1)S(1)}, bf16[4096,128]{0,1:T(8,128)(2,1)}, u32[]{:S(2)}, u32[]{:S(2)}) %collective-permute-start.4) | collective-permute-done | bytes 1048608 | tf_op jit(solution)/shard_map/ppermute | solution.py:16
  376.4 2.8 convert_add_fusion
  380.1 2.0 collective-permute-start.5
  382.1 26.2 %collective-permute-done.5 = bf16[2048,128]{0,1:T(8,128)(2,1)} collective-permute-done((bf16[2048,128]{0,1:T(8,128)(2,1)}, bf16[2048,128]{0,1:T(8,128)(2,1)}, u32[]{:S(2)}, u32[]{:S(2)}) %collective-permute-start.5) | collective-permute-done | bytes 524320 | tf_op jit(solution)/shard_map/ppermute | solution.py:16
  408.2 1.2 convert_add_fusion.1
  410.5 1.9 collective-permute-start.6
  412.4 7.4 %collective-permute-done.6 = bf16[1024,128]{0,1:T(8,128)(2,1)S(1)} collective-permute-done((bf16[1024,128]{0,1:T(8,128)(2,1)S(1)}, bf16[1024,128]{0,1:T(8,128)(2,1)S(1)}, u32[]{:S(2)}, u32[]{:S(2)}) %collective-permute-start.6) | collective-permute-done | bytes 262176 | tf_op jit(solution)/shard_map/ppermute | solution.py:16
  419.7 1.3 convert_add_fusion.2
  421.1 3.2 collective-permute-start.7
  424.3 1.0 collective-permute-done.7
  427.7 79.7 %reduce-scatter.4.cloned.1.call-done = bf16[64,128]{1,0:T(8,128)(2,1)} async-done(((bf16[512,128]{1,0:T(8,128)(2,1)}), bf16[64,128]{1,0:T(8,128)(2,1)}) %reduce-scatter.4.cloned.1.call-update) | async-done | bytes 16400
  (74 shorter events, 16.3 us)
Async XLA Ops:
  7.2 99.9 %copy-start = (bf16[1,64,8192]{2,1,0:T(8,128)(2,1)S(1)}, bf16[1,64,8192]{2,1,0:T(8,128)(2,1)}, u32[]{:S(2)}) copy-start(bf16[1,64,8192]{2,1,0:T(8,128)(2,1)} %param.13) | copy-start | bytes 3145732
  7.2 95.7 %copy-start.10 = (bf16[6,128]{1,0:T(8,128)(2,1)S(1)}, bf16[6,128]{1,0:T(8,128)(2,1)}, u32[]{:S(2)}) copy-start(bf16[6,128]{1,0:T(8,128)(2,1)} %param.19) | copy-start | bytes 4612
  7.2 96.8 %copy-start.15 = (f32[1,64]{1,0:T(1,128)S(1)}, f32[1,64]{1,0:T(1,128)}, u32[]{:S(2)}) copy-start(f32[1,64]{1,0:T(1,128)} %param.16) | copy-start | bytes 772
  7.2 500.2 %reduce-scatter.4.cloned.1.call-start = ((), (), s32[]{:S(2)}) async-start(), calls=%async_computation.1 | async-start | bytes 147456
  49.8 11.3 %collective-permute-start = (bf16[512,128]{1,0:T(8,128)(2,1)S(1)}, bf16[512,128]{1,0:T(8,128)(2,1)S(1)}, u32[]{:S(2)}, u32[]{:S(2)}) collective-permute-start(bf16[512,128]{1,0:T(8,128)(2,1)S(1)} %bitcast.81), channel_id=1, source_target_pairs={{0,8},{8,0},{16,24},{24,16},{32,40},{40,32},{48,56},{56,48},{64,72... | collective-permute-start | bytes 393224 | tf_op jit(solution)/shard_map/ppermute | solution.py:16
  61.1 2.0 copy-start.5
  61.2 9.4 %collective-permute-start.1 = (bf16[1024,128]{1,0:T(8,128)(2,1)S(1)}, bf16[1024,128]{1,0:T(8,128)(2,1)S(1)}, u32[]{:S(2)}, u32[]{:S(2)}) collective-permute-start(bf16[1024,128]{1,0:T(8,128)(2,1)S(1)} %maximum_select_fusion.2), channel_id=1, source_target_pairs={{0,16},{8,24},{16,0},{24,8},{32,48},{40,56},{48,32},{56,40},{64,80... | collective-permute-start | bytes 786440 | tf_op jit(solution)/shard_map/ppermute | solution.py:16
  70.7 27.8 %collective-permute-start.2 = (bf16[2048,128]{1,0:T(8,128)(2,1)S(1)}, bf16[2048,128]{1,0:T(8,128)(2,1)S(1)}, u32[]{:S(2)}, u32[]{:S(2)}) collective-permute-start(bf16[2048,128]{1,0:T(8,128)(2,1)S(1)} %maximum_select_fusion.1), channel_id=1, source_target_pairs={{0,32},{8,40},{16,48},{24,56},{32,0},{40,8},{48,16},{56,24},{64,96... | collective-permute-start | bytes 1572872 | tf_op jit(solution)/shard_map/ppermute | solution.py:16
  99.8 26.4 %collective-permute-start.3 = (bf16[4096,128]{1,0:T(8,128)(2,1)}, bf16[4096,128]{1,0:T(8,128)(2,1)}, u32[]{:S(2)}, u32[]{:S(2)}) collective-permute-start(bf16[4096,128]{1,0:T(8,128)(2,1)} %maximum_select_fusion), channel_id=1, source_target_pairs={{0,64},{8,72},{16,80},{24,88},{32,96},{40,104},{48,112},{56,120},{... | collective-permute-start | bytes 3145736 | tf_op jit(solution)/shard_map/ppermute | solution.py:16
  105.7 22.0 %copy-start.6 = (bf16[512,128]{1,0:T(8,128)(2,1)S(1)}, bf16[512,128]{1,0:T(8,128)(2,1)}, u32[]{:S(2)}) copy-start(bf16[512,128]{1,0:T(8,128)(2,1)} %copy-done.5) | copy-start | bytes 393220
  105.7 22.2 %copy-start.3 = (bf16[1,1536,64]{1,2,0:T(8,128)(2,1)S(1)}, bf16[1,1536,64]{1,2,0:T(8,128)(2,1)}, u32[]{:S(2)}) copy-start(bf16[1,1536,64]{1,2,0:T(8,128)(2,1)} %param.14) | copy-start | bytes 589828
  107.6 22.9 %copy-start.13 = (s32[12]{0:T(128)S(1)}, s32[12]{0:T(128)}, u32[]{:S(2)}) copy-start(s32[12]{0:T(128)} %fusion.38) | copy-start | bytes 148
  133.4 106.1 %copy-start.7 = (bf16[6,3072]{1,0:T(8,128)(2,1)S(1)}, bf16[6,3072]{1,0:T(8,128)(2,1)}, u32[]{:S(2)}) copy-start(bf16[6,3072]{1,0:T(8,128)(2,1)} %param.20) | copy-start | bytes 110596
  133.4 106.3 %copy-start.11 = (f32[3]{0:T(128)S(1)}, f32[3]{0:T(128)}, u32[]{:S(2)}) copy-start(f32[3]{0:T(128)} %get-tuple-element.10) | copy-start | bytes 40
  133.4 106.3 %copy-start.12 = (f32[3]{0:T(128)S(1)}, f32[3]{0:T(128)}, u32[]{:S(2)}) copy-start(f32[3]{0:T(128)} %get-tuple-element.11) | copy-start | bytes 40
  342.1 1.3 copy-start.2
  342.3 1.2 copy-start.8
  342.3 1.2 copy-start.9
  342.3 1.2 copy-start.14
  343.0 0.9 copy-start.4
  349.2 27.2 %collective-permute-start.4 = (bf16[4096,128]{0,1:T(8,128)(2,1)S(1)}, bf16[4096,128]{0,1:T(8,128)(2,1)}, u32[]{:S(2)}, u32[]{:S(2)}) collective-permute-start(bf16[4096,128]{0,1:T(8,128)(2,1)S(1)} %select_convert_fusion), channel_id=1, source_target_pairs={{0,64},{8,72},{16,80},{24,88},{32,96},{40,104},{48,112},{56,120},{... | collective-permute-start | bytes 3145736 | tf_op jit(solution)/shard_map/ppermute | solution.py:16
  380.1 28.1 %collective-permute-start.5 = (bf16[2048,128]{0,1:T(8,128)(2,1)}, bf16[2048,128]{0,1:T(8,128)(2,1)}, u32[]{:S(2)}, u32[]{:S(2)}) collective-permute-start(bf16[2048,128]{0,1:T(8,128)(2,1)} %select_convert_fusion.1), channel_id=1, source_target_pairs={{0,32},{8,40},{16,48},{24,56},{32,0},{40,8},{48,16},{56,24},{64,96... | collective-permute-start | bytes 1572872 | tf_op jit(solution)/shard_map/ppermute | solution.py:16
  409.4 1.0 copy-start.1
  410.5 9.3 %collective-permute-start.6 = (bf16[1024,128]{0,1:T(8,128)(2,1)S(1)}, bf16[1024,128]{0,1:T(8,128)(2,1)S(1)}, u32[]{:S(2)}, u32[]{:S(2)}) collective-permute-start(bf16[1024,128]{0,1:T(8,128)(2,1)S(1)} %select_convert_fusion.2), channel_id=1, source_target_pairs={{0,16},{8,24},{16,0},{24,8},{32,48},{40,56},{48,32},{56,40},{64,80... | collective-permute-start | bytes 786440 | tf_op jit(solution)/shard_map/ppermute | solution.py:16
  421.1 4.2 collective-permute-start.7
Sparse Core Ops, SparseCore 0:
  426.3 81.1 reduce-scatter.3
where the time goes:
time: 518 us; the launch traced here: 516 us
  blocking collectives  250 us (48%)
  waiting for transfers between devices  187 us (36%)
  starting transfers between devices  27.4 us (5%)
  other arithmetic  15 us (3%)
  between operations  14.5 us (3%)
  local copies, waits for them, and re-layouts  12.7 us (2%)
  matrix products  8.52 us (2%)
    ppermute x8, waiting for transfers between devices, partner(): return lax.ppermute(value, axis, pairs)  108 us
    psum x1, blocking collectives, on_device(): lax.psum(own_rows - scattered, ('leaf', 'node')).astype(jnp.bfloat16)  106 us
    psum x1, blocking collectives, on_device(): root_full = lax.psum(full_term, ('leaf', 'node')).astype(jnp.bfloat16)  102 us
    unnamed x2, waiting for transfers between devices  79.7 us
    all_gather x1, blocking collectives, on_device(): holding = lax.all_gather(leaf_rhs[0], 'node', axis=0, tiled=True)  42.6 us
    ppermute x8, starting transfers between devices, partner(): return lax.ppermute(value, axis, pairs)  27.3 us
  transfers between devices with their start and end apart: 9, of which 9 were waited for; matrix products, arithmetic and copies ran while one was open for 2% of the time, Pallas kernels for 0%

commit v1 on v0

v1 whole, which is shorter than its diff:
```python
import jax
import jax.numpy as jnp
from jax import lax
from jax.experimental import pallas as pl
from jax.experimental.pallas import tpu as pltpu
from jax.sharding import Mesh
from jax.sharding import PartitionSpec as P

LEAVES = 4
ROOT_TILES = 24
LEAF_TILES = 12
TILE = 128
RHS = 128
ROOT_ROWS = ROOT_TILES * TILE
LEAF_ROWS = 8192

AXES = ("p", "yl", "zl", "c", "zh", "x")
SIZES = (4, 2, 4, 2, 2, 4)
LEAF = ("p", "yl", "zl", "c")
NODE = ("zh", "x")
CX = ("c", "x")
YZ = ("yl", "zl", "zh")
YALL = ("p", "yl")
Q = ("zl", "c", "zh", "x")
GRAN = ("c", "zl", "zh")
XGRAN = ("x", "c", "zl", "zh")
PYX = ("p", "yl", "x")

F32 = jnp.float32
BF16 = jnp.bfloat16


def exchange(blocks, axes):
    return lax.all_to_all(blocks, axes, 0, 0)


def gather(value, axes):
    count = 1
    for axis in axes:
        count *= lax.axis_size(axis)
    return exchange(jnp.broadcast_to(value[None], (count,) + value.shape), axes)


def summed(blocks):
    return jnp.sum(blocks.astype(F32), axis=0)


def split_columns_kernel(source_ref, out_ref):
    lane = lax.broadcasted_iota(jnp.int32, (64, TILE), 1)
    low = lane < 64
    for m in range(8):
        for core in range(2):
            for xh in range(2):
                first = ((m * 2 + core) * 2) * 2 + xh
                second = first + 2
                a = source_ref[:, first * TILE : (first + 1) * TILE].astype(F32)
                b = source_ref[:, second * TILE : (second + 1) * TILE].astype(F32)
                even = jnp.where(low, a, pltpu.roll(b, 64, 1))
                odd = jnp.where(low, pltpu.roll(a, 64, 1), b)
                place = slice(m * TILE, (m + 1) * TILE)
                out_ref[core * 4 + xh * 2, :, place] = even.astype(BF16)
                out_ref[core * 4 + xh * 2 + 1, :, place] = odd.astype(BF16)


def split_columns(factor_rows):
    return pl.pallas_call(
        split_columns_kernel,
        out_shape=jax.ShapeDtypeStruct((8, 64, 1024), BF16),
    )(factor_rows)


def combine_kernel(tiles_ref, terms_ref, rhs_ref, out_ref, total_ref):
    total_ref[...] = jnp.zeros_like(total_ref)
    for p in range(LEAVES):
        for k in range(LEAF_TILES):
            tile = tiles_ref[p, k]
            term = terms_ref[p * 24 + k].astype(F32) + terms_ref[p * 24 + 12 + k].astype(F32)
            total_ref[tile] = total_ref[tile] + term
    out_ref[...] = (rhs_ref[...].astype(F32) - total_ref[...]).astype(BF16)


def combine(root_tiles, terms, rhs):
    return pl.pallas_call(
        combine_kernel,
        out_shape=jax.ShapeDtypeStruct((ROOT_TILES, 8, RHS), BF16),
        in_specs=[
            pl.BlockSpec(memory_space=pltpu.SMEM),
            pl.BlockSpec(memory_space=pltpu.VMEM),
            pl.BlockSpec(memory_space=pltpu.VMEM),
        ],
        out_specs=pl.BlockSpec(memory_space=pltpu.VMEM),
        scratch_shapes=[pltpu.VMEM((ROOT_TILES, 8, RHS), F32)],
    )(root_tiles, terms, rhs)


def pivot_solve(values, diagonal, joined):
    length = values.shape[0]
    halves = values.reshape(length // 2, 2, values.shape[1])
    swapped = halves[:, ::-1, :].reshape(length, values.shape[1])
    return diagonal * values + joined * swapped


def parts_of(value):
    high = lax.reduce_precision(value, 8, 7)
    rest = value - high
    middle = lax.reduce_precision(rest, 8, 7)
    low = lax.reduce_precision(rest - middle, 8, 7)
    return [high, middle, low]


def transposed_product(matrix, vector):
    return lax.dot_general(
        matrix, vector, (((0,), (0,)), ((), ())), preferred_element_type=F32
    )


def on_device(
    leaf_rhs,
    leaf_inverse,
    leaf_update,
    root_tiles,
    leaf_dinv,
    leaf_doff,
    leaf_pairs,
    root_rhs,
    root_inverse,
    root_dinv,
    root_doff,
    root_pairs,
):
    blocks = exchange(split_columns(leaf_inverse[0]), CX).reshape(512, 1024)
    rhs_part = gather(leaf_rhs[0], YZ).reshape(1024, RHS)

    joined = jnp.repeat(root_doff * root_pairs.astype(F32), 2)
    columns = jnp.stack(parts_of(root_dinv) + parts_of(joined), axis=1).astype(BF16)
    columns = jnp.pad(columns, ((0, 0), (0, TILE - 6)))
    root_pack = jnp.concatenate([root_inverse, root_rhs, columns], axis=1)
    root_pack = gather(jnp.pad(root_pack, ((0, 2), (0, 0))), YALL).reshape(64, ROOT_ROWS + 2 * TILE)
    root_rows = root_pack[:, :ROOT_ROWS]
    pivots = root_pack[:, ROOT_ROWS + TILE :].astype(F32)
    dinv_rows = pivots[:, 0:1] + pivots[:, 1:2] + pivots[:, 2:3]
    joined_rows = pivots[:, 3:4] + pivots[:, 4:5] + pivots[:, 5:6]
    all_rhs = gather(root_pack[:, ROOT_ROWS : ROOT_ROWS + TILE], Q).reshape(64 * 64, RHS)
    granule = lax.axis_index(GRAN)
    at = jnp.arange(64 * 64, dtype=jnp.int32)
    held = jnp.where(at % 8 < 6, 384 * (at // 8 % 8) + 6 * (at // 64) + at % 8, -1)
    want = jnp.arange(ROOT_TILES * 8, dtype=jnp.int32)
    want = TILE * (want // 8) + 8 * granule + want % 8
    select = (want[:, None] == held[None, :]).astype(BF16)
    rhs_rows = jnp.dot(select, all_rhs, preferred_element_type=F32).astype(BF16)
    rhs_rows = rhs_rows.reshape(ROOT_TILES, 8, RHS)

    partial = jnp.dot(blocks, rhs_part, preferred_element_type=F32).astype(BF16)
    leaf_forward = summed(exchange(partial.reshape(8, 64, RHS), CX)).astype(BF16)

    update = leaf_update[0]
    ordered = update.reshape(4, 3, 16, 8, 64).transpose(0, 2, 1, 3, 4).reshape(1536, 64)
    term = jnp.dot(ordered, leaf_forward, preferred_element_type=F32).astype(BF16)
    term = summed(exchange(term.reshape(64, 24, RHS), XGRAN)).astype(BF16)
    terms = gather(term, PYX).reshape(96, 8, RHS)
    reduced = combine(root_tiles, terms, rhs_rows)
    reduced = gather(reduced, GRAN).transpose(1, 0, 2, 3).reshape(ROOT_ROWS, RHS)

    root_forward = jnp.dot(root_rows, reduced, preferred_element_type=F32)
    root_scaled = pivot_solve(root_forward, dinv_rows, joined_rows).astype(BF16)
    back = transposed_product(root_rows, root_scaled).astype(BF16)
    root_part = summed(exchange(back.reshape(64, 48, RHS), Q)).astype(BF16)
    root_full = gather(root_part, Q).reshape(ROOT_ROWS, RHS)
    root_own = lax.dynamic_slice_in_dim(root_full, lax.axis_index(AXES) * 6, 6, 0)

    tile_ids = lax.dynamic_index_in_dim(root_tiles, lax.axis_index("p"), 0, keepdims=False)
    onehot = (tile_ids[:, None] == jnp.arange(ROOT_TILES, dtype=jnp.int32)[None, :]).astype(BF16)
    tile_values = jnp.einsum(
        "kt,tar->kar", onehot, root_full.reshape(ROOT_TILES, TILE, RHS), preferred_element_type=F32
    )
    tile_values = tile_values.astype(BF16).reshape(LEAF_TILES * TILE, RHS)
    coupling = transposed_product(update, tile_values)
    leaf_joined = jnp.repeat(leaf_doff[0] * leaf_pairs[0].astype(F32), 2)[:, None]
    scaled = pivot_solve(leaf_forward.astype(F32), leaf_dinv[0][:, None], leaf_joined)
    leaf_vector = (scaled - coupling).astype(BF16)
    vector = gather(leaf_vector, CX).reshape(512, RHS)
    back_leaf = transposed_product(blocks, vector).astype(BF16)
    leaf_solution = summed(exchange(back_leaf.reshape(16, 64, RHS), YZ)).astype(BF16)
    return (leaf_solution[None], root_own)


def solution(mesh):
    fine = Mesh(mesh.devices.reshape(SIZES), AXES)
    in_specs = (
        P(LEAF, NODE, None),
        P(LEAF, NODE, None),
        P(LEAF, None, NODE),
        P(),
        P(LEAF, NODE),
        P(LEAF, NODE),
        P(LEAF, NODE),
        P(AXES, None),
        P(AXES, None),
        P(AXES),
        P(AXES),
        P(AXES),
    )
    out_specs = (P(LEAF, NODE, None), P(AXES, None))
    return jax.shard_map(
        on_device, mesh=fine, in_specs=in_specs, out_specs=out_specs, check_vma=False
    )
```

time: 518 us -> 268 us (0.52)
  blocking collectives: 250 us -> 38.6 us
  waiting for transfers between devices: 187 us -> 146 us
  starting transfers between devices: 27.4 us -> 59.2 us
  other arithmetic: 15 us -> 1.18 us
  between operations: 14.5 us -> 0.94 us
    psum x2 -> x0, blocking collectives: 208 us -> none  [the longest x1 106 us: on_device(): lax.psum(own_rows - scattered, ('leaf', 'node')).astype(jnp.bfloat16)]
    all_to_all x0 -> x10, waiting for transfers between devices: none -> 146 us  [exchange(): return lax.all_to_all(blocks, axes, 0, 0)]
    ppermute x8 -> x0, waiting for transfers between devices: 108 us -> none  [partner(): return lax.ppermute(value, axis, pairs)]
    unnamed x2 -> x0, waiting for transfers between devices: 79.7 us -> none
    all_to_all x0 -> x10, starting transfers between devices: none -> 59.2 us  [exchange(): return lax.all_to_all(blocks, axes, 0, 0)]
    all_gather x1 -> x0, blocking collectives: 42.6 us -> none  [on_device(): holding = lax.all_gather(leaf_rhs[0], 'node', axis=0, tiled=True)]
    all_to_all x0 -> x2, blocking collectives: none -> 38.6 us  [exchange(): return lax.all_to_all(blocks, axes, 0, 0)]
    ppermute x8 -> x0, starting transfers between devices: 27.3 us -> none  [partner(): return lax.ppermute(value, axis, pairs)]
  transfers between devices with their start and end apart: 9 -> 10, of which waited for: 9 -> 10; matrix products, arithmetic and copies ran while one was open for 2% -> 2% of each run, Pallas kernels for 0% -> 1%
where the time goes in v1:
time: 268 us; the launch traced here: 267 us
  waiting for transfers between devices  146 us (54%)
  starting transfers between devices  59.2 us (22%)
  blocking collectives  38.6 us (14%)
  local copies, waits for them, and re-layouts  12.1 us (5%)
  matrix products  4.53 us (2%)
  Pallas kernels  4.33 us (2%)
    all_to_all x10, waiting for transfers between devices, exchange(): return lax.all_to_all(blocks, axes, 0, 0)  146 us
    all_to_all x10, starting transfers between devices, exchange(): return lax.all_to_all(blocks, axes, 0, 0)  59.2 us
    all_to_all x2, blocking collectives, exchange(): return lax.all_to_all(blocks, axes, 0, 0)  38.6 us
    broadcast_in_dim x7, local copies, waits for them, and re-layouts, gather(): return exchange(jnp.broadcast_to(value[None], (count,) + value.shape), axes)  7.09 us
  transfers between devices with their start and end apart: 10, of which 10 were waited for; matrix products, arithmetic and copies ran while one was open for 2% of the time, Pallas kernels for 1%

profile of v1, /device:TPU:1, one launch (start us, length us, event | category | flops | bytes accessed | tf_op | source)
XLA Modules:
  0.0 267.0 jit_solution(3774009383747579932)
XLA Ops:
  0.6 1.5 broadcast_in_dim.25
  2.1 12.0 %all-to-all-start.1 = ((bf16[16,64,128]{2,1,0:T(8,128)(2,1)}), bf16[16,64,128]{2,1,0:T(8,128)(2,1)S(1)}, u32[]{:S(2)}, u32[]{:S(2)}) async-start(bf16[16,64,128]{2,1,0:T(8,128)(2,1)} %broadcast_in_dim.25), calls=%async_computation.1 | async-start | bytes 524288 | tf_op jit(solution)/shard_map/all_to_all | solution.py:34
  14.1 2.7 shard_map.131
  16.8 6.2 %all-to-all-done.1 = bf16[16,64,128]{2,1,0:T(8,128)(2,1)S(1)} async-done(((bf16[16,64,128]{2,1,0:T(8,128)(2,1)}), bf16[16,64,128]{2,1,0:T(8,128)(2,1)S(1)}, u32[]{:S(2)}, u32[]{:S(2)}) %all-to-all-start.1) | async-done | bytes 262176 | tf_op jit(solution)/shard_map/all_to_all | solution.py:34
  23.0 7.3 %all-to-all-start = ((bf16[8,64,1024]{2,1,0:T(8,128)(2,1)}), bf16[8,64,1024]{2,1,0:T(8,128)(2,1)S(1)}, u32[]{:S(2)}, u32[]{:S(2)}) async-start(bf16[8,64,1024]{2,1,0:T(8,128)(2,1)} %shard_map.131), calls=%async_computation | async-start | bytes 2097152 | tf_op jit(solution)/shard_map/all_to_all | solution.py:34
  30.7 14.6 %all-to-all-done = bf16[8,64,1024]{2,1,0:T(8,128)(2,1)S(1)} async-done(((bf16[8,64,1024]{2,1,0:T(8,128)(2,1)}), bf16[8,64,1024]{2,1,0:T(8,128)(2,1)S(1)}, u32[]{:S(2)}, u32[]{:S(2)}) %all-to-all-start) | async-done | bytes 1048608 | tf_op jit(solution)/shard_map/all_to_all | solution.py:34
  45.3 1.1 convolution_convert_fusion.3
  46.4 3.7 %all-to-all-start.2 = ((bf16[8,64,128]{2,1,0:T(8,128)(2,1)}), bf16[8,64,128]{2,1,0:T(8,128)(2,1)S(1)}, u32[]{:S(2)}, u32[]{:S(2)}) async-start(bf16[8,64,128]{2,1,0:T(8,128)(2,1)} %bitcast.5), calls=%async_computation.2 | async-start | bytes 262144 | tf_op jit(solution)/shard_map/all_to_all | solution.py:34
  50.1 5.1 %all-to-all-done.2 = bf16[8,64,128]{2,1,0:T(8,128)(2,1)S(1)} async-done(((bf16[8,64,128]{2,1,0:T(8,128)(2,1)}), bf16[8,64,128]{2,1,0:T(8,128)(2,1)S(1)}, u32[]{:S(2)}, u32[]{:S(2)}) %all-to-all-start.2) | async-done | bytes 131104 | tf_op jit(solution)/shard_map/all_to_all | solution.py:34
  56.1 5.9 %all-to-all-start.3 = ((bf16[8,8,3328]{2,1,0:T(8,128)(2,1)}), bf16[8,8,3328]{2,1,0:T(8,128)(2,1)S(1)}, u32[]{:S(2)}, u32[]{:S(2)}) async-start(bf16[8,8,3328]{2,1,0:T(8,128)(2,1)} %broadcast_in_dim.28), calls=%async_computation.3 | async-start | bytes 851968 | tf_op jit(solution)/shard_map/all_to_all | solution.py:34
  62.6 0.9 copy.34
  63.5 14.3 %all-to-all-done.3 = bf16[8,8,3328]{2,1,0:T(8,128)(2,1)S(1)} async-done(((bf16[8,8,3328]{2,1,0:T(8,128)(2,1)}), bf16[8,8,3328]{2,1,0:T(8,128)(2,1)S(1)}, u32[]{:S(2)}, u32[]{:S(2)}) %all-to-all-start.3) | async-done | bytes 426016 | tf_op jit(solution)/shard_map/all_to_all | solution.py:34
  77.8 4.7 %all-to-all-start.4 = ((bf16[64,24,128]{2,1,0:T(8,128)(2,1)}), bf16[64,24,128]{2,1,0:T(8,128)(2,1)S(1)}, u32[]{:S(2)}, u32[]{:S(2)}) async-start(bf16[64,24,128]{2,1,0:T(8,128)(2,1)} %bitcast.19), calls=%async_computation.4 | async-start | bytes 786432 | tf_op jit(solution)/shard_map/all_to_all | solution.py:34
  82.6 15.8 %all-to-all-done.4 = bf16[64,24,128]{2,1,0:T(8,128)(2,1)S(1)} async-done(((bf16[64,24,128]{2,1,0:T(8,128)(2,1)}), bf16[64,24,128]{2,1,0:T(8,128)(2,1)S(1)}, u32[]{:S(2)}, u32[]{:S(2)}) %all-to-all-start.4) | async-done | bytes 393248 | tf_op jit(solution)/shard_map/all_to_all | solution.py:34
  98.4 1.2 broadcast_in_dim.30
  99.7 5.5 %all-to-all-start.6 = ((bf16[64,64,128]{2,1,0:T(8,128)(2,1)}), bf16[64,64,128]{2,1,0:T(8,128)(2,1)S(1)}, u32[]{:S(2)}, u32[]{:S(2)}) async-start(bf16[64,64,128]{2,1,0:T(8,128)(2,1)} %broadcast_in_dim.30), calls=%async_computation.6 | async-start | bytes 2097152 | tf_op jit(solution)/shard_map/all_to_all | solution.py:34
  105.2 28.8 %all-to-all-done.6 = bf16[64,64,128]{2,1,0:T(8,128)(2,1)S(1)} async-done(((bf16[64,64,128]{2,1,0:T(8,128)(2,1)}), bf16[64,64,128]{2,1,0:T(8,128)(2,1)S(1)}, u32[]{:S(2)}, u32[]{:S(2)}) %all-to-all-start.6) | async-done | bytes 1048608 | tf_op jit(solution)/shard_map/all_to_all | solution.py:34
  134.7 3.9 %all-to-all-start.5 = ((bf16[32,24,128]{2,1,0:T(8,128)(2,1)}), bf16[32,24,128]{2,1,0:T(8,128)(2,1)S(1)}, u32[]{:S(2)}, u32[]{:S(2)}) async-start(bf16[32,24,128]{2,1,0:T(8,128)(2,1)} %broadcast_in_dim.29), calls=%async_computation.5 | async-start | bytes 393216 | tf_op jit(solution)/shard_map/all_to_all | solution.py:34
  138.6 1.2 fusion.10.rhs_ref
  139.9 8.7 %all-to-all-done.5 = bf16[32,24,128]{2,1,0:T(8,128)(2,1)S(1)} async-done(((bf16[32,24,128]{2,1,0:T(8,128)(2,1)}), bf16[32,24,128]{2,1,0:T(8,128)(2,1)S(1)}, u32[]{:S(2)}, u32[]{:S(2)}) %all-to-all-start.5) | async-done | bytes 196640 | tf_op jit(solution)/shard_map/all_to_all | solution.py:34
  149.3 1.7 shard_map.132
  150.9 1.9 broadcast_in_dim.31
  152.8 6.7 %all-to-all-start.7 = ((bf16[16,24,8,128]{3,2,1,0:T(8,128)(2,1)}), bf16[16,24,8,128]{3,2,1,0:T(8,128)(2,1)S(1)}, u32[]{:S(2)}, u32[]{:S(2)}) async-start(bf16[16,24,8,128]{3,2,1,0:T(8,128)(2,1)} %broadcast_in_dim.31), calls=%async_computation.7 | async-start | bytes 1572864 | tf_op jit(solution)/shard_map/all_to_all | solution.py:34
  159.7 20.8 %all-to-all-done.7 = bf16[16,24,8,128]{3,2,1,0:T(8,128)(2,1)S(1)} async-done(((bf16[16,24,8,128]{3,2,1,0:T(8,128)(2,1)}), bf16[16,24,8,128]{3,2,1,0:T(8,128)(2,1)S(1)}, u32[]{:S(2)}, u32[]{:S(2)}) %all-to-all-start.7) | async-done | bytes 786464 | tf_op jit(solution)/shard_map/all_to_all | solution.py:34
  181.5 29.0 %all_to_all.60 = bf16[64,48,128]{2,1,0:T(8,128)(2,1)S(1)} all-to-all(bf16[64,48,128]{2,1,0:T(8,128)(2,1)S(1)} %bitcast.78), channel_id=1, replica_groups=mesh['p'=4,'yl'=2,'zl'=4,'c'=2,'zh'=2,'x'=4] {'zl','c','zh','x'}, dimensions={0} | all-to-all | bytes 1572864 | tf_op jit(solution)/shard_map/all_to_all | solution.py:34
  210.7 1.0 broadcast_in_dim.32
  211.7 6.1 %all-to-all-start.9 = ((bf16[64,48,128]{2,1,0:T(8,128)(2,1)}), bf16[64,48,128]{2,1,0:T(8,128)(2,1)S(1)}, u32[]{:S(2)}, u32[]{:S(2)}) async-start(bf16[64,48,128]{2,1,0:T(8,128)(2,1)} %broadcast_in_dim.32), calls=%async_computation.9 | async-start | bytes 1572864 | tf_op jit(solution)/shard_map/all_to_all | solution.py:34
  218.7 22.1 %all-to-all-done.9 = bf16[64,48,128]{2,1,0:T(8,128)(2,1)S(1)} async-done(((bf16[64,48,128]{2,1,0:T(8,128)(2,1)}), bf16[64,48,128]{2,1,0:T(8,128)(2,1)S(1)}, u32[]{:S(2)}, u32[]{:S(2)}) %all-to-all-start.9) | async-done | bytes 786464 | tf_op jit(solution)/shard_map/all_to_all | solution.py:34
  241.9 9.6 %all_to_all.61 = bf16[8,64,128]{2,1,0:T(8,128)(2,1)S(1)} all-to-all(bf16[8,64,128]{2,1,0:T(8,128)(2,1)S(1)} %broadcast_in_dim.33), channel_id=1, replica_groups=mesh['p'=4,'yl'=2,'zl'=4,'c'=2,'zh'=2,'x'=4] {'c','x'}, dimensions={0} | all-to-all | bytes 262144 | tf_op jit(solution)/shard_map/all_to_all | solution.py:34
  251.8 0.8 copy.38
  252.6 3.5 %all-to-all-start.11 = ((bf16[16,64,128]{2,1,0:T(8,128)(2,1)}), bf16[16,64,128]{2,1,0:T(8,128)(2,1)S(1)}, u32[]{:S(2)}, u32[]{:S(2)}) async-start(bf16[16,64,128]{2,1,0:T(8,128)(2,1)} %bitcast.34), calls=%async_computation.11 | async-start | bytes 524288 | tf_op jit(solution)/shard_map/all_to_all | solution.py:34
  256.8 9.5 %all-to-all-done.11 = bf16[16,64,128]{2,1,0:T(8,128)(2,1)S(1)} async-done(((bf16[16,64,128]{2,1,0:T(8,128)(2,1)}), bf16[16,64,128]{2,1,0:T(8,128)(2,1)S(1)}, u32[]{:S(2)}, u32[]{:S(2)}) %all-to-all-start.11) | async-done | bytes 262176 | tf_op jit(solution)/shard_map/all_to_all | solution.py:34
  (57 shorter events, 8.1 us)
Async XLA Ops:
  2.1 20.9 %all-to-all-start.1 = ((bf16[16,64,128]{2,1,0:T(8,128)(2,1)}), bf16[16,64,128]{2,1,0:T(8,128)(2,1)S(1)}, u32[]{:S(2)}, u32[]{:S(2)}) async-start(bf16[16,64,128]{2,1,0:T(8,128)(2,1)} %broadcast_in_dim.25), calls=%async_computation.1 | async-start | bytes 524288 | tf_op jit(solution)/shard_map/all_to_all | solution.py:34
  16.8 13.6 %copy-start.6 = (f32[3]{0:T(128)S(1)}, f32[3]{0:T(128)}, u32[]{:S(2)}) copy-start(f32[3]{0:T(128)} %param.22) | copy-start | bytes 40
  16.8 13.6 %copy-start.7 = (s32[3]{0:T(128)S(1)}, s32[3]{0:T(128)}, u32[]{:S(2)}) copy-start(s32[3]{0:T(128)} %param.23) | copy-start | bytes 40
  16.8 13.8 %copy-start.5 = (f32[6]{0:T(128)S(1)}, f32[6]{0:T(128)}, u32[]{:S(2)}) copy-start(f32[6]{0:T(128)} %param.21) | copy-start | bytes 76
  23.0 22.3 %all-to-all-start = ((bf16[8,64,1024]{2,1,0:T(8,128)(2,1)}), bf16[8,64,1024]{2,1,0:T(8,128)(2,1)S(1)}, u32[]{:S(2)}, u32[]{:S(2)}) async-start(bf16[8,64,1024]{2,1,0:T(8,128)(2,1)} %shard_map.131), calls=%async_computation | async-start | bytes 2097152 | tf_op jit(solution)/shard_map/all_to_all | solution.py:34
  30.3 19.8 %copy-start.2 = (bf16[6,3072]{1,0:T(8,128)(2,1)S(1)}, bf16[6,3072]{1,0:T(8,128)(2,1)}, u32[]{:S(2)}) copy-start(bf16[6,3072]{1,0:T(8,128)(2,1)} %param.20) | copy-start | bytes 110596
  30.3 19.8 %copy-start.3 = (bf16[6,128]{1,0:T(8,128)(2,1)S(1)}, bf16[6,128]{1,0:T(8,128)(2,1)}, u32[]{:S(2)}) copy-start(bf16[6,128]{1,0:T(8,128)(2,1)} %param.19) | copy-start | bytes 4612
  46.4 15.6 %copy-start.1 = (bf16[1,1536,64]{1,2,0:T(8,128)(2,1)S(1)}, bf16[1,1536,64]{1,2,0:T(8,128)(2,1)}, u32[]{:S(2)}) copy-start(bf16[1,1536,64]{1,2,0:T(8,128)(2,1)} %param.14) | copy-start | bytes 589828
  46.4 8.9 %all-to-all-start.2 = ((bf16[8,64,128]{2,1,0:T(8,128)(2,1)}), bf16[8,64,128]{2,1,0:T(8,128)(2,1)S(1)}, u32[]{:S(2)}, u32[]{:S(2)}) async-start(bf16[8,64,128]{2,1,0:T(8,128)(2,1)} %bitcast.5), calls=%async_computation.2 | async-start | bytes 262144 | tf_op jit(solution)/shard_map/all_to_all | solution.py:34
  56.1 21.8 %all-to-all-start.3 = ((bf16[8,8,3328]{2,1,0:T(8,128)(2,1)}), bf16[8,8,3328]{2,1,0:T(8,128)(2,1)S(1)}, u32[]{:S(2)}, u32[]{:S(2)}) async-start(bf16[8,8,3328]{2,1,0:T(8,128)(2,1)} %broadcast_in_dim.28), calls=%async_computation.3 | async-start | bytes 851968 | tf_op jit(solution)/shard_map/all_to_all | solution.py:34
  77.8 20.6 %all-to-all-start.4 = ((bf16[64,24,128]{2,1,0:T(8,128)(2,1)}), bf16[64,24,128]{2,1,0:T(8,128)(2,1)S(1)}, u32[]{:S(2)}, u32[]{:S(2)}) async-start(bf16[64,24,128]{2,1,0:T(8,128)(2,1)} %bitcast.19), calls=%async_computation.4 | async-start | bytes 786432 | tf_op jit(solution)/shard_map/all_to_all | solution.py:34
  99.7 34.4 %all-to-all-start.6 = ((bf16[64,64,128]{2,1,0:T(8,128)(2,1)}), bf16[64,64,128]{2,1,0:T(8,128)(2,1)S(1)}, u32[]{:S(2)}, u32[]{:S(2)}) async-start(bf16[64,64,128]{2,1,0:T(8,128)(2,1)} %broadcast_in_dim.30), calls=%async_computation.6 | async-start | bytes 2097152 | tf_op jit(solution)/shard_map/all_to_all | solution.py:34
  134.7 13.9 %all-to-all-start.5 = ((bf16[32,24,128]{2,1,0:T(8,128)(2,1)}), bf16[32,24,128]{2,1,0:T(8,128)(2,1)S(1)}, u32[]{:S(2)}, u32[]{:S(2)}) async-start(bf16[32,24,128]{2,1,0:T(8,128)(2,1)} %broadcast_in_dim.29), calls=%async_computation.5 | async-start | bytes 393216 | tf_op jit(solution)/shard_map/all_to_all | solution.py:34
  148.6 0.7 copy-start
  152.8 27.7 %all-to-all-start.7 = ((bf16[16,24,8,128]{3,2,1,0:T(8,128)(2,1)}), bf16[16,24,8,128]{3,2,1,0:T(8,128)(2,1)S(1)}, u32[]{:S(2)}, u32[]{:S(2)}) async-start(bf16[16,24,8,128]{3,2,1,0:T(8,128)(2,1)} %broadcast_in_dim.31), calls=%async_computation.7 | async-start | bytes 1572864 | tf_op jit(solution)/shard_map/all_to_all | solution.py:34
  210.6 7.1 %copy-start.8 = (f32[1,32]{1,0:T(1,128)S(1)}, f32[1,32]{1,0:T(1,128)}, u32[]{:S(2)}) copy-start(f32[1,32]{1,0:T(1,128)} %param.17) | copy-start | bytes 388
  210.6 7.1 %copy-start.9 = (s32[1,32]{1,0:T(1,128)S(1)}, s32[1,32]{1,0:T(1,128)}, u32[]{:S(2)}) copy-start(s32[1,32]{1,0:T(1,128)} %param.18) | copy-start | bytes 388
  211.7 29.2 %all-to-all-start.9 = ((bf16[64,48,128]{2,1,0:T(8,128)(2,1)}), bf16[64,48,128]{2,1,0:T(8,128)(2,1)S(1)}, u32[]{:S(2)}, u32[]{:S(2)}) async-start(bf16[64,48,128]{2,1,0:T(8,128)(2,1)} %broadcast_in_dim.32), calls=%async_computation.9 | async-start | bytes 1572864 | tf_op jit(solution)/shard_map/all_to_all | solution.py:34
  240.9 0.8 copy-start.4
  252.6 13.7 %all-to-all-start.11 = ((bf16[16,64,128]{2,1,0:T(8,128)(2,1)}), bf16[16,64,128]{2,1,0:T(8,128)(2,1)S(1)}, u32[]{:S(2)}, u32[]{:S(2)}) async-start(bf16[16,64,128]{2,1,0:T(8,128)(2,1)} %bitcast.34), calls=%async_computation.11 | async-start | bytes 524288 | tf_op jit(solution)/shard_map/all_to_all | solution.py:34

commit v2 on v1

--- a/solution.py
+++ b/solution.py
@@ -21,9 +21,9 @@
 CX = ("c", "x")
 YZ = ("yl", "zl", "zh")
 YALL = ("p", "yl")
-Q = ("zl", "c", "zh", "x")
-GRAN = ("c", "zl", "zh")
-XGRAN = ("x", "c", "zl", "zh")
+Z = ("zl", "zh")
+XZ = ("x", "zl", "zh")
+ZX = ("zl", "zh", "x")
 PYX = ("p", "yl", "x")
 
 F32 = jnp.float32
@@ -69,28 +69,31 @@
     )(factor_rows)
 
 
-def combine_kernel(tiles_ref, terms_ref, rhs_ref, out_ref, total_ref):
-    total_ref[...] = jnp.zeros_like(total_ref)
+def combine_kernel(tiles_ref, terms_ref, out_ref, total_ref):
+    for y in range(8):
+        for x in range(3):
+            total_ref[3 * y + x] = -terms_ref[(y * 4 + x) * 4 + 3].astype(F32)
     for p in range(LEAVES):
-        for k in range(LEAF_TILES):
-            tile = tiles_ref[p, k]
-            term = terms_ref[p * 24 + k].astype(F32) + terms_ref[p * 24 + 12 + k].astype(F32)
-            total_ref[tile] = total_ref[tile] + term
-    out_ref[...] = (rhs_ref[...].astype(F32) - total_ref[...]).astype(BF16)
-
-
-def combine(root_tiles, terms, rhs):
+        for x in range(4):
+            for k in range(3):
+                tile = tiles_ref[p, 3 * x + k]
+                first = (p * 8 + x) * 4 + k
+                term = terms_ref[first].astype(F32) + terms_ref[first + 16].astype(F32)
+                total_ref[tile] = total_ref[tile] + term
+    out_ref[...] = (-total_ref[...]).astype(BF16)
+
+
+def combine(root_tiles, terms):
     return pl.pallas_call(
         combine_kernel,
         out_shape=jax.ShapeDtypeStruct((ROOT_TILES, 8, RHS), BF16),
         in_specs=[
             pl.BlockSpec(memory_space=pltpu.SMEM),
             pl.BlockSpec(memory_space=pltpu.VMEM),
-            pl.BlockSpec(memory_space=pltpu.VMEM),
         ],
         out_specs=pl.BlockSpec(memory_space=pltpu.VMEM),
         scratch_shapes=[pltpu.VMEM((ROOT_TILES, 8, RHS), F32)],
-    )(root_tiles, terms, rhs)
+    )(root_tiles, terms)
 
 
 def pivot_solve(values, diagonal, joined):
@@ -100,12 +103,28 @@
     return diagonal * values + joined * swapped
 
 
-def parts_of(value):
-    high = lax.reduce_precision(value, 8, 7)
-    rest = value - high
-    middle = lax.reduce_precision(rest, 8, 7)
-    low = lax.reduce_precision(rest - middle, 8, 7)
-    return [high, middle, low]
+def other_core(value):
+    return lax.ppermute(value, "c", [(0, 1), (1, 0)])
+
+
+def both_cores(value):
+    other = other_core(value)
+    first = lax.axis_index("c") == 0
+    return jnp.where(first, jnp.stack([value, other]), jnp.stack([other, value]))
+
+
+def gather_leaf_rhs(value):
+    def doubled(held, axis, mask, low, place):
+        pairs = [(i, i ^ mask) for i in range(lax.axis_size(axis))]
+        other = lax.ppermute(held, axis, pairs)
+        return jnp.where(low, jnp.stack([held, other], place), jnp.stack([other, held], place))
+
+    zl = lax.axis_index("zl")
+    held = doubled(value, "zh", 1, lax.axis_index("zh") == 0, 0)
+    held = doubled(held, "zl", 2, zl < 2, 0)
+    held = doubled(held, "zl", 1, zl % 2 == 0, 1)
+    held = doubled(held, "yl", 1, lax.axis_index("yl") == 0, 0)
+    return held.reshape(1024, RHS)
 
 
 def transposed_product(matrix, vector):
@@ -129,43 +148,39 @@
     root_pairs,
 ):
     blocks = exchange(split_columns(leaf_inverse[0]), CX).reshape(512, 1024)
-    rhs_part = gather(leaf_rhs[0], YZ).reshape(1024, RHS)
-
-    joined = jnp.repeat(root_doff * root_pairs.astype(F32), 2)
-    columns = jnp.stack(parts_of(root_dinv) + parts_of(joined), axis=1).astype(BF16)
-    columns = jnp.pad(columns, ((0, 0), (0, TILE - 6)))
-    root_pack = jnp.concatenate([root_inverse, root_rhs, columns], axis=1)
-    root_pack = gather(jnp.pad(root_pack, ((0, 2), (0, 0))), YALL).reshape(64, ROOT_ROWS + 2 * TILE)
-    root_rows = root_pack[:, :ROOT_ROWS]
-    pivots = root_pack[:, ROOT_ROWS + TILE :].astype(F32)
-    dinv_rows = pivots[:, 0:1] + pivots[:, 1:2] + pivots[:, 2:3]
-    joined_rows = pivots[:, 3:4] + pivots[:, 4:5] + pivots[:, 5:6]
-    all_rhs = gather(root_pack[:, ROOT_ROWS : ROOT_ROWS + TILE], Q).reshape(64 * 64, RHS)
-    granule = lax.axis_index(GRAN)
-    at = jnp.arange(64 * 64, dtype=jnp.int32)
-    held = jnp.where(at % 8 < 6, 384 * (at // 8 % 8) + 6 * (at // 64) + at % 8, -1)
-    want = jnp.arange(ROOT_TILES * 8, dtype=jnp.int32)
-    want = TILE * (want // 8) + 8 * granule + want % 8
-    select = (want[:, None] == held[None, :]).astype(BF16)
-    rhs_rows = jnp.dot(select, all_rhs, preferred_element_type=F32).astype(BF16)
-    rhs_rows = rhs_rows.reshape(ROOT_TILES, 8, RHS)
-
+    rhs_part = gather_leaf_rhs(leaf_rhs[0])
     partial = jnp.dot(blocks, rhs_part, preferred_element_type=F32).astype(BF16)
     leaf_forward = summed(exchange(partial.reshape(8, 64, RHS), CX)).astype(BF16)
 
     update = leaf_update[0]
-    ordered = update.reshape(4, 3, 16, 8, 64).transpose(0, 2, 1, 3, 4).reshape(1536, 64)
-    term = jnp.dot(ordered, leaf_forward, preferred_element_type=F32).astype(BF16)
-    term = summed(exchange(term.reshape(64, 24, RHS), XGRAN)).astype(BF16)
-    terms = gather(term, PYX).reshape(96, 8, RHS)
-    reduced = combine(root_tiles, terms, rhs_rows)
-    reduced = gather(reduced, GRAN).transpose(1, 0, 2, 3).reshape(ROOT_ROWS, RHS)
-
-    root_forward = jnp.dot(root_rows, reduced, preferred_element_type=F32)
-    root_scaled = pivot_solve(root_forward, dinv_rows, joined_rows).astype(BF16)
-    back = transposed_product(root_rows, root_scaled).astype(BF16)
-    root_part = summed(exchange(back.reshape(64, 48, RHS), Q)).astype(BF16)
-    root_full = gather(root_part, Q).reshape(ROOT_ROWS, RHS)
+    ordered = update.reshape(4, 3, 2, 8, 8, 64).transpose(2, 0, 3, 1, 4, 5).reshape(64, 24, 64)
+    chunk = jnp.arange(512, dtype=jnp.int32)
+    place = chunk // 8
+    x_of = place // 8 % 4
+    tile_row = 8 * (place // 32 * 8 + place % 8) + chunk % 8
+    row = TILE * (3 * lax.axis_index(YALL) + x_of) + tile_row
+    row = jnp.where(x_of < 3, row, -1) - 6 * lax.axis_index(AXES)
+    select = (row[:, None] == jnp.arange(8, dtype=jnp.int32)[None, :]) & (row < 6)[:, None]
+    select = select.astype(BF16).reshape(64, 8, 8)
+    left = jnp.concatenate(
+        [jnp.pad(ordered, ((0, 0), (0, 0), (0, 8))), jnp.pad(select, ((0, 0), (0, 0), (64, 0)))], 1
+    ).reshape(2048, 72)
+    right = jnp.concatenate([leaf_forward, jnp.pad(root_rhs, ((0, 2), (0, 0)))], 0)
+    term = jnp.dot(left, right, preferred_element_type=F32).astype(BF16)
+    term = summed(exchange(term.reshape(2, 1024, RHS), ("c",))).astype(BF16)
+    term = summed(exchange(term.reshape(32, 32, RHS), XZ)).astype(BF16)
+    reduced = combine(root_tiles, gather(term, PYX).reshape(128, 8, RHS))
+    reduced = both_cores(gather(reduced, Z)).reshape(16, ROOT_TILES, 8, RHS)
+    reduced = reduced.transpose(1, 0, 2, 3).reshape(ROOT_ROWS, RHS)
+
+    root_forward = jnp.dot(root_inverse, reduced, preferred_element_type=F32)
+    joined = jnp.repeat(root_doff * root_pairs.astype(F32), 2)[:, None]
+    root_scaled = pivot_solve(root_forward, root_dinv[:, None], joined).astype(BF16)
+    back = transposed_product(root_inverse, root_scaled).astype(BF16)
+    back = summed(exchange(back.reshape(2, ROOT_ROWS // 2, RHS), ("c",))).astype(BF16)
+    back = summed(exchange(back.reshape(32, 48, RHS), ZX)).astype(BF16)
+    root_part = summed(gather(back, YALL)).astype(BF16)
+    root_full = both_cores(gather(root_part, ZX)).reshape(ROOT_ROWS, RHS)
     root_own = lax.dynamic_slice_in_dim(root_full, lax.axis_index(AXES) * 6, 6, 0)
 
     tile_ids = lax.dynamic_index_in_dim(root_tiles, lax.axis_index("p"), 0, keepdims=False)

time: 268 us -> 203 us (0.76)
  waiting for transfers between devices: 146 us -> 22.5 us
  blocking collectives: 38.6 us -> 111 us
  local copies, waits for them, and re-layouts: 12.1 us -> 5.39 us
  starting transfers between devices: 59.2 us -> 52.6 us
    all_to_all x10 -> x3, waiting for transfers between devices: 146 us -> 14.6 us  [exchange(): return lax.all_to_all(blocks, axes, 0, 0)]
    all_to_all x2 -> x9, blocking collectives: 38.6 us -> 111 us  [exchange(): return lax.all_to_all(blocks, axes, 0, 0)]
    all_to_all x10 -> x3, starting transfers between devices: 59.2 us -> 16.9 us  [exchange(): return lax.all_to_all(blocks, axes, 0, 0)]
    ppermute x0 -> x6, starting transfers between devices: none -> 35.6 us  [the longest x4 21.9 us: doubled(): other = lax.ppermute(held, axis, pairs)]
    ppermute x0 -> x6, waiting for transfers between devices: none -> 7.88 us  [the longest x4 6.41 us: doubled(): other = lax.ppermute(held, axis, pairs)]
    broadcast_in_dim x7 -> x5, local copies, waits for them, and re-layouts: 7.09 us -> 0.98 us  [gather(): return exchange(jnp.broadcast_to(value[None], (count,) + value.shape), axes)]
  transfers between devices with their start and end apart: 10 -> 9, of which waited for: 10 -> 7; matrix products, arithmetic and copies ran while one was open for 2% -> 1% of each run, Pallas kernels for 1% -> 1%
where the time goes in v2:
time: 203 us; the launch traced here: 202 us
  blocking collectives  111 us (55%)
  starting transfers between devices  52.6 us (26%)
  waiting for transfers between devices  22.5 us (11%)
  local copies, waits for them, and re-layouts  5.39 us (3%)
  Pallas kernels  4.38 us (2%)
  matrix products  2.67 us (1%)
  other arithmetic  2.22 us (1%)
    all_to_all x9, blocking collectives, exchange(): return lax.all_to_all(blocks, axes, 0, 0)  111 us
    ppermute x4, starting transfers between devices, doubled(): other = lax.ppermute(held, axis, pairs)  21.9 us
    all_to_all x3, starting transfers between devices, exchange(): return lax.all_to_all(blocks, axes, 0, 0)  16.9 us
    all_to_all x3, waiting for transfers between devices, exchange(): return lax.all_to_all(blocks, axes, 0, 0)  14.6 us
    ppermute x2, starting transfers between devices, other_core(): return lax.ppermute(value, 'c', [(0, 1), (1, 0)])  13.7 us
    ppermute x4, waiting for transfers between devices, doubled(): other = lax.ppermute(held, axis, pairs)  6.41 us
  transfers between devices with their start and end apart: 9, of which 7 were waited for; matrix products, arithmetic and copies ran while one was open for 1% of the time, Pallas kernels for 1%

profile of v2, /device:TPU:1, one launch (start us, length us, event | category | flops | bytes accessed | tf_op | source)
XLA Modules:
  0.0 202.3 jit_solution(3472113073808004317)
XLA Ops:
  0.6 11.6 %collective-permute-start = (bf16[64,128]{1,0:T(8,128)(2,1)}, bf16[64,128]{1,0:T(8,128)(2,1)S(1)}, u32[]{:S(2)}, u32[]{:S(2)}) collective-permute-start(bf16[64,128]{1,0:T(8,128)(2,1)} %bitcast.112), channel_id=1, source_target_pairs={{0,4},{4,0},{1,5},{5,1},{2,6},{6,2},{3,7},{7,3},{8,12},{12,8},{9,1... | collective-permute-start | bytes 49160 | tf_op jit(solution)/shard_map/ppermute | solution.py:119
  12.2 2.6 %shard_map.131 = bf16[8,64,1024]{2,1,0:T(8,128)(2,1)} custom-call(bf16[64,8192]{1,0:T(8,128)(2,1)} %bitcast.100), custom_call_target="tpu_custom_call" | custom-call | tf_op jit(solution)/shard_map/pallas_call | solution.py:66
  14.9 5.4 %all-to-all-start = ((bf16[8,64,1024]{2,1,0:T(8,128)(2,1)}), bf16[8,64,1024]{2,1,0:T(8,128)(2,1)S(1)}, u32[]{:S(2)}, u32[]{:S(2)}) async-start(bf16[8,64,1024]{2,1,0:T(8,128)(2,1)} %shard_map.131), calls=%async_computation | async-start | bytes 2097152 | tf_op jit(solution)/shard_map/all_to_all | solution.py:34
  21.2 4.0 %collective-permute-start.1 = (bf16[2,64,128]{2,1,0:T(8,128)(2,1)S(1)}, bf16[2,64,128]{2,1,0:T(8,128)(2,1)S(1)}, u32[]{:S(2)}, u32[]{:S(2)}) collective-permute-start(bf16[2,64,128]{2,1,0:T(8,128)(2,1)S(1)} %maximum_select_fusion.7), channel_id=1, source_target_pairs={{0,32},{16,48},{32,0},{48,16},{1,33},{17,49},{33,1},{49,17},{2,34}... | collective-permute-start | bytes 98312 | tf_op jit(solution)/shard_map/ppermute | solution.py:119
  25.3 1.8 collective-permute-done.1
  27.1 3.1 %collective-permute-start.2 = (bf16[2,2,64,128]{3,2,1,0:T(8,128)(2,1)S(1)}, bf16[2,2,64,128]{3,2,1,0:T(8,128)(2,1)S(1)}, u32[]{:S(2)}, u32[]{:S(2)}) collective-permute-start(bf16[2,2,64,128]{3,2,1,0:T(8,128)(2,1)S(1)} %maximum_select_fusion.5), channel_id=1, source_target_pairs={{0,16},{16,0},{32,48},{48,32},{1,17},{17,1},{33,49},{49,33},{2,18}... | collective-permute-start | bytes 196616 | tf_op jit(solution)/shard_map/ppermute | solution.py:119
  30.2 2.2 %collective-permute-done.2 = bf16[2,2,64,128]{3,2,1,0:T(8,128)(2,1)S(1)} collective-permute-done((bf16[2,2,64,128]{3,2,1,0:T(8,128)(2,1)S(1)}, bf16[2,2,64,128]{3,2,1,0:T(8,128)(2,1)S(1)}, u32[]{:S(2)}, u32[]{:S(2)}) %collective-permute-start.2) | collective-permute-done | bytes 65568 | tf_op jit(solution)/shard_map/ppermute | solution.py:119
  32.4 3.2 %collective-permute-start.3 = (bf16[2,2,2,64,128]{4,3,2,1,0:T(8,128)(2,1)S(1)}, bf16[2,2,2,64,128]{4,3,2,1,0:T(8,128)(2,1)S(1)}, u32[]{:S(2)}, u32[]{:S(2)}) collective-permute-start(bf16[2,2,2,64,128]{4,3,2,1,0:T(8,128)(2,1)S(1)} %maximum_select_fusion.3), channel_id=1, source_target_pairs={{0,64},{64,0},{1,65},{65,1},{2,66},{66,2},{3,67},{67,3},{4,68},{68... | collective-permute-start | bytes 393224 | tf_op jit(solution)/shard_map/ppermute | solution.py:119
  35.7 2.4 %collective-permute-done.3 = bf16[2,2,2,64,128]{4,3,2,1,0:T(8,128)(2,1)S(1)} collective-permute-done((bf16[2,2,2,64,128]{4,3,2,1,0:T(8,128)(2,1)S(1)}, bf16[2,2,2,64,128]{4,3,2,1,0:T(8,128)(2,1)S(1)}, u32[]{:S(2)}, u32[]{:S(2)}) %collective-permute-start.3) | collective-permute-done | bytes 131104 | tf_op jit(solution)/shard_map/ppermute | solution.py:119
  38.7 0.8 copy.47
  39.4 8.0 %all-to-all-start.1 = ((bf16[8,64,128]{2,1,0:T(8,128)(2,1)}), bf16[8,64,128]{2,1,0:T(8,128)(2,1)S(1)}, u32[]{:S(2)}, u32[]{:S(2)}) async-start(bf16[8,64,128]{2,1,0:T(8,128)(2,1)} %bitcast.16), calls=%async_computation.1 | async-start | bytes 262144 | tf_op jit(solution)/shard_map/all_to_all | solution.py:34
  47.5 5.1 %all-to-all-done.1 = bf16[8,64,128]{2,1,0:T(8,128)(2,1)S(1)} async-done(((bf16[8,64,128]{2,1,0:T(8,128)(2,1)}), bf16[8,64,128]{2,1,0:T(8,128)(2,1)S(1)}, u32[]{:S(2)}, u32[]{:S(2)}) %all-to-all-start.1) | async-done | bytes 131104 | tf_op jit(solution)/shard_map/all_to_all | solution.py:34
  52.9 4.2 %all_to_all.60 = bf16[2,1024,128]{2,1,0:T(8,128)(2,1)S(1)} all-to-all(bf16[2,1024,128]{2,1,0:T(8,128)(2,1)S(1)} %bitcast.93), channel_id=1, replica_groups=mesh['p'=4,'yl'=2,'zl'=4,'c'=2,'zh'=2,'x'=4] {'c'}, dimensions={0} | all-to-all | bytes 1048576 | tf_op jit(solution)/shard_map/all_to_all | solution.py:34
  57.3 15.9 %all_to_all.61 = bf16[32,32,128]{2,1,0:T(8,128)(2,1)S(1)} all-to-all(bf16[32,32,128]{2,1,0:T(8,128)(2,1)S(1)} %bitcast.103), channel_id=1, replica_groups=mesh['p'=4,'yl'=2,'zl'=4,'c'=2,'zh'=2,'x'=4] {'x','zl','zh'}, dimensions={0} | all-to-all | bytes 524288 | tf_op jit(solution)/shard_map/all_to_all | solution.py:34
  73.3 20.1 %all_to_all.62 = bf16[32,32,128]{2,1,0:T(8,128)(2,1)} all-to-all(bf16[32,32,128]{2,1,0:T(8,128)(2,1)S(1)} %broadcast_in_dim.19), channel_id=1, replica_groups=mesh['p'=4,'yl'=2,'zl'=4,'c'=2,'zh'=2,'x'=4] {'p','yl','x'}, dimensions={0} | all-to-all | bytes 524288 | tf_op jit(solution)/shard_map/all_to_all | solution.py:34
  93.4 1.7 shard_map.132
  95.2 0.8 broadcast_in_dim.20
  96.0 13.0 %all_to_all.63 = bf16[8,24,8,128]{3,2,1,0:T(8,128)(2,1)S(1)} all-to-all(bf16[8,24,8,128]{3,2,1,0:T(8,128)(2,1)S(1)} %broadcast_in_dim.20), channel_id=1, replica_groups=mesh['p'=4,'yl'=2,'zl'=4,'c'=2,'zh'=2,'x'=4] {'zl','zh'}, dimensions={0} | all-to-all | bytes 786432 | tf_op jit(solution)/shard_map/all_to_all | solution.py:34
  109.0 7.0 %collective-permute-start.4 = (bf16[8,24,8,128]{3,2,1,0:T(8,128)(2,1)S(1)}, bf16[8,24,8,128]{3,2,1,0:T(8,128)(2,1)S(1)}, u32[]{:S(2)}, u32[]{:S(2)}) collective-permute-start(bf16[8,24,8,128]{3,2,1,0:T(8,128)(2,1)S(1)} %all_to_all.63), channel_id=1, source_target_pairs={{0,8},{8,0},{1,9},{9,1},{2,10},{10,2},{3,11},{11,3},{4,12},{12,4},... | collective-permute-start | bytes 1179656 | tf_op jit(solution)/shard_map/ppermute | solution.py:107
  116.2 1.1 collective-permute-done.4
  118.6 4.4 %all_to_all.64 = bf16[2,1536,128]{1,2,0:T(8,128)(2,1)S(1)} all-to-all(bf16[2,1536,128]{1,2,0:T(8,128)(2,1)S(1)} %bitcast.91), channel_id=1, replica_groups=mesh['p'=4,'yl'=2,'zl'=4,'c'=2,'zh'=2,'x'=4] {'c'}, dimensions={0} | all-to-all | bytes 1572864 | tf_op jit(solution)/shard_map/all_to_all | solution.py:34
  123.4 19.1 %all_to_all.65 = bf16[32,48,128]{2,1,0:T(8,128)(2,1)S(1)} all-to-all(bf16[32,48,128]{2,1,0:T(8,128)(2,1)S(1)} %bitcast.95), channel_id=1, replica_groups=mesh['p'=4,'yl'=2,'zl'=4,'c'=2,'zh'=2,'x'=4] {'zl','zh','x'}, dimensions={0} | all-to-all | bytes 786432 | tf_op jit(solution)/shard_map/all_to_all | solution.py:34
  142.6 10.6 %all_to_all.66 = bf16[8,48,128]{2,1,0:T(8,128)(2,1)S(1)} all-to-all(bf16[8,48,128]{2,1,0:T(8,128)(2,1)S(1)} %broadcast_in_dim.22), channel_id=1, replica_groups=mesh['p'=4,'yl'=2,'zl'=4,'c'=2,'zh'=2,'x'=4] {'p','yl'}, dimensions={0} | all-to-all | bytes 196608 | tf_op jit(solution)/shard_map/all_to_all | solution.py:34
  153.2 16.3 %all_to_all.67 = bf16[32,48,128]{2,1,0:T(8,128)(2,1)S(1)} all-to-all(bf16[32,48,128]{2,1,0:T(8,128)(2,1)S(1)} %broadcast_in_dim.23), channel_id=1, replica_groups=mesh['p'=4,'yl'=2,'zl'=4,'c'=2,'zh'=2,'x'=4] {'zl','zh','x'}, dimensions={0} | all-to-all | bytes 786432 | tf_op jit(solution)/shard_map/all_to_all | solution.py:34
  169.6 6.8 %collective-permute-start.5 = (bf16[32,48,128]{2,1,0:T(8,128)(2,1)S(1)}, bf16[32,48,128]{2,1,0:T(8,128)(2,1)S(1)}, u32[]{:S(2)}, u32[]{:S(2)}) collective-permute-start(bf16[32,48,128]{2,1,0:T(8,128)(2,1)S(1)} %all_to_all.67), channel_id=1, source_target_pairs={{0,8},{8,0},{1,9},{9,1},{2,10},{10,2},{3,11},{11,3},{4,12},{12,4},... | collective-permute-start | bytes 1179656 | tf_op jit(solution)/shard_map/ppermute | solution.py:107
  176.5 0.7 dynamic-slice_bitcast_fusion
  177.8 0.7 convolution_convert_fusion.2
  178.8 7.9 %all_to_all.68 = bf16[8,64,128]{2,1,0:T(8,128)(2,1)S(1)} all-to-all(bf16[8,64,128]{2,1,0:T(8,128)(2,1)S(1)} %broadcast_in_dim.24), channel_id=1, replica_groups=mesh['p'=4,'yl'=2,'zl'=4,'c'=2,'zh'=2,'x'=4] {'c','x'}, dimensions={0} | all-to-all | bytes 262144 | tf_op jit(solution)/shard_map/all_to_all | solution.py:34
  187.1 0.8 copy.56
  188.0 3.5 %all-to-all-start.11 = ((bf16[16,64,128]{2,1,0:T(8,128)(2,1)}), bf16[16,64,128]{2,1,0:T(8,128)(2,1)S(1)}, u32[]{:S(2)}, u32[]{:S(2)}) async-start(bf16[16,64,128]{2,1,0:T(8,128)(2,1)} %bitcast.45), calls=%async_computation.11 | async-start | bytes 524288 | tf_op jit(solution)/shard_map/all_to_all | solution.py:34
  192.1 9.6 %all-to-all-done.11 = bf16[16,64,128]{2,1,0:T(8,128)(2,1)S(1)} async-done(((bf16[16,64,128]{2,1,0:T(8,128)(2,1)}), bf16[16,64,128]{2,1,0:T(8,128)(2,1)S(1)}, u32[]{:S(2)}, u32[]{:S(2)}) %all-to-all-start.11) | async-done | bytes 262176 | tf_op jit(solution)/shard_map/all_to_all | solution.py:34
  201.6 0.6 reduce_sum.90
  (73 shorter events, 6.2 us)
Async XLA Ops:
  0.6 117.0 %copy-start = (bf16[6,3072]{1,0:T(8,128)(2,1)S(1)}, bf16[6,3072]{1,0:T(8,128)(2,1)}, u32[]{:S(2)}) copy-start(bf16[6,3072]{1,0:T(8,128)(2,1)} %param.20) | copy-start | bytes 110596
  0.6 20.5 %collective-permute-start = (bf16[64,128]{1,0:T(8,128)(2,1)}, bf16[64,128]{1,0:T(8,128)(2,1)S(1)}, u32[]{:S(2)}, u32[]{:S(2)}) collective-permute-start(bf16[64,128]{1,0:T(8,128)(2,1)} %bitcast.112), channel_id=1, source_target_pairs={{0,4},{4,0},{1,5},{5,1},{2,6},{6,2},{3,7},{7,3},{8,12},{12,8},{9,1... | collective-permute-start | bytes 49160 | tf_op jit(solution)/shard_map/ppermute | solution.py:119
  14.9 6.0 %copy-start.1 = (bf16[1,1536,64]{1,2,0:T(8,128)(2,1)S(1)}, bf16[1,1536,64]{1,2,0:T(8,128)(2,1)}, u32[]{:S(2)}) copy-start(bf16[1,1536,64]{1,2,0:T(8,128)(2,1)} %param.14) | copy-start | bytes 589828
  14.9 23.3 %all-to-all-start = ((bf16[8,64,1024]{2,1,0:T(8,128)(2,1)}), bf16[8,64,1024]{2,1,0:T(8,128)(2,1)S(1)}, u32[]{:S(2)}, u32[]{:S(2)}) async-start(bf16[8,64,1024]{2,1,0:T(8,128)(2,1)} %shard_map.131), calls=%async_computation | async-start | bytes 2097152 | tf_op jit(solution)/shard_map/all_to_all | solution.py:34
  20.3 0.9 copy-start.2
  21.2 5.9 %collective-permute-start.1 = (bf16[2,64,128]{2,1,0:T(8,128)(2,1)S(1)}, bf16[2,64,128]{2,1,0:T(8,128)(2,1)S(1)}, u32[]{:S(2)}, u32[]{:S(2)}) collective-permute-start(bf16[2,64,128]{2,1,0:T(8,128)(2,1)S(1)} %maximum_select_fusion.7), channel_id=1, source_target_pairs={{0,32},{16,48},{32,0},{48,16},{1,33},{17,49},{33,1},{49,17},{2,34}... | collective-permute-start | bytes 98312 | tf_op jit(solution)/shard_map/ppermute | solution.py:119
  27.1 5.3 %collective-permute-start.2 = (bf16[2,2,64,128]{3,2,1,0:T(8,128)(2,1)S(1)}, bf16[2,2,64,128]{3,2,1,0:T(8,128)(2,1)S(1)}, u32[]{:S(2)}, u32[]{:S(2)}) collective-permute-start(bf16[2,2,64,128]{3,2,1,0:T(8,128)(2,1)S(1)} %maximum_select_fusion.5), channel_id=1, source_target_pairs={{0,16},{16,0},{32,48},{48,32},{1,17},{17,1},{33,49},{49,33},{2,18}... | collective-permute-start | bytes 196616 | tf_op jit(solution)/shard_map/ppermute | solution.py:119
  32.4 5.7 %collective-permute-start.3 = (bf16[2,2,2,64,128]{4,3,2,1,0:T(8,128)(2,1)S(1)}, bf16[2,2,2,64,128]{4,3,2,1,0:T(8,128)(2,1)S(1)}, u32[]{:S(2)}, u32[]{:S(2)}) collective-permute-start(bf16[2,2,2,64,128]{4,3,2,1,0:T(8,128)(2,1)S(1)} %maximum_select_fusion.3), channel_id=1, source_target_pairs={{0,64},{64,0},{1,65},{65,1},{2,66},{66,2},{3,67},{67,3},{4,68},{68... | collective-permute-start | bytes 393224 | tf_op jit(solution)/shard_map/ppermute | solution.py:119
  38.7 14.0 %copy-start.3 = (bf16[6,128]{1,0:T(8,128)(2,1)S(1)}, bf16[6,128]{1,0:T(8,128)(2,1)}, u32[]{:S(2)}) copy-start(bf16[6,128]{1,0:T(8,128)(2,1)} %param.19) | copy-start | bytes 4612
  39.4 13.2 %all-to-all-start.1 = ((bf16[8,64,128]{2,1,0:T(8,128)(2,1)}), bf16[8,64,128]{2,1,0:T(8,128)(2,1)S(1)}, u32[]{:S(2)}, u32[]{:S(2)}) async-start(bf16[8,64,128]{2,1,0:T(8,128)(2,1)} %bitcast.16), calls=%async_computation.1 | async-start | bytes 262144 | tf_op jit(solution)/shard_map/all_to_all | solution.py:34
  73.3 42.6 %copy-start.6 = (f32[3]{0:T(128)S(1)}, f32[3]{0:T(128)}, u32[]{:S(2)}) copy-start(f32[3]{0:T(128)} %param.22) | copy-start | bytes 40
  73.3 42.6 %copy-start.7 = (s32[3]{0:T(128)S(1)}, s32[3]{0:T(128)}, u32[]{:S(2)}) copy-start(s32[3]{0:T(128)} %param.23) | copy-start | bytes 40
  109.0 8.3 %collective-permute-start.4 = (bf16[8,24,8,128]{3,2,1,0:T(8,128)(2,1)S(1)}, bf16[8,24,8,128]{3,2,1,0:T(8,128)(2,1)S(1)}, u32[]{:S(2)}, u32[]{:S(2)}) collective-permute-start(bf16[8,24,8,128]{3,2,1,0:T(8,128)(2,1)S(1)} %all_to_all.63), channel_id=1, source_target_pairs={{0,8},{8,0},{1,9},{9,1},{2,10},{10,2},{3,11},{11,3},{4,12},{12,4},... | collective-permute-start | bytes 1179656 | tf_op jit(solution)/shard_map/ppermute | solution.py:107
  117.4 0.7 copy-start.4
  142.5 33.8 %copy-start.8 = (f32[1,32]{1,0:T(1,128)S(1)}, f32[1,32]{1,0:T(1,128)}, u32[]{:S(2)}) copy-start(f32[1,32]{1,0:T(1,128)} %param.17) | copy-start | bytes 388
  142.5 33.9 %copy-start.9 = (s32[1,32]{1,0:T(1,128)S(1)}, s32[1,32]{1,0:T(1,128)}, u32[]{:S(2)}) copy-start(s32[1,32]{1,0:T(1,128)} %param.18) | copy-start | bytes 388
  169.6 8.1 %collective-permute-start.5 = (bf16[32,48,128]{2,1,0:T(8,128)(2,1)S(1)}, bf16[32,48,128]{2,1,0:T(8,128)(2,1)S(1)}, u32[]{:S(2)}, u32[]{:S(2)}) collective-permute-start(bf16[32,48,128]{2,1,0:T(8,128)(2,1)S(1)} %all_to_all.67), channel_id=1, source_target_pairs={{0,8},{8,0},{1,9},{9,1},{2,10},{10,2},{3,11},{11,3},{4,12},{12,4},... | collective-permute-start | bytes 1179656 | tf_op jit(solution)/shard_map/ppermute | solution.py:107
  177.8 0.8 copy-start.5
  188.0 13.7 %all-to-all-start.11 = ((bf16[16,64,128]{2,1,0:T(8,128)(2,1)}), bf16[16,64,128]{2,1,0:T(8,128)(2,1)S(1)}, u32[]{:S(2)}, u32[]{:S(2)}) async-start(bf16[16,64,128]{2,1,0:T(8,128)(2,1)} %bitcast.45), calls=%async_computation.11 | async-start | bytes 524288 | tf_op jit(solution)/shard_map/all_to_all | solution.py:34

commit v3 on v2

--- a/solution.py
+++ b/solution.py
@@ -22,9 +22,8 @@
 YZ = ("yl", "zl", "zh")
 YALL = ("p", "yl")
 Z = ("zl", "zh")
-XZ = ("x", "zl", "zh")
+GRAN = ("c", "zl", "zh")
 ZX = ("zl", "zh", "x")
-PYX = ("p", "yl", "x")
 
 F32 = jnp.float32
 BF16 = jnp.bfloat16
@@ -71,15 +70,13 @@
 
 def combine_kernel(tiles_ref, terms_ref, out_ref, total_ref):
     for y in range(8):
-        for x in range(3):
-            total_ref[3 * y + x] = -terms_ref[(y * 4 + x) * 4 + 3].astype(F32)
+        for j in range(3):
+            total_ref[3 * y + j] = -terms_ref[15 * y + 12 + j].astype(F32)
     for p in range(LEAVES):
-        for x in range(4):
-            for k in range(3):
-                tile = tiles_ref[p, 3 * x + k]
-                first = (p * 8 + x) * 4 + k
-                term = terms_ref[first].astype(F32) + terms_ref[first + 16].astype(F32)
-                total_ref[tile] = total_ref[tile] + term
+        for k in range(LEAF_TILES):
+            tile = tiles_ref[p, k]
+            term = terms_ref[30 * p + k].astype(F32) + terms_ref[30 * p + 15 + k].astype(F32)
+            total_ref[tile] = total_ref[tile] + term
     out_ref[...] = (-total_ref[...]).astype(BF16)
 
 
@@ -94,6 +91,35 @@
         out_specs=pl.BlockSpec(memory_space=pltpu.VMEM),
         scratch_shapes=[pltpu.VMEM((ROOT_TILES, 8, RHS), F32)],
     )(root_tiles, terms)
+
+
+def granule_columns_kernel(source_ref, pivots_ref, out_ref):
+    slot = lax.broadcasted_iota(jnp.int32, (8, TILE), 1) // 8
+    tiles = [source_ref[:, t * TILE : (t + 1) * TILE].astype(F32) for t in range(ROOT_TILES)]
+    for a in range(16):
+        first = tiles[0] * 0.0
+        second = pivots_ref[...]
+        for t in range(16):
+            first = jnp.where(slot == t, pltpu.roll(tiles[t], (t - a) * 8 % TILE, 1), first)
+        for t in range(8):
+            second = jnp.where(slot == t, pltpu.roll(tiles[16 + t], (t - a) * 8 % TILE, 1), second)
+        out_ref[a, :, :TILE] = first.astype(BF16)
+        out_ref[a, :, TILE:] = second.astype(BF16)
+
+
+def granule_columns(rows, pivots):
+    return pl.pallas_call(
+        granule_columns_kernel,
+        out_shape=jax.ShapeDtypeStruct((16, 8, 2 * TILE), BF16),
+    )(rows, pivots)
+
+
+def parts_of(value):
+    high = lax.reduce_precision(value, 8, 7)
+    rest = value - high
+    middle = lax.reduce_precision(rest, 8, 7)
+    low = lax.reduce_precision(rest - middle, 8, 7)
+    return [high, middle, low]
 
 
 def pivot_solve(values, diagonal, joined):
@@ -152,35 +178,42 @@
     partial = jnp.dot(blocks, rhs_part, preferred_element_type=F32).astype(BF16)
     leaf_forward = summed(exchange(partial.reshape(8, 64, RHS), CX)).astype(BF16)
 
+    joined = jnp.repeat(root_doff * root_pairs.astype(F32), 2)
+    pivots = jnp.stack(parts_of(root_dinv) + parts_of(joined), axis=1)
+    pivots = jnp.pad(pivots, ((0, 2), (64, TILE - 70)))
+    root_block = granule_columns(jnp.pad(root_inverse, ((0, 2), (0, 0))), pivots)
+    root_block = exchange(root_block, GRAN).reshape(128, 2 * TILE)
+    pivots = root_block[:, 192:198].astype(F32)
+    dinv_rows = pivots[:, 0:1] + pivots[:, 1:2] + pivots[:, 2:3]
+    joined_rows = pivots[:, 3:4] + pivots[:, 4:5] + pivots[:, 5:6]
+    root_block = root_block[:, :192]
+
     update = leaf_update[0]
-    ordered = update.reshape(4, 3, 2, 8, 8, 64).transpose(2, 0, 3, 1, 4, 5).reshape(64, 24, 64)
-    chunk = jnp.arange(512, dtype=jnp.int32)
-    place = chunk // 8
-    x_of = place // 8 % 4
-    tile_row = 8 * (place // 32 * 8 + place % 8) + chunk % 8
-    row = TILE * (3 * lax.axis_index(YALL) + x_of) + tile_row
-    row = jnp.where(x_of < 3, row, -1) - 6 * lax.axis_index(AXES)
+    ordered = update.reshape(12, 16, 8, 64).transpose(1, 0, 2, 3).reshape(16, 96, 64)
+    at = jnp.arange(16 * 24, dtype=jnp.int32)
+    row = TILE * (3 * lax.axis_index(YALL) + at // 8 % 3) + 8 * (at // 24) + at % 8
+    row = row - 6 * lax.axis_index(AXES)
     select = (row[:, None] == jnp.arange(8, dtype=jnp.int32)[None, :]) & (row < 6)[:, None]
-    select = select.astype(BF16).reshape(64, 8, 8)
+    select = select.astype(BF16).reshape(16, 24, 8)
     left = jnp.concatenate(
         [jnp.pad(ordered, ((0, 0), (0, 0), (0, 8))), jnp.pad(select, ((0, 0), (0, 0), (64, 0)))], 1
-    ).reshape(2048, 72)
+    ).reshape(1920, 72)
     right = jnp.concatenate([leaf_forward, jnp.pad(root_rhs, ((0, 2), (0, 0)))], 0)
     term = jnp.dot(left, right, preferred_element_type=F32).astype(BF16)
-    term = summed(exchange(term.reshape(2, 1024, RHS), ("c",))).astype(BF16)
-    term = summed(exchange(term.reshape(32, 32, RHS), XZ)).astype(BF16)
-    reduced = combine(root_tiles, gather(term, PYX).reshape(128, 8, RHS))
-    reduced = both_cores(gather(reduced, Z)).reshape(16, ROOT_TILES, 8, RHS)
-    reduced = reduced.transpose(1, 0, 2, 3).reshape(ROOT_ROWS, RHS)
-
-    root_forward = jnp.dot(root_inverse, reduced, preferred_element_type=F32)
-    joined = jnp.repeat(root_doff * root_pairs.astype(F32), 2)[:, None]
-    root_scaled = pivot_solve(root_forward, root_dinv[:, None], joined).astype(BF16)
-    back = transposed_product(root_inverse, root_scaled).astype(BF16)
-    back = summed(exchange(back.reshape(2, ROOT_ROWS // 2, RHS), ("c",))).astype(BF16)
-    back = summed(exchange(back.reshape(32, 48, RHS), ZX)).astype(BF16)
+    term = summed(exchange(term.reshape(2, 960, RHS), ("c",))).astype(BF16)
+    term = summed(exchange(term.reshape(8, 120, RHS), Z)).astype(BF16)
+    term = summed(gather(term, ("x",))).astype(BF16)
+    reduced = combine(root_tiles, gather(term, YALL).reshape(120, 8, RHS)).reshape(192, RHS)
+
+    forward = jnp.dot(root_block, reduced, preferred_element_type=F32)
+    forward = forward + other_core(forward.astype(BF16)).astype(F32)
+    forward = summed(gather(forward.astype(BF16), Z))
+    root_scaled = pivot_solve(forward, dinv_rows, joined_rows).astype(BF16)
+    back = transposed_product(root_block, root_scaled).astype(BF16)
+    back = summed(exchange(back.reshape(4, 48, RHS), ("x",))).astype(BF16)
     root_part = summed(gather(back, YALL)).astype(BF16)
-    root_full = both_cores(gather(root_part, ZX)).reshape(ROOT_ROWS, RHS)
+    root_full = both_cores(gather(root_part, ZX)).reshape(16, ROOT_TILES, 8, RHS)
+    root_full = root_full.transpose(1, 0, 2, 3).reshape(ROOT_ROWS, RHS)
     root_own = lax.dynamic_slice_in_dim(root_full, lax.axis_index(AXES) * 6, 6, 0)
 
     tile_ids = lax.dynamic_index_in_dim(root_tiles, lax.axis_index("p"), 0, keepdims=False)

time: 203 us -> 200 us (0.985)
  blocking collectives: 111 us -> 58.9 us
  waiting for transfers between devices: 22.5 us -> 44.9 us
  starting transfers between devices: 52.6 us -> 71.9 us
  local copies, waits for them, and re-layouts: 5.39 us -> 11.2 us
    all_to_all x9 -> x6, blocking collectives: 111 us -> 58.9 us  [exchange(): return lax.all_to_all(blocks, axes, 0, 0)]
    all_to_all x3 -> x7, starting transfers between devices: 16.9 us -> 40.5 us  [exchange(): return lax.all_to_all(blocks, axes, 0, 0)]
    all_to_all x3 -> x7, waiting for transfers between devices: 14.6 us -> 37.7 us  [exchange(): return lax.all_to_all(blocks, axes, 0, 0)]
    ppermute x2, starting transfers between devices: 13.7 us -> 9.68 us  [other_core(): return lax.ppermute(value, 'c', [(0, 1), (1, 0)])]
    unnamed x21 -> x24, local copies, waits for them, and re-layouts: 0.42 us -> 3.44 us
  transfers between devices with their start and end apart: 9 -> 13, of which waited for: 7 -> 10; matrix products, arithmetic and copies ran while one was open for 1% -> 2% of each run, Pallas kernels for 1% -> 3%
where the time goes in v3:
time: 200 us; the launch traced here: 199 us
  starting transfers between devices  71.9 us (36%)
  blocking collectives  58.9 us (29%)
  waiting for transfers between devices  44.9 us (22%)
  local copies, waits for them, and re-layouts  11.2 us (6%)
  Pallas kernels  6.03 us (3%)
  matrix products  3.14 us (2%)
    all_to_all x6, blocking collectives, exchange(): return lax.all_to_all(blocks, axes, 0, 0)  58.9 us
    all_to_all x7, starting transfers between devices, exchange(): return lax.all_to_all(blocks, axes, 0, 0)  40.5 us
    all_to_all x7, waiting for transfers between devices, exchange(): return lax.all_to_all(blocks, axes, 0, 0)  37.7 us
    ppermute x4, starting transfers between devices, doubled(): other = lax.ppermute(held, axis, pairs)  21.8 us
    ppermute x2, starting transfers between devices, other_core(): return lax.ppermute(value, 'c', [(0, 1), (1, 0)])  9.68 us
    ppermute x4, waiting for transfers between devices, doubled(): other = lax.ppermute(held, axis, pairs)  6.41 us
  transfers between devices with their start and end apart: 13, of which 10 were waited for; matrix products, arithmetic and copies ran while one was open for 2% of the time, Pallas kernels for 3%

profile of v3, /device:TPU:1, one launch (start us, length us, event | category | flops | bytes accessed | tf_op | source)
XLA Modules:
  0.0 198.9 jit_solution(14032952206887735229)
XLA Ops:
  0.6 11.5 %collective-permute-start = (bf16[64,128]{1,0:T(8,128)(2,1)}, bf16[64,128]{1,0:T(8,128)(2,1)S(1)}, u32[]{:S(2)}, u32[]{:S(2)}) collective-permute-start(bf16[64,128]{1,0:T(8,128)(2,1)} %bitcast.120), channel_id=1, source_target_pairs={{0,4},{4,0},{1,5},{5,1},{2,6},{6,2},{3,7},{7,3},{8,12},{12,8},{9,1... | collective-permute-start | bytes 49160 | tf_op jit(solution)/shard_map/ppermute | solution.py:145
  12.1 2.7 %shard_map.131 = bf16[8,64,1024]{2,1,0:T(8,128)(2,1)} custom-call(bf16[64,8192]{1,0:T(8,128)(2,1)} %bitcast.103), custom_call_target="tpu_custom_call" | custom-call | tf_op jit(solution)/shard_map/pallas_call | solution.py:65
  14.7 5.3 %all-to-all-start = ((bf16[8,64,1024]{2,1,0:T(8,128)(2,1)}), bf16[8,64,1024]{2,1,0:T(8,128)(2,1)S(1)}, u32[]{:S(2)}, u32[]{:S(2)}) async-start(bf16[8,64,1024]{2,1,0:T(8,128)(2,1)} %shard_map.131), calls=%async_computation | async-start | bytes 2097152 | tf_op jit(solution)/shard_map/all_to_all | solution.py:33
  21.9 4.0 %collective-permute-start.1 = (bf16[2,64,128]{2,1,0:T(8,128)(2,1)S(1)}, bf16[2,64,128]{2,1,0:T(8,128)(2,1)S(1)}, u32[]{:S(2)}, u32[]{:S(2)}) collective-permute-start(bf16[2,64,128]{2,1,0:T(8,128)(2,1)S(1)} %maximum_select_fusion.6), channel_id=1, source_target_pairs={{0,32},{16,48},{32,0},{48,16},{1,33},{17,49},{33,1},{49,17},{2,34}... | collective-permute-start | bytes 98312 | tf_op jit(solution)/shard_map/ppermute | solution.py:145
  25.9 1.8 collective-permute-done.1
  27.7 3.1 %collective-permute-start.2 = (bf16[2,2,64,128]{3,2,1,0:T(8,128)(2,1)S(1)}, bf16[2,2,64,128]{3,2,1,0:T(8,128)(2,1)S(1)}, u32[]{:S(2)}, u32[]{:S(2)}) collective-permute-start(bf16[2,2,64,128]{3,2,1,0:T(8,128)(2,1)S(1)} %maximum_select_fusion.4), channel_id=1, source_target_pairs={{0,16},{16,0},{32,48},{48,32},{1,17},{17,1},{33,49},{49,33},{2,18}... | collective-permute-start | bytes 196616 | tf_op jit(solution)/shard_map/ppermute | solution.py:145
  30.9 2.2 %collective-permute-done.2 = bf16[2,2,64,128]{3,2,1,0:T(8,128)(2,1)S(1)} collective-permute-done((bf16[2,2,64,128]{3,2,1,0:T(8,128)(2,1)S(1)}, bf16[2,2,64,128]{3,2,1,0:T(8,128)(2,1)S(1)}, u32[]{:S(2)}, u32[]{:S(2)}) %collective-permute-start.2) | collective-permute-done | bytes 65568 | tf_op jit(solution)/shard_map/ppermute | solution.py:145
  33.1 3.2 %collective-permute-start.3 = (bf16[2,2,2,64,128]{4,3,2,1,0:T(8,128)(2,1)S(1)}, bf16[2,2,2,64,128]{4,3,2,1,0:T(8,128)(2,1)S(1)}, u32[]{:S(2)}, u32[]{:S(2)}) collective-permute-start(bf16[2,2,2,64,128]{4,3,2,1,0:T(8,128)(2,1)S(1)} %maximum_select_fusion.2), channel_id=1, source_target_pairs={{0,64},{64,0},{1,65},{65,1},{2,66},{66,2},{3,67},{67,3},{4,68},{68... | collective-permute-start | bytes 393224 | tf_op jit(solution)/shard_map/ppermute | solution.py:145
  36.3 2.4 %collective-permute-done.3 = bf16[2,2,2,64,128]{4,3,2,1,0:T(8,128)(2,1)S(1)} collective-permute-done((bf16[2,2,2,64,128]{4,3,2,1,0:T(8,128)(2,1)S(1)}, bf16[2,2,2,64,128]{4,3,2,1,0:T(8,128)(2,1)S(1)}, u32[]{:S(2)}, u32[]{:S(2)}) %collective-permute-start.3) | collective-permute-done | bytes 131104 | tf_op jit(solution)/shard_map/ppermute | solution.py:145
  40.1 8.0 %all-to-all-start.1 = ((bf16[8,64,128]{2,1,0:T(8,128)(2,1)}), bf16[8,64,128]{2,1,0:T(8,128)(2,1)S(1)}, u32[]{:S(2)}, u32[]{:S(2)}) async-start(bf16[8,64,128]{2,1,0:T(8,128)(2,1)} %bitcast.16), calls=%async_computation.1 | async-start | bytes 262144 | tf_op jit(solution)/shard_map/all_to_all | solution.py:33
  48.2 5.1 %all-to-all-done.1 = bf16[8,64,128]{2,1,0:T(8,128)(2,1)S(1)} async-done(((bf16[8,64,128]{2,1,0:T(8,128)(2,1)}), bf16[8,64,128]{2,1,0:T(8,128)(2,1)S(1)}, u32[]{:S(2)}, u32[]{:S(2)}) %all-to-all-start.1) | async-done | bytes 131104 | tf_op jit(solution)/shard_map/all_to_all | solution.py:33
  54.2 4.1 %all_to_all.65 = bf16[2,960,128]{2,1,0:T(8,128)(2,1)S(1)} all-to-all(bf16[2,960,128]{2,1,0:T(8,128)(2,1)S(1)} %bitcast.98), channel_id=1, replica_groups=mesh['p'=4,'yl'=2,'zl'=4,'c'=2,'zh'=2,'x'=4] {'c'}, dimensions={0} | all-to-all | bytes 983040 | tf_op jit(solution)/shard_map/all_to_all | solution.py:33
  58.5 11.2 %all_to_all.66 = bf16[8,120,128]{2,1,0:T(8,128)(2,1)S(1)} all-to-all(bf16[8,120,128]{2,1,0:T(8,128)(2,1)S(1)} %bitcast.106), channel_id=1, replica_groups=mesh['p'=4,'yl'=2,'zl'=4,'c'=2,'zh'=2,'x'=4] {'zl','zh'}, dimensions={0} | all-to-all | bytes 491520 | tf_op jit(solution)/shard_map/all_to_all | solution.py:33
  70.4 3.5 %all-to-all-start.5 = ((bf16[4,120,128]{2,1,0:T(8,128)(2,1)}), bf16[4,120,128]{2,1,0:T(8,128)(2,1)S(1)}, u32[]{:S(2)}, u32[]{:S(2)}) async-start(bf16[4,120,128]{2,1,0:T(8,128)(2,1)} %broadcast_in_dim.20), calls=%async_computation.5 | async-start | bytes 245760 | tf_op jit(solution)/shard_map/all_to_all | solution.py:33
  74.0 4.6 %all-to-all-done.5 = bf16[4,120,128]{2,1,0:T(8,128)(2,1)S(1)} async-done(((bf16[4,120,128]{2,1,0:T(8,128)(2,1)}), bf16[4,120,128]{2,1,0:T(8,128)(2,1)S(1)}, u32[]{:S(2)}, u32[]{:S(2)}) %all-to-all-start.5) | async-done | bytes 122912 | tf_op jit(solution)/shard_map/all_to_all | solution.py:33
  79.4 7.0 %all-to-all-start.6 = ((bf16[8,120,128]{2,1,0:T(8,128)(2,1)}), bf16[8,120,128]{2,1,0:T(8,128)(2,1)S(1)}, u32[]{:S(2)}, u32[]{:S(2)}) async-start(bf16[8,120,128]{2,1,0:T(8,128)(2,1)} %broadcast_in_dim.21), calls=%async_computation.6 | async-start | bytes 491520 | tf_op jit(solution)/shard_map/all_to_all | solution.py:33
  88.0 1.7 shard_map.132
  89.7 5.8 %all-to-all-done.6 = bf16[8,120,128]{2,1,0:T(8,128)(2,1)S(1)} async-done(((bf16[8,120,128]{2,1,0:T(8,128)(2,1)}), bf16[8,120,128]{2,1,0:T(8,128)(2,1)S(1)}, u32[]{:S(2)}, u32[]{:S(2)}) %all-to-all-start.6) | async-done | bytes 245792 | tf_op jit(solution)/shard_map/all_to_all | solution.py:33
  95.5 9.8 %all-to-all-start.2 = ((bf16[16,8,256]{2,1,0:T(8,128)(2,1)}), bf16[16,8,256]{2,1,0:T(8,128)(2,1)S(1)}, u32[]{:S(2)}, u32[]{:S(2)}) async-start(bf16[16,8,256]{2,1,0:T(8,128)(2,1)} %shard_map.132), calls=%async_computation.2 | async-start | bytes 131072 | tf_op jit(solution)/shard_map/all_to_all | solution.py:33
  105.4 1.7 shard_map.133
  107.1 5.8 %all-to-all-done.2 = bf16[16,8,256]{2,1,0:T(8,128)(2,1)S(1)} async-done(((bf16[16,8,256]{2,1,0:T(8,128)(2,1)}), bf16[16,8,256]{2,1,0:T(8,128)(2,1)S(1)}, u32[]{:S(2)}, u32[]{:S(2)}) %all-to-all-start.2) | async-done | bytes 65568 | tf_op jit(solution)/shard_map/all_to_all | solution.py:33
  112.8 0.9 fusion.47
  113.8 2.8 %collective-permute-start.4 = (bf16[128,128]{1,0:T(8,128)(2,1)S(1)}, bf16[128,128]{1,0:T(8,128)(2,1)S(1)}, u32[]{:S(2)}, u32[]{:S(2)}) collective-permute-start(bf16[128,128]{1,0:T(8,128)(2,1)S(1)} %get-tuple-element.14), channel_id=1, source_target_pairs={{0,8},{8,0},{1,9},{9,1},{2,10},{10,2},{3,11},{11,3},{4,12},{12,4},... | collective-permute-start | bytes 98312 | tf_op jit(solution)/shard_map/ppermute | solution.py:133
  118.1 3.4 %all-to-all-start.7 = ((bf16[8,128,128]{2,1,0:T(8,128)(2,1)}), bf16[8,128,128]{2,1,0:T(8,128)(2,1)S(1)}, u32[]{:S(2)}, u32[]{:S(2)}) async-start(bf16[8,128,128]{2,1,0:T(8,128)(2,1)} %broadcast_in_dim.22), calls=%async_computation.7 | async-start | bytes 524288 | tf_op jit(solution)/shard_map/all_to_all | solution.py:33
  121.7 6.9 %all-to-all-done.7 = bf16[8,128,128]{2,1,0:T(8,128)(2,1)S(1)} async-done(((bf16[8,128,128]{2,1,0:T(8,128)(2,1)}), bf16[8,128,128]{2,1,0:T(8,128)(2,1)S(1)}, u32[]{:S(2)}, u32[]{:S(2)}) %all-to-all-start.7) | async-done | bytes 262176 | tf_op jit(solution)/shard_map/all_to_all | solution.py:33
  129.1 6.7 %all_to_all.67 = bf16[4,48,128]{2,1,0:T(8,128)(2,1)S(1)} all-to-all(bf16[4,48,128]{2,1,0:T(8,128)(2,1)S(1)} %bitcast.119), channel_id=1, replica_groups=mesh['p'=4,'yl'=2,'zl'=4,'c'=2,'zh'=2,'x'=4] {'x'}, dimensions={0} | all-to-all | bytes 98304 | tf_op jit(solution)/shard_map/all_to_all | solution.py:33
  135.9 10.0 %all_to_all.68 = bf16[8,48,128]{2,1,0:T(8,128)(2,1)S(1)} all-to-all(bf16[8,48,128]{2,1,0:T(8,128)(2,1)S(1)} %broadcast_in_dim.23), channel_id=1, replica_groups=mesh['p'=4,'yl'=2,'zl'=4,'c'=2,'zh'=2,'x'=4] {'p','yl'}, dimensions={0} | all-to-all | bytes 196608 | tf_op jit(solution)/shard_map/all_to_all | solution.py:33
  145.9 19.2 %all_to_all.69 = bf16[32,48,128]{2,1,0:T(8,128)(2,1)S(1)} all-to-all(bf16[32,48,128]{2,1,0:T(8,128)(2,1)S(1)} %broadcast_in_dim.24), channel_id=1, replica_groups=mesh['p'=4,'yl'=2,'zl'=4,'c'=2,'zh'=2,'x'=4] {'zl','zh','x'}, dimensions={0} | all-to-all | bytes 786432 | tf_op jit(solution)/shard_map/all_to_all | solution.py:33
  165.2 6.9 %collective-permute-start.5 = (bf16[32,48,128]{2,1,0:T(8,128)(2,1)S(1)}, bf16[32,48,128]{2,1,0:T(8,128)(2,1)S(1)}, u32[]{:S(2)}, u32[]{:S(2)}) collective-permute-start(bf16[32,48,128]{2,1,0:T(8,128)(2,1)S(1)} %all_to_all.69), channel_id=1, source_target_pairs={{0,8},{8,0},{1,9},{9,1},{2,10},{10,2},{3,11},{11,3},{4,12},{12,4},... | collective-permute-start | bytes 1179656 | tf_op jit(solution)/shard_map/ppermute | solution.py:133
  175.8 7.6 %all_to_all.70 = bf16[8,64,128]{2,1,0:T(8,128)(2,1)S(1)} all-to-all(bf16[8,64,128]{2,1,0:T(8,128)(2,1)S(1)} %broadcast_in_dim.25), channel_id=1, replica_groups=mesh['p'=4,'yl'=2,'zl'=4,'c'=2,'zh'=2,'x'=4] {'c','x'}, dimensions={0} | all-to-all | bytes 262144 | tf_op jit(solution)/shard_map/all_to_all | solution.py:33
  184.6 3.5 %all-to-all-start.12 = ((bf16[16,64,128]{2,1,0:T(8,128)(2,1)}), bf16[16,64,128]{2,1,0:T(8,128)(2,1)S(1)}, u32[]{:S(2)}, u32[]{:S(2)}) async-start(bf16[16,64,128]{2,1,0:T(8,128)(2,1)} %bitcast.49), calls=%async_computation.12 | async-start | bytes 524288 | tf_op jit(solution)/shard_map/all_to_all | solution.py:33
  188.7 9.6 %all-to-all-done.12 = bf16[16,64,128]{2,1,0:T(8,128)(2,1)S(1)} async-done(((bf16[16,64,128]{2,1,0:T(8,128)(2,1)}), bf16[16,64,128]{2,1,0:T(8,128)(2,1)S(1)}, u32[]{:S(2)}, u32[]{:S(2)}) %all-to-all-start.12) | async-done | bytes 262176 | tf_op jit(solution)/shard_map/all_to_all | solution.py:33
  (91 shorter events, 16.0 us)
Async XLA Ops:
  0.6 20.6 %collective-permute-start = (bf16[64,128]{1,0:T(8,128)(2,1)}, bf16[64,128]{1,0:T(8,128)(2,1)S(1)}, u32[]{:S(2)}, u32[]{:S(2)}) collective-permute-start(bf16[64,128]{1,0:T(8,128)(2,1)} %bitcast.120), channel_id=1, source_target_pairs={{0,4},{4,0},{1,5},{5,1},{2,6},{6,2},{3,7},{7,3},{8,12},{12,8},{9,1... | collective-permute-start | bytes 49160 | tf_op jit(solution)/shard_map/ppermute | solution.py:145
  14.7 24.1 %all-to-all-start = ((bf16[8,64,1024]{2,1,0:T(8,128)(2,1)}), bf16[8,64,1024]{2,1,0:T(8,128)(2,1)S(1)}, u32[]{:S(2)}, u32[]{:S(2)}) async-start(bf16[8,64,1024]{2,1,0:T(8,128)(2,1)} %shard_map.131), calls=%async_computation | async-start | bytes 2097152 | tf_op jit(solution)/shard_map/all_to_all | solution.py:33
  20.0 0.9 copy-start.1
  21.2 0.7 copy-start.2
  21.9 5.8 %collective-permute-start.1 = (bf16[2,64,128]{2,1,0:T(8,128)(2,1)S(1)}, bf16[2,64,128]{2,1,0:T(8,128)(2,1)S(1)}, u32[]{:S(2)}, u32[]{:S(2)}) collective-permute-start(bf16[2,64,128]{2,1,0:T(8,128)(2,1)S(1)} %maximum_select_fusion.6), channel_id=1, source_target_pairs={{0,32},{16,48},{32,0},{48,16},{1,33},{17,49},{33,1},{49,17},{2,34}... | collective-permute-start | bytes 98312 | tf_op jit(solution)/shard_map/ppermute | solution.py:145
  27.7 5.3 %collective-permute-start.2 = (bf16[2,2,64,128]{3,2,1,0:T(8,128)(2,1)S(1)}, bf16[2,2,64,128]{3,2,1,0:T(8,128)(2,1)S(1)}, u32[]{:S(2)}, u32[]{:S(2)}) collective-permute-start(bf16[2,2,64,128]{3,2,1,0:T(8,128)(2,1)S(1)} %maximum_select_fusion.4), channel_id=1, source_target_pairs={{0,16},{16,0},{32,48},{48,32},{1,17},{17,1},{33,49},{49,33},{2,18}... | collective-permute-start | bytes 196616 | tf_op jit(solution)/shard_map/ppermute | solution.py:145
  33.1 5.7 %collective-permute-start.3 = (bf16[2,2,2,64,128]{4,3,2,1,0:T(8,128)(2,1)S(1)}, bf16[2,2,2,64,128]{4,3,2,1,0:T(8,128)(2,1)S(1)}, u32[]{:S(2)}, u32[]{:S(2)}) collective-permute-start(bf16[2,2,2,64,128]{4,3,2,1,0:T(8,128)(2,1)S(1)} %maximum_select_fusion.2), channel_id=1, source_target_pairs={{0,64},{64,0},{1,65},{65,1},{2,66},{66,2},{3,67},{67,3},{4,68},{68... | collective-permute-start | bytes 393224 | tf_op jit(solution)/shard_map/ppermute | solution.py:145
  40.1 13.2 %all-to-all-start.1 = ((bf16[8,64,128]{2,1,0:T(8,128)(2,1)}), bf16[8,64,128]{2,1,0:T(8,128)(2,1)S(1)}, u32[]{:S(2)}, u32[]{:S(2)}) async-start(bf16[8,64,128]{2,1,0:T(8,128)(2,1)} %bitcast.16), calls=%async_computation.1 | async-start | bytes 262144 | tf_op jit(solution)/shard_map/all_to_all | solution.py:33
  53.3 0.7 copy-start.4
  70.4 3.5 %copy-start.7 = (f32[3]{0:T(128)S(1)}, f32[3]{0:T(128)}, u32[]{:S(2)}) copy-start(f32[3]{0:T(128)} %param.22) | copy-start | bytes 40
  70.4 3.5 %copy-start.8 = (s32[3]{0:T(128)S(1)}, s32[3]{0:T(128)}, u32[]{:S(2)}) copy-start(s32[3]{0:T(128)} %param.23) | copy-start | bytes 40
  70.4 8.2 %all-to-all-start.5 = ((bf16[4,120,128]{2,1,0:T(8,128)(2,1)}), bf16[4,120,128]{2,1,0:T(8,128)(2,1)S(1)}, u32[]{:S(2)}, u32[]{:S(2)}) async-start(bf16[4,120,128]{2,1,0:T(8,128)(2,1)} %broadcast_in_dim.20), calls=%async_computation.5 | async-start | bytes 245760 | tf_op jit(solution)/shard_map/all_to_all | solution.py:33
  79.4 7.0 %copy-start.6 = (f32[6]{0:T(128)S(1)}, f32[6]{0:T(128)}, u32[]{:S(2)}) copy-start(f32[6]{0:T(128)} %param.21) | copy-start | bytes 76
  79.4 7.3 %copy-start.3 = (bf16[6,3072]{1,0:T(8,128)(2,1)S(1)}, bf16[6,3072]{1,0:T(8,128)(2,1)}, u32[]{:S(2)}) copy-start(bf16[6,3072]{1,0:T(8,128)(2,1)} %param.20) | copy-start | bytes 110596
  79.4 16.1 %all-to-all-start.6 = ((bf16[8,120,128]{2,1,0:T(8,128)(2,1)}), bf16[8,120,128]{2,1,0:T(8,128)(2,1)S(1)}, u32[]{:S(2)}, u32[]{:S(2)}) async-start(bf16[8,120,128]{2,1,0:T(8,128)(2,1)} %broadcast_in_dim.21), calls=%async_computation.6 | async-start | bytes 491520 | tf_op jit(solution)/shard_map/all_to_all | solution.py:33
  95.5 9.9 %copy-start = (bf16[8,120,128]{2,1,0:T(8,128)(2,1)}, bf16[8,120,128]{2,1,0:T(8,128)(2,1)S(1)}, u32[]{:S(2)}) copy-start(bf16[8,120,128]{2,1,0:T(8,128)(2,1)S(1)} %all-to-all-done.6) | copy-start | bytes 737284
  95.5 17.3 %all-to-all-start.2 = ((bf16[16,8,256]{2,1,0:T(8,128)(2,1)}), bf16[16,8,256]{2,1,0:T(8,128)(2,1)S(1)}, u32[]{:S(2)}, u32[]{:S(2)}) async-start(bf16[16,8,256]{2,1,0:T(8,128)(2,1)} %shard_map.132), calls=%async_computation.2 | async-start | bytes 131072 | tf_op jit(solution)/shard_map/all_to_all | solution.py:33
  113.8 3.6 %collective-permute-start.4 = (bf16[128,128]{1,0:T(8,128)(2,1)S(1)}, bf16[128,128]{1,0:T(8,128)(2,1)S(1)}, u32[]{:S(2)}, u32[]{:S(2)}) collective-permute-start(bf16[128,128]{1,0:T(8,128)(2,1)S(1)} %get-tuple-element.14), channel_id=1, source_target_pairs={{0,8},{8,0},{1,9},{9,1},{2,10},{10,2},{3,11},{11,3},{4,12},{12,4},... | collective-permute-start | bytes 98312 | tf_op jit(solution)/shard_map/ppermute | solution.py:133
  118.1 10.5 %all-to-all-start.7 = ((bf16[8,128,128]{2,1,0:T(8,128)(2,1)}), bf16[8,128,128]{2,1,0:T(8,128)(2,1)S(1)}, u32[]{:S(2)}, u32[]{:S(2)}) async-start(bf16[8,128,128]{2,1,0:T(8,128)(2,1)} %broadcast_in_dim.22), calls=%async_computation.7 | async-start | bytes 524288 | tf_op jit(solution)/shard_map/all_to_all | solution.py:33
  165.2 8.6 %collective-permute-start.5 = (bf16[32,48,128]{2,1,0:T(8,128)(2,1)S(1)}, bf16[32,48,128]{2,1,0:T(8,128)(2,1)S(1)}, u32[]{:S(2)}, u32[]{:S(2)}) collective-permute-start(bf16[32,48,128]{2,1,0:T(8,128)(2,1)S(1)} %all_to_all.69), channel_id=1, source_target_pairs={{0,8},{8,0},{1,9},{9,1},{2,10},{10,2},{3,11},{11,3},{4,12},{12,4},... | collective-permute-start | bytes 1179656 | tf_op jit(solution)/shard_map/ppermute | solution.py:133
  172.1 0.7 copy-start.9
  172.1 0.7 copy-start.10
  174.9 0.7 copy-start.5
  184.6 13.7 %all-to-all-start.12 = ((bf16[16,64,128]{2,1,0:T(8,128)(2,1)}), bf16[16,64,128]{2,1,0:T(8,128)(2,1)S(1)}, u32[]{:S(2)}, u32[]{:S(2)}) async-start(bf16[16,64,128]{2,1,0:T(8,128)(2,1)} %bitcast.49), calls=%async_computation.12 | async-start | bytes 524288 | tf_op jit(solution)/shard_map/all_to_all | solution.py:33

commit v4 on v3

--- a/solution.py
+++ b/solution.py
@@ -12,7 +12,6 @@
 TILE = 128
 RHS = 128
 ROOT_ROWS = ROOT_TILES * TILE
-LEAF_ROWS = 8192
 
 AXES = ("p", "yl", "zl", "c", "zh", "x")
 SIZES = (4, 2, 4, 2, 2, 4)
@@ -22,7 +21,6 @@
 YZ = ("yl", "zl", "zh")
 YALL = ("p", "yl")
 Z = ("zl", "zh")
-GRAN = ("c", "zl", "zh")
 ZX = ("zl", "zh", "x")
 
 F32 = jnp.float32
@@ -151,6 +149,26 @@
     held = doubled(held, "zl", 1, zl % 2 == 0, 1)
     held = doubled(held, "yl", 1, lax.axis_index("yl") == 0, 0)
     return held.reshape(1024, RHS)
+
+
+def spread_granules(blocks):
+    zl = lax.axis_index("zl")
+    blocks = blocks.reshape((2, 2, 2, 2) + blocks.shape[1:])
+    steps = (
+        (3, "zh", 1, lax.axis_index("zh")),
+        (1, "zl", 2, zl // 2),
+        (2, "zl", 1, zl % 2),
+        (0, "c", 1, lax.axis_index("c")),
+    )
+    for dim, axis, mask, bit in steps:
+        low = bit == 0
+        first = lax.index_in_dim(blocks, 0, dim, keepdims=False)
+        second = lax.index_in_dim(blocks, 1, dim, keepdims=False)
+        keep = jnp.where(low, first, second)
+        send = jnp.where(low, second, first)
+        other = lax.ppermute(send, axis, [(i, i ^ mask) for i in range(lax.axis_size(axis))])
+        blocks = jnp.where(low, jnp.stack([keep, other], dim), jnp.stack([other, keep], dim))
+    return blocks
 
 
 def transposed_product(matrix, vector):
@@ -176,13 +194,14 @@
     blocks = exchange(split_columns(leaf_inverse[0]), CX).reshape(512, 1024)
     rhs_part = gather_leaf_rhs(leaf_rhs[0])
     partial = jnp.dot(blocks, rhs_part, preferred_element_type=F32).astype(BF16)
-    leaf_forward = summed(exchange(partial.reshape(8, 64, RHS), CX)).astype(BF16)
+    partial = exchange(partial.reshape(8, 64, RHS), CX)
+    leaf_forward = summed(partial).astype(BF16)
 
     joined = jnp.repeat(root_doff * root_pairs.astype(F32), 2)
     pivots = jnp.stack(parts_of(root_dinv) + parts_of(joined), axis=1)
     pivots = jnp.pad(pivots, ((0, 2), (64, TILE - 70)))
     root_block = granule_columns(jnp.pad(root_inverse, ((0, 2), (0, 0))), pivots)
-    root_block = exchange(root_block, GRAN).reshape(128, 2 * TILE)
+    root_block = spread_granules(root_block).reshape(128, 2 * TILE)
     pivots = root_block[:, 192:198].astype(F32)
     dinv_rows = pivots[:, 0:1] + pivots[:, 1:2] + pivots[:, 2:3]
     joined_rows = pivots[:, 3:4] + pivots[:, 4:5] + pivots[:, 5:6]
@@ -201,9 +220,12 @@
     right = jnp.concatenate([leaf_forward, jnp.pad(root_rhs, ((0, 2), (0, 0)))], 0)
     term = jnp.dot(left, right, preferred_element_type=F32).astype(BF16)
     term = summed(exchange(term.reshape(2, 960, RHS), ("c",))).astype(BF16)
-    term = summed(exchange(term.reshape(8, 120, RHS), Z)).astype(BF16)
-    term = summed(gather(term, ("x",))).astype(BF16)
-    reduced = combine(root_tiles, gather(term, YALL).reshape(120, 8, RHS)).reshape(192, RHS)
+    term = exchange(term.reshape(8, 120, RHS), Z)
+    term = summed(term).astype(BF16)
+    term = gather(term, ("x",))
+    term = summed(term).astype(BF16)
+    term = gather(term, YALL)
+    reduced = combine(root_tiles, term.reshape(120, 8, RHS)).reshape(192, RHS)
 
     forward = jnp.dot(root_block, reduced, preferred_element_type=F32)
     forward = forward + other_core(forward.astype(BF16)).astype(F32)
@@ -249,6 +271,7 @@
         P(AXES),
     )
     out_specs = (P(LEAF, NODE, None), P(AXES, None))
+
     return jax.shard_map(
         on_device, mesh=fine, in_specs=in_specs, out_specs=out_specs, check_vma=False
     )

time: 200 us -> 201 us (level)
  starting transfers between devices: 71.9 us -> 85 us
  blocking collectives: 58.9 us -> 47.7 us
  waiting for transfers between devices: 44.9 us -> 41.4 us
    ppermute x0 -> x4, starting transfers between devices: none -> 15.9 us  [spread_granules(): lax.ppermute(send, axis, [(i, i ^ mask) for i in range(lax.axis_size(axis...]
    all_to_all x6 -> x5, blocking collectives: 58.9 us -> 47.7 us  [exchange(): return lax.all_to_all(blocks, axes, 0, 0)]
    all_to_all x7, waiting for transfers between devices: 37.7 us -> 28.9 us  [exchange(): return lax.all_to_all(blocks, axes, 0, 0)]
    ppermute x2, starting transfers between devices: 9.68 us -> 14.6 us  [other_core(): return lax.ppermute(value, 'c', [(0, 1), (1, 0)])]
    all_to_all x7, starting transfers between devices: 40.5 us -> 36.4 us  [exchange(): return lax.all_to_all(blocks, axes, 0, 0)]
    ppermute x4, starting transfers between devices: 21.8 us -> 18.1 us  [doubled(): other = lax.ppermute(held, axis, pairs)]
    ppermute x0 -> x4, waiting for transfers between devices: none -> 2.92 us  [spread_granules(): lax.ppermute(send, axis, [(i, i ^ mask) for i in range(lax.axis_size(axis...]
    ppermute x4, waiting for transfers between devices: 6.41 us -> 8.71 us  [doubled(): other = lax.ppermute(held, axis, pairs)]
  transfers between devices with their start and end apart: 13 -> 17, of which waited for: 10 -> 12; matrix products, arithmetic and copies ran while one was open for 2% -> 4% of each run, Pallas kernels for 3% -> 2%
where the time goes in v4:
time: 201 us; the launch traced here: 199 us
  starting transfers between devices  85 us (42%)
  blocking collectives  47.7 us (24%)
  waiting for transfers between devices  41.4 us (21%)
  local copies, waits for them, and re-layouts  12.1 us (6%)
  Pallas kernels  6.03 us (3%)
  matrix products  3.13 us (2%)
  other arithmetic  2.79 us (1%)
    all_to_all x5, blocking collectives, exchange(): return lax.all_to_all(blocks, axes, 0, 0)  47.7 us
    all_to_all x7, starting transfers between devices, exchange(): return lax.all_to_all(blocks, axes, 0, 0)  36.4 us
    all_to_all x7, waiting for transfers between devices, exchange(): return lax.all_to_all(blocks, axes, 0, 0)  28.9 us
    ppermute x4, starting transfers between devices, doubled(): other = lax.ppermute(held, axis, pairs)  18.1 us
    ppermute x4, starting transfers between devices, spread_granules(): lax.ppermute(send, axis, [(i, i ^ mask) for i in range(lax.axis_size(axis...  15.9 us
    ppermute x2, starting transfers between devices, other_core(): return lax.ppermute(value, 'c', [(0, 1), (1, 0)])  14.6 us
    ppermute x4, waiting for transfers between devices, doubled(): other = lax.ppermute(held, axis, pairs)  8.71 us
  transfers between devices with their start and end apart: 17, of which 12 were waited for; matrix products, arithmetic and copies ran while one was open for 4% of the time, Pallas kernels for 2%

profile of v4, /device:TPU:1, one launch (start us, length us, event | category | flops | bytes accessed | tf_op | source)
XLA Modules:
  0.0 199.4 jit_solution(1677183208321044207)
XLA Ops:
  0.6 11.5 %collective-permute-start = (bf16[64,128]{1,0:T(8,128)(2,1)}, bf16[64,128]{1,0:T(8,128)(2,1)S(1)}, u32[]{:S(2)}, u32[]{:S(2)}) collective-permute-start(bf16[64,128]{1,0:T(8,128)(2,1)} %bitcast.147), channel_id=1, source_target_pairs={{0,4},{4,0},{1,5},{5,1},{2,6},{6,2},{3,7},{7,3},{8,12},{12,8},{9,1... | collective-permute-start | bytes 49160 | tf_op jit(solution)/shard_map/ppermute | solution.py:143
  12.1 2.7 %shard_map.131 = bf16[8,64,1024]{2,1,0:T(8,128)(2,1)} custom-call(bf16[64,8192]{1,0:T(8,128)(2,1)} %bitcast.130), custom_call_target="tpu_custom_call" | custom-call | tf_op jit(solution)/shard_map/pallas_call | solution.py:63
  14.8 5.4 %all-to-all-start = ((bf16[8,64,1024]{2,1,0:T(8,128)(2,1)}), bf16[8,64,1024]{2,1,0:T(8,128)(2,1)S(1)}, u32[]{:S(2)}, u32[]{:S(2)}) async-start(bf16[8,64,1024]{2,1,0:T(8,128)(2,1)} %shard_map.131), calls=%async_computation | async-start | bytes 2097152 | tf_op jit(solution)/shard_map/all_to_all | solution.py:31
  24.5 3.2 %collective-permute-start.4 = (bf16[2,2,2,8,256]{4,3,0,2,1:T(8,128)(2,1)S(1)}, bf16[2,2,2,8,256]{4,3,0,2,1:T(8,128)(2,1)S(1)}, u32[]{:S(2)}, u32[]{:S(2)}) collective-permute-start(bf16[2,2,2,8,256]{4,3,0,2,1:T(8,128)(2,1)S(1)} %select_bitcast_fusion.3), channel_id=1, source_target_pairs={{0,4},{4,0},{1,5},{5,1},{2,6},{6,2},{3,7},{7,3},{8,12},{12,8},{9,1... | collective-permute-start | bytes 98312 | tf_op jit(solution)/shard_map/ppermute | solution.py:169
  29.3 2.9 %collective-permute-start.1 = (bf16[2,64,128]{2,1,0:T(8,128)(2,1)S(1)}, bf16[2,64,128]{2,1,0:T(8,128)(2,1)S(1)}, u32[]{:S(2)}, u32[]{:S(2)}) collective-permute-start(bf16[2,64,128]{2,1,0:T(8,128)(2,1)S(1)} %maximum_select_fusion.10), channel_id=1, source_target_pairs={{0,32},{16,48},{32,0},{48,16},{1,33},{17,49},{33,1},{49,17},{2,34}... | collective-permute-start | bytes 98312 | tf_op jit(solution)/shard_map/ppermute | solution.py:143
  32.1 2.1 %collective-permute-done.4 = bf16[2,2,2,8,256]{4,3,0,2,1:T(8,128)(2,1)S(1)} collective-permute-done((bf16[2,2,2,8,256]{4,3,0,2,1:T(8,128)(2,1)S(1)}, bf16[2,2,2,8,256]{4,3,0,2,1:T(8,128)(2,1)S(1)}, u32[]{:S(2)}, u32[]{:S(2)}) %collective-permute-start.4) | collective-permute-done | bytes 32800 | tf_op jit(solution)/shard_map/ppermute | solution.py:169
  34.2 1.9 collective-permute-done.1
  36.2 1.9 collective-permute-start.2
  38.1 3.0 %collective-permute-done.2 = bf16[2,2,64,128]{3,2,1,0:T(8,128)(2,1)S(1)} collective-permute-done((bf16[2,2,64,128]{3,2,1,0:T(8,128)(2,1)S(1)}, bf16[2,2,64,128]{3,2,1,0:T(8,128)(2,1)S(1)}, u32[]{:S(2)}, u32[]{:S(2)}) %collective-permute-start.2) | collective-permute-done | bytes 65568 | tf_op jit(solution)/shard_map/ppermute | solution.py:143
  41.2 1.9 collective-permute-start.3
  43.2 3.7 %collective-permute-done.3 = bf16[2,2,2,64,128]{4,3,2,1,0:T(8,128)(2,1)S(1)} collective-permute-done((bf16[2,2,2,64,128]{4,3,2,1,0:T(8,128)(2,1)S(1)}, bf16[2,2,2,64,128]{4,3,2,1,0:T(8,128)(2,1)S(1)}, u32[]{:S(2)}, u32[]{:S(2)}) %collective-permute-start.3) | collective-permute-done | bytes 131104 | tf_op jit(solution)/shard_map/ppermute | solution.py:143
  48.2 7.2 %all-to-all-start.1 = ((bf16[8,64,128]{2,1,0:T(8,128)(2,1)}), bf16[8,64,128]{2,1,0:T(8,128)(2,1)S(1)}, u32[]{:S(2)}, u32[]{:S(2)}) async-start(bf16[8,64,128]{2,1,0:T(8,128)(2,1)} %bitcast.16), calls=%async_computation.1 | async-start | bytes 262144 | tf_op jit(solution)/shard_map/all_to_all | solution.py:31
  55.5 2.7 %collective-permute-start.5 = (bf16[2,2,2,8,256]{4,3,2,0,1:T(8,128)(2,1)S(1)}, bf16[2,2,2,8,256]{4,3,2,0,1:T(8,128)(2,1)S(1)}, u32[]{:S(2)}, u32[]{:S(2)}) collective-permute-start(bf16[2,2,2,8,256]{4,3,2,0,1:T(8,128)(2,1)S(1)} %select_bitcast_fusion.2), channel_id=1, source_target_pairs={{0,32},{16,48},{32,0},{48,16},{1,33},{17,49},{33,1},{49,17},{2,34}... | collective-permute-start | bytes 98312 | tf_op jit(solution)/shard_map/ppermute | solution.py:169
  58.2 2.5 %all-to-all-done.1 = bf16[8,64,128]{2,1,0:T(8,128)(2,1)S(1)} async-done(((bf16[8,64,128]{2,1,0:T(8,128)(2,1)}), bf16[8,64,128]{2,1,0:T(8,128)(2,1)S(1)}, u32[]{:S(2)}, u32[]{:S(2)}) %all-to-all-start.1) | async-done | bytes 131104 | tf_op jit(solution)/shard_map/all_to_all | solution.py:31
  61.6 4.1 %all_to_all.60 = bf16[2,960,128]{2,1,0:T(8,128)(2,1)S(1)} all-to-all(bf16[2,960,128]{2,1,0:T(8,128)(2,1)S(1)} %bitcast.125), channel_id=1, replica_groups=mesh['p'=4,'yl'=2,'zl'=4,'c'=2,'zh'=2,'x'=4] {'c'}, dimensions={0} | all-to-all | bytes 983040 | tf_op jit(solution)/shard_map/all_to_all | solution.py:31
  66.5 5.8 %all-to-all-start.3 = ((bf16[8,120,128]{2,1,0:T(8,128)(2,1)}), bf16[8,120,128]{2,1,0:T(8,128)(2,1)S(1)}, u32[]{:S(2)}, u32[]{:S(2)}) async-start(bf16[8,120,128]{2,1,0:T(8,128)(2,1)} %bitcast.49), calls=%async_computation.3 | async-start | bytes 491520 | tf_op jit(solution)/shard_map/all_to_all | solution.py:31
  72.4 3.4 %collective-permute-start.6 = (bf16[2,2,2,8,256]{4,3,2,1,0:T(8,128)(2,1)S(1)}, bf16[2,2,2,8,256]{4,3,2,1,0:T(8,128)(2,1)S(1)}, u32[]{:S(2)}, u32[]{:S(2)}) collective-permute-start(bf16[2,2,2,8,256]{4,3,2,1,0:T(8,128)(2,1)S(1)} %select_bitcast_fusion.1), channel_id=1, source_target_pairs={{0,16},{16,0},{32,48},{48,32},{1,17},{17,1},{33,49},{49,33},{2,18}... | collective-permute-start | bytes 98312 | tf_op jit(solution)/shard_map/ppermute | solution.py:169
  75.8 3.7 %all-to-all-done.3 = bf16[8,120,128]{2,1,0:T(8,128)(2,1)S(1)} async-done(((bf16[8,120,128]{2,1,0:T(8,128)(2,1)}), bf16[8,120,128]{2,1,0:T(8,128)(2,1)S(1)}, u32[]{:S(2)}, u32[]{:S(2)}) %all-to-all-start.3) | async-done | bytes 245792 | tf_op jit(solution)/shard_map/all_to_all | solution.py:31
  80.2 3.3 %all-to-all-start.4 = ((bf16[4,120,128]{2,1,0:T(8,128)(2,1)}), bf16[4,120,128]{2,1,0:T(8,128)(2,1)S(1)}, u32[]{:S(2)}, u32[]{:S(2)}) async-start(bf16[4,120,128]{2,1,0:T(8,128)(2,1)} %broadcast_in_dim.20), calls=%async_computation.4 | async-start | bytes 245760 | tf_op jit(solution)/shard_map/all_to_all | solution.py:31
  83.5 4.7 %all-to-all-done.4 = bf16[4,120,128]{2,1,0:T(8,128)(2,1)S(1)} async-done(((bf16[4,120,128]{2,1,0:T(8,128)(2,1)}), bf16[4,120,128]{2,1,0:T(8,128)(2,1)S(1)}, u32[]{:S(2)}, u32[]{:S(2)}) %all-to-all-start.4) | async-done | bytes 122912 | tf_op jit(solution)/shard_map/all_to_all | solution.py:31
  89.0 6.8 %all-to-all-start.5 = ((bf16[8,120,128]{2,1,0:T(8,128)(2,1)}), bf16[8,120,128]{2,1,0:T(8,128)(2,1)S(1)}, u32[]{:S(2)}, u32[]{:S(2)}) async-start(bf16[8,120,128]{2,1,0:T(8,128)(2,1)} %broadcast_in_dim.21), calls=%async_computation.5 | async-start | bytes 491520 | tf_op jit(solution)/shard_map/all_to_all | solution.py:31
  95.9 6.6 %collective-permute-start.7 = (bf16[2,2,2,8,256]{4,3,2,1,0:T(8,128)(2,1)S(1)}, bf16[2,2,2,8,256]{4,3,2,1,0:T(8,128)(2,1)S(1)}, u32[]{:S(2)}, u32[]{:S(2)}) collective-permute-start(bf16[2,2,2,8,256]{4,3,2,1,0:T(8,128)(2,1)S(1)} %get-tuple-element.9), channel_id=1, source_target_pairs={{0,8},{8,0},{1,9},{9,1},{2,10},{10,2},{3,11},{11,3},{4,12},{12,4},... | collective-permute-start | bytes 98312 | tf_op jit(solution)/shard_map/ppermute | solution.py:169
  108.4 7.7 %collective-permute-start.8 = (bf16[128,128]{1,0:T(8,128)(2,1)S(1)}, bf16[128,128]{1,0:T(8,128)(2,1)S(1)}, u32[]{:S(2)}, u32[]{:S(2)}) collective-permute-start(bf16[128,128]{1,0:T(8,128)(2,1)S(1)} %get-tuple-element.18), channel_id=1, source_target_pairs={{0,8},{8,0},{1,9},{9,1},{2,10},{10,2},{3,11},{11,3},{4,12},{12,4},... | collective-permute-start | bytes 98312 | tf_op jit(solution)/shard_map/ppermute | solution.py:131
  117.7 4.3 %all-to-all-start.6 = ((bf16[8,128,128]{2,1,0:T(8,128)(2,1)}), bf16[8,128,128]{2,1,0:T(8,128)(2,1)S(1)}, u32[]{:S(2)}, u32[]{:S(2)}) async-start(bf16[8,128,128]{2,1,0:T(8,128)(2,1)} %broadcast_in_dim.22), calls=%async_computation.6 | async-start | bytes 524288 | tf_op jit(solution)/shard_map/all_to_all | solution.py:31
  122.3 6.8 %all-to-all-done.6 = bf16[8,128,128]{2,1,0:T(8,128)(2,1)S(1)} async-done(((bf16[8,128,128]{2,1,0:T(8,128)(2,1)}), bf16[8,128,128]{2,1,0:T(8,128)(2,1)S(1)}, u32[]{:S(2)}, u32[]{:S(2)}) %all-to-all-start.6) | async-done | bytes 262176 | tf_op jit(solution)/shard_map/all_to_all | solution.py:31
  129.5 6.7 %all_to_all.61 = bf16[4,48,128]{2,1,0:T(8,128)(2,1)S(1)} all-to-all(bf16[4,48,128]{2,1,0:T(8,128)(2,1)S(1)} %bitcast.146), channel_id=1, replica_groups=mesh['p'=4,'yl'=2,'zl'=4,'c'=2,'zh'=2,'x'=4] {'x'}, dimensions={0} | all-to-all | bytes 98304 | tf_op jit(solution)/shard_map/all_to_all | solution.py:31
  136.3 10.0 %all_to_all.62 = bf16[8,48,128]{2,1,0:T(8,128)(2,1)S(1)} all-to-all(bf16[8,48,128]{2,1,0:T(8,128)(2,1)S(1)} %broadcast_in_dim.23), channel_id=1, replica_groups=mesh['p'=4,'yl'=2,'zl'=4,'c'=2,'zh'=2,'x'=4] {'p','yl'}, dimensions={0} | all-to-all | bytes 196608 | tf_op jit(solution)/shard_map/all_to_all | solution.py:31
  146.3 19.3 %all_to_all.63 = bf16[32,48,128]{2,1,0:T(8,128)(2,1)S(1)} all-to-all(bf16[32,48,128]{2,1,0:T(8,128)(2,1)S(1)} %broadcast_in_dim.24), channel_id=1, replica_groups=mesh['p'=4,'yl'=2,'zl'=4,'c'=2,'zh'=2,'x'=4] {'zl','zh','x'}, dimensions={0} | all-to-all | bytes 786432 | tf_op jit(solution)/shard_map/all_to_all | solution.py:31
  165.6 6.9 %collective-permute-start.9 = (bf16[32,48,128]{2,1,0:T(8,128)(2,1)S(1)}, bf16[32,48,128]{2,1,0:T(8,128)(2,1)S(1)}, u32[]{:S(2)}, u32[]{:S(2)}) collective-permute-start(bf16[32,48,128]{2,1,0:T(8,128)(2,1)S(1)} %all_to_all.63), channel_id=1, source_target_pairs={{0,8},{8,0},{1,9},{9,1},{2,10},{10,2},{3,11},{11,3},{4,12},{12,4},... | collective-permute-start | bytes 1179656 | tf_op jit(solution)/shard_map/ppermute | solution.py:131
  176.2 7.6 %all_to_all.64 = bf16[8,64,128]{2,1,0:T(8,128)(2,1)S(1)} all-to-all(bf16[8,64,128]{2,1,0:T(8,128)(2,1)S(1)} %broadcast_in_dim.25), channel_id=1, replica_groups=mesh['p'=4,'yl'=2,'zl'=4,'c'=2,'zh'=2,'x'=4] {'c','x'}, dimensions={0} | all-to-all | bytes 262144 | tf_op jit(solution)/shard_map/all_to_all | solution.py:31
  185.0 3.5 %all-to-all-start.11 = ((bf16[16,64,128]{2,1,0:T(8,128)(2,1)}), bf16[16,64,128]{2,1,0:T(8,128)(2,1)S(1)}, u32[]{:S(2)}, u32[]{:S(2)}) async-start(bf16[16,64,128]{2,1,0:T(8,128)(2,1)} %bitcast.65), calls=%async_computation.11 | async-start | bytes 524288 | tf_op jit(solution)/shard_map/all_to_all | solution.py:31
  189.2 9.6 %all-to-all-done.11 = bf16[16,64,128]{2,1,0:T(8,128)(2,1)S(1)} async-done(((bf16[16,64,128]{2,1,0:T(8,128)(2,1)}), bf16[16,64,128]{2,1,0:T(8,128)(2,1)S(1)}, u32[]{:S(2)}, u32[]{:S(2)}) %all-to-all-start.11) | async-done | bytes 262176 | tf_op jit(solution)/shard_map/all_to_all | solution.py:31
  (108 shorter events, 24.8 us)
Async XLA Ops:
  0.6 27.9 %collective-permute-start = (bf16[64,128]{1,0:T(8,128)(2,1)}, bf16[64,128]{1,0:T(8,128)(2,1)S(1)}, u32[]{:S(2)}, u32[]{:S(2)}) collective-permute-start(bf16[64,128]{1,0:T(8,128)(2,1)} %bitcast.147), channel_id=1, source_target_pairs={{0,4},{4,0},{1,5},{5,1},{2,6},{6,2},{3,7},{7,3},{8,12},{12,8},{9,1... | collective-permute-start | bytes 49160 | tf_op jit(solution)/shard_map/ppermute | solution.py:143
  14.7 5.4 %copy-start.7 = (f32[3]{0:T(128)S(1)}, f32[3]{0:T(128)}, u32[]{:S(2)}) copy-start(f32[3]{0:T(128)} %param.22) | copy-start | bytes 40
  14.7 5.4 %copy-start.8 = (s32[3]{0:T(128)S(1)}, s32[3]{0:T(128)}, u32[]{:S(2)}) copy-start(s32[3]{0:T(128)} %param.23) | copy-start | bytes 40
  14.7 5.6 %copy-start.6 = (f32[6]{0:T(128)S(1)}, f32[6]{0:T(128)}, u32[]{:S(2)}) copy-start(f32[6]{0:T(128)} %param.21) | copy-start | bytes 76
  14.8 32.2 %all-to-all-start = ((bf16[8,64,1024]{2,1,0:T(8,128)(2,1)}), bf16[8,64,1024]{2,1,0:T(8,128)(2,1)S(1)}, u32[]{:S(2)}, u32[]{:S(2)}) async-start(bf16[8,64,1024]{2,1,0:T(8,128)(2,1)} %shard_map.131), calls=%async_computation | async-start | bytes 2097152 | tf_op jit(solution)/shard_map/all_to_all | solution.py:31
  20.1 1.2 copy-start.3
  24.5 3.6 %copy-start.1 = (bf16[1,1536,64]{1,2,0:T(8,128)(2,1)S(1)}, bf16[1,1536,64]{1,2,0:T(8,128)(2,1)}, u32[]{:S(2)}) copy-start(bf16[1,1536,64]{1,2,0:T(8,128)(2,1)} %param.14) | copy-start | bytes 589828
  24.5 9.8 %collective-permute-start.4 = (bf16[2,2,2,8,256]{4,3,0,2,1:T(8,128)(2,1)S(1)}, bf16[2,2,2,8,256]{4,3,0,2,1:T(8,128)(2,1)S(1)}, u32[]{:S(2)}, u32[]{:S(2)}) collective-permute-start(bf16[2,2,2,8,256]{4,3,0,2,1:T(8,128)(2,1)S(1)} %select_bitcast_fusion.3), channel_id=1, source_target_pairs={{0,4},{4,0},{1,5},{5,1},{2,6},{6,2},{3,7},{7,3},{8,12},{12,8},{9,1... | collective-permute-start | bytes 98312 | tf_op jit(solution)/shard_map/ppermute | solution.py:169
  28.5 0.7 copy-start.2
  29.3 6.9 %collective-permute-start.1 = (bf16[2,64,128]{2,1,0:T(8,128)(2,1)S(1)}, bf16[2,64,128]{2,1,0:T(8,128)(2,1)S(1)}, u32[]{:S(2)}, u32[]{:S(2)}) collective-permute-start(bf16[2,64,128]{2,1,0:T(8,128)(2,1)S(1)} %maximum_select_fusion.10), channel_id=1, source_target_pairs={{0,32},{16,48},{32,0},{48,16},{1,33},{17,49},{33,1},{49,17},{2,34}... | collective-permute-start | bytes 98312 | tf_op jit(solution)/shard_map/ppermute | solution.py:143
  36.2 5.0 %collective-permute-start.2 = (bf16[2,2,64,128]{3,2,1,0:T(8,128)(2,1)S(1)}, bf16[2,2,64,128]{3,2,1,0:T(8,128)(2,1)S(1)}, u32[]{:S(2)}, u32[]{:S(2)}) collective-permute-start(bf16[2,2,64,128]{3,2,1,0:T(8,128)(2,1)S(1)} %maximum_select_fusion.4), channel_id=1, source_target_pairs={{0,16},{16,0},{32,48},{48,32},{1,17},{17,1},{33,49},{49,33},{2,18}... | collective-permute-start | bytes 196616 | tf_op jit(solution)/shard_map/ppermute | solution.py:143
  41.2 5.7 %collective-permute-start.3 = (bf16[2,2,2,64,128]{4,3,2,1,0:T(8,128)(2,1)S(1)}, bf16[2,2,2,64,128]{4,3,2,1,0:T(8,128)(2,1)S(1)}, u32[]{:S(2)}, u32[]{:S(2)}) collective-permute-start(bf16[2,2,2,64,128]{4,3,2,1,0:T(8,128)(2,1)S(1)} %maximum_select_fusion.2), channel_id=1, source_target_pairs={{0,64},{64,0},{1,65},{65,1},{2,66},{66,2},{3,67},{67,3},{4,68},{68... | collective-permute-start | bytes 393224 | tf_op jit(solution)/shard_map/ppermute | solution.py:143
  48.2 12.4 %all-to-all-start.1 = ((bf16[8,64,128]{2,1,0:T(8,128)(2,1)}), bf16[8,64,128]{2,1,0:T(8,128)(2,1)S(1)}, u32[]{:S(2)}, u32[]{:S(2)}) async-start(bf16[8,64,128]{2,1,0:T(8,128)(2,1)} %bitcast.16), calls=%async_computation.1 | async-start | bytes 262144 | tf_op jit(solution)/shard_map/all_to_all | solution.py:31
  55.5 16.9 %collective-permute-start.5 = (bf16[2,2,2,8,256]{4,3,2,0,1:T(8,128)(2,1)S(1)}, bf16[2,2,2,8,256]{4,3,2,0,1:T(8,128)(2,1)S(1)}, u32[]{:S(2)}, u32[]{:S(2)}) collective-permute-start(bf16[2,2,2,8,256]{4,3,2,0,1:T(8,128)(2,1)S(1)} %select_bitcast_fusion.2), channel_id=1, source_target_pairs={{0,32},{16,48},{32,0},{48,16},{1,33},{17,49},{33,1},{49,17},{2,34}... | collective-permute-start | bytes 98312 | tf_op jit(solution)/shard_map/ppermute | solution.py:169
  60.6 0.7 copy-start.4
  66.5 12.9 %all-to-all-start.3 = ((bf16[8,120,128]{2,1,0:T(8,128)(2,1)}), bf16[8,120,128]{2,1,0:T(8,128)(2,1)S(1)}, u32[]{:S(2)}, u32[]{:S(2)}) async-start(bf16[8,120,128]{2,1,0:T(8,128)(2,1)} %bitcast.49), calls=%async_computation.3 | async-start | bytes 491520 | tf_op jit(solution)/shard_map/all_to_all | solution.py:31
  72.4 23.4 %collective-permute-start.6 = (bf16[2,2,2,8,256]{4,3,2,1,0:T(8,128)(2,1)S(1)}, bf16[2,2,2,8,256]{4,3,2,1,0:T(8,128)(2,1)S(1)}, u32[]{:S(2)}, u32[]{:S(2)}) collective-permute-start(bf16[2,2,2,8,256]{4,3,2,1,0:T(8,128)(2,1)S(1)} %select_bitcast_fusion.1), channel_id=1, source_target_pairs={{0,16},{16,0},{32,48},{48,32},{1,17},{17,1},{33,49},{49,33},{2,18}... | collective-permute-start | bytes 98312 | tf_op jit(solution)/shard_map/ppermute | solution.py:169
  80.2 8.1 %all-to-all-start.4 = ((bf16[4,120,128]{2,1,0:T(8,128)(2,1)}), bf16[4,120,128]{2,1,0:T(8,128)(2,1)S(1)}, u32[]{:S(2)}, u32[]{:S(2)}) async-start(bf16[4,120,128]{2,1,0:T(8,128)(2,1)} %broadcast_in_dim.20), calls=%async_computation.4 | async-start | bytes 245760 | tf_op jit(solution)/shard_map/all_to_all | solution.py:31
  89.0 16.0 %all-to-all-start.5 = ((bf16[8,120,128]{2,1,0:T(8,128)(2,1)}), bf16[8,120,128]{2,1,0:T(8,128)(2,1)S(1)}, u32[]{:S(2)}, u32[]{:S(2)}) async-start(bf16[8,120,128]{2,1,0:T(8,128)(2,1)} %broadcast_in_dim.21), calls=%async_computation.5 | async-start | bytes 491520 | tf_op jit(solution)/shard_map/all_to_all | solution.py:31
  95.9 7.4 %collective-permute-start.7 = (bf16[2,2,2,8,256]{4,3,2,1,0:T(8,128)(2,1)S(1)}, bf16[2,2,2,8,256]{4,3,2,1,0:T(8,128)(2,1)S(1)}, u32[]{:S(2)}, u32[]{:S(2)}) collective-permute-start(bf16[2,2,2,8,256]{4,3,2,1,0:T(8,128)(2,1)S(1)} %get-tuple-element.9), channel_id=1, source_target_pairs={{0,8},{8,0},{1,9},{9,1},{2,10},{10,2},{3,11},{11,3},{4,12},{12,4},... | collective-permute-start | bytes 98312 | tf_op jit(solution)/shard_map/ppermute | solution.py:169
  105.0 0.7 copy-start
  108.4 8.6 %collective-permute-start.8 = (bf16[128,128]{1,0:T(8,128)(2,1)S(1)}, bf16[128,128]{1,0:T(8,128)(2,1)S(1)}, u32[]{:S(2)}, u32[]{:S(2)}) collective-permute-start(bf16[128,128]{1,0:T(8,128)(2,1)S(1)} %get-tuple-element.18), channel_id=1, source_target_pairs={{0,8},{8,0},{1,9},{9,1},{2,10},{10,2},{3,11},{11,3},{4,12},{12,4},... | collective-permute-start | bytes 98312 | tf_op jit(solution)/shard_map/ppermute | solution.py:131
  117.7 11.4 %all-to-all-start.6 = ((bf16[8,128,128]{2,1,0:T(8,128)(2,1)}), bf16[8,128,128]{2,1,0:T(8,128)(2,1)S(1)}, u32[]{:S(2)}, u32[]{:S(2)}) async-start(bf16[8,128,128]{2,1,0:T(8,128)(2,1)} %broadcast_in_dim.22), calls=%async_computation.6 | async-start | bytes 524288 | tf_op jit(solution)/shard_map/all_to_all | solution.py:31
  165.6 8.6 %collective-permute-start.9 = (bf16[32,48,128]{2,1,0:T(8,128)(2,1)S(1)}, bf16[32,48,128]{2,1,0:T(8,128)(2,1)S(1)}, u32[]{:S(2)}, u32[]{:S(2)}) collective-permute-start(bf16[32,48,128]{2,1,0:T(8,128)(2,1)S(1)} %all_to_all.63), channel_id=1, source_target_pairs={{0,8},{8,0},{1,9},{9,1},{2,10},{10,2},{3,11},{11,3},{4,12},{12,4},... | collective-permute-start | bytes 1179656 | tf_op jit(solution)/shard_map/ppermute | solution.py:131
  172.5 0.7 copy-start.9
  172.6 0.7 copy-start.10
  175.3 0.7 copy-start.5
  185.0 13.7 %all-to-all-start.11 = ((bf16[16,64,128]{2,1,0:T(8,128)(2,1)}), bf16[16,64,128]{2,1,0:T(8,128)(2,1)S(1)}, u32[]{:S(2)}, u32[]{:S(2)}) async-start(bf16[16,64,128]{2,1,0:T(8,128)(2,1)} %bitcast.65), calls=%async_computation.11 | async-start | bytes 524288 | tf_op jit(solution)/shard_map/all_to_all | solution.py:31

commit v5 on v3

--- a/solution.py
+++ b/solution.py
@@ -12,7 +12,6 @@
 TILE = 128
 RHS = 128
 ROOT_ROWS = ROOT_TILES * TILE
-LEAF_ROWS = 8192
 
 AXES = ("p", "yl", "zl", "c", "zh", "x")
 SIZES = (4, 2, 4, 2, 2, 4)
@@ -22,7 +21,6 @@
 YZ = ("yl", "zl", "zh")
 YALL = ("p", "yl")
 Z = ("zl", "zh")
-GRAN = ("c", "zl", "zh")
 ZX = ("zl", "zh", "x")
 
 F32 = jnp.float32
@@ -94,23 +92,28 @@
 
 
 def granule_columns_kernel(source_ref, pivots_ref, out_ref):
-    slot = lax.broadcasted_iota(jnp.int32, (8, TILE), 1) // 8
+    lane = lax.broadcasted_iota(jnp.int32, (6, TILE), 1)
+    slot = lane // 8
     tiles = [source_ref[:, t * TILE : (t + 1) * TILE].astype(F32) for t in range(ROOT_TILES)]
+    spare = jnp.zeros((6, TILE), F32)
+    for j in range(6):
+        spare = jnp.where(lane == 64 + j, pivots_ref[:, j : j + 1], spare)
+    out_ref[...] = jnp.zeros_like(out_ref)
     for a in range(16):
-        first = tiles[0] * 0.0
-        second = pivots_ref[...]
+        first = spare
+        second = spare
         for t in range(16):
             first = jnp.where(slot == t, pltpu.roll(tiles[t], (t - a) * 8 % TILE, 1), first)
         for t in range(8):
             second = jnp.where(slot == t, pltpu.roll(tiles[16 + t], (t - a) * 8 % TILE, 1), second)
-        out_ref[a, :, :TILE] = first.astype(BF16)
-        out_ref[a, :, TILE:] = second.astype(BF16)
+        out_ref[a, 0, :6] = first.astype(BF16)
+        out_ref[a, 1, :6] = second.astype(BF16)
 
 
 def granule_columns(rows, pivots):
     return pl.pallas_call(
         granule_columns_kernel,
-        out_shape=jax.ShapeDtypeStruct((16, 8, 2 * TILE), BF16),
+        out_shape=jax.ShapeDtypeStruct((16, 2, 8, TILE), BF16),
     )(rows, pivots)
 
 
@@ -176,17 +179,12 @@
     blocks = exchange(split_columns(leaf_inverse[0]), CX).reshape(512, 1024)
     rhs_part = gather_leaf_rhs(leaf_rhs[0])
     partial = jnp.dot(blocks, rhs_part, preferred_element_type=F32).astype(BF16)
-    leaf_forward = summed(exchange(partial.reshape(8, 64, RHS), CX)).astype(BF16)
+    partial = exchange(partial.reshape(8, 64, RHS), CX)
+    leaf_forward = summed(partial).astype(BF16)
 
     joined = jnp.repeat(root_doff * root_pairs.astype(F32), 2)
     pivots = jnp.stack(parts_of(root_dinv) + parts_of(joined), axis=1)
-    pivots = jnp.pad(pivots, ((0, 2), (64, TILE - 70)))
-    root_block = granule_columns(jnp.pad(root_inverse, ((0, 2), (0, 0))), pivots)
-    root_block = exchange(root_block, GRAN).reshape(128, 2 * TILE)
-    pivots = root_block[:, 192:198].astype(F32)
-    dinv_rows = pivots[:, 0:1] + pivots[:, 1:2] + pivots[:, 2:3]
-    joined_rows = pivots[:, 3:4] + pivots[:, 4:5] + pivots[:, 5:6]
-    root_block = root_block[:, :192]
+    root_block = granule_columns(root_inverse, pivots)
 
     update = leaf_update[0]
     ordered = update.reshape(12, 16, 8, 64).transpose(1, 0, 2, 3).reshape(16, 96, 64)
@@ -200,8 +198,17 @@
     ).reshape(1920, 72)
     right = jnp.concatenate([leaf_forward, jnp.pad(root_rhs, ((0, 2), (0, 0)))], 0)
     term = jnp.dot(left, right, preferred_element_type=F32).astype(BF16)
-    term = summed(exchange(term.reshape(2, 960, RHS), ("c",))).astype(BF16)
-    term = summed(exchange(term.reshape(8, 120, RHS), Z)).astype(BF16)
+    term = jnp.concatenate([term.reshape(2, 8, 120, RHS), root_block.reshape(2, 8, 16, RHS)], 2)
+    term = exchange(term.reshape(2, 1088, RHS), ("c",)).reshape(2, 8, 136, RHS)
+    root_block = term[:, :, 120:].transpose(1, 0, 2, 3).reshape(8, 32, RHS)
+    term = summed(term[:, :, :120]).astype(BF16)
+    term = exchange(jnp.concatenate([term, root_block], 1), Z)
+    root_block = term[:, 120:].reshape(8, 2, 2, 8, RHS).transpose(0, 1, 3, 2, 4).reshape(128, 2 * TILE)
+    pivots = root_block[:, 192:198].astype(F32)
+    dinv_rows = pivots[:, 0:1] + pivots[:, 1:2] + pivots[:, 2:3]
+    joined_rows = pivots[:, 3:4] + pivots[:, 4:5] + pivots[:, 5:6]
+    root_block = root_block[:, :192]
+    term = summed(term[:, :120]).astype(BF16)
     term = summed(gather(term, ("x",))).astype(BF16)
     reduced = combine(root_tiles, gather(term, YALL).reshape(120, 8, RHS)).reshape(192, RHS)
 
@@ -249,6 +256,7 @@
         P(AXES),
     )
     out_specs = (P(LEAF, NODE, None), P(AXES, None))
+
     return jax.shard_map(
         on_device, mesh=fine, in_specs=in_specs, out_specs=out_specs, check_vma=False
     )

time: 200 us -> 192 us (0.960)
  blocking collectives: 58.9 us -> 69.6 us
  starting transfers between devices: 71.9 us -> 63.4 us
  waiting for transfers between devices: 44.9 us -> 38.2 us
  local copies, waits for them, and re-layouts: 11.2 us -> 7.26 us
    all_to_all x7 -> x5, starting transfers between devices: 40.5 us -> 27.2 us  [exchange(): return lax.all_to_all(blocks, axes, 0, 0)]
    all_to_all x6 -> x7, blocking collectives: 58.9 us -> 69.6 us  [exchange(): return lax.all_to_all(blocks, axes, 0, 0)]
    all_to_all x7 -> x5, waiting for transfers between devices: 37.7 us -> 30.7 us  [exchange(): return lax.all_to_all(blocks, axes, 0, 0)]
    ppermute x2, starting transfers between devices: 9.68 us -> 14.4 us  [other_core(): return lax.ppermute(value, 'c', [(0, 1), (1, 0)])]
    unnamed x24 -> x23, local copies, waits for them, and re-layouts: 3.44 us -> 0.95 us
  transfers between devices with their start and end apart: 13 -> 11, of which waited for: 10 -> 9; matrix products, arithmetic and copies ran while one was open for 2% -> 2% of each run, Pallas kernels for 3% -> 2%
where the time goes in v5:
time: 192 us; the launch traced here: 191 us
  blocking collectives  69.6 us (36%)
  starting transfers between devices  63.4 us (33%)
  waiting for transfers between devices  38.2 us (20%)
  local copies, waits for them, and re-layouts  7.26 us (4%)
  Pallas kernels  6.04 us (3%)
  matrix products  3.14 us (2%)
  other arithmetic  2 us (1%)
    all_to_all x7, blocking collectives, exchange(): return lax.all_to_all(blocks, axes, 0, 0)  69.6 us
    all_to_all x5, waiting for transfers between devices, exchange(): return lax.all_to_all(blocks, axes, 0, 0)  30.7 us
    all_to_all x5, starting transfers between devices, exchange(): return lax.all_to_all(blocks, axes, 0, 0)  27.2 us
    ppermute x4, starting transfers between devices, doubled(): other = lax.ppermute(held, axis, pairs)  21.8 us
    ppermute x2, starting transfers between devices, other_core(): return lax.ppermute(value, 'c', [(0, 1), (1, 0)])  14.4 us
    ppermute x4, waiting for transfers between devices, doubled(): other = lax.ppermute(held, axis, pairs)  6.38 us
  transfers between devices with their start and end apart: 11, of which 9 were waited for; matrix products, arithmetic and copies ran while one was open for 2% of the time, Pallas kernels for 2%

profile of v5, /device:TPU:1, one launch (start us, length us, event | category | flops | bytes accessed | tf_op | source)
XLA Modules:
  0.0 190.9 jit_solution(6741649785247419561)
XLA Ops:
  0.6 11.5 %collective-permute-start = (bf16[64,128]{1,0:T(8,128)(2,1)}, bf16[64,128]{1,0:T(8,128)(2,1)S(1)}, u32[]{:S(2)}, u32[]{:S(2)}) collective-permute-start(bf16[64,128]{1,0:T(8,128)(2,1)} %bitcast.129), channel_id=1, source_target_pairs={{0,4},{4,0},{1,5},{5,1},{2,6},{6,2},{3,7},{7,3},{8,12},{12,8},{9,1... | collective-permute-start | bytes 49160 | tf_op jit(solution)/shard_map/ppermute | solution.py:148
  12.1 2.6 %shard_map.131 = bf16[8,64,1024]{2,1,0:T(8,128)(2,1)} custom-call(bf16[64,8192]{1,0:T(8,128)(2,1)} %bitcast.111), custom_call_target="tpu_custom_call" | custom-call | tf_op jit(solution)/shard_map/pallas_call | solution.py:63
  14.8 5.4 %all-to-all-start = ((bf16[8,64,1024]{2,1,0:T(8,128)(2,1)}), bf16[8,64,1024]{2,1,0:T(8,128)(2,1)S(1)}, u32[]{:S(2)}, u32[]{:S(2)}) async-start(bf16[8,64,1024]{2,1,0:T(8,128)(2,1)} %shard_map.131), calls=%async_computation | async-start | bytes 2097152 | tf_op jit(solution)/shard_map/all_to_all | solution.py:31
  22.0 1.7 shard_map.132
  23.7 4.0 %collective-permute-start.1 = (bf16[2,64,128]{2,1,0:T(8,128)(2,1)S(1)}, bf16[2,64,128]{2,1,0:T(8,128)(2,1)S(1)}, u32[]{:S(2)}, u32[]{:S(2)}) collective-permute-start(bf16[2,64,128]{2,1,0:T(8,128)(2,1)S(1)} %maximum_select_fusion.6), channel_id=1, source_target_pairs={{0,32},{16,48},{32,0},{48,16},{1,33},{17,49},{33,1},{49,17},{2,34}... | collective-permute-start | bytes 98312 | tf_op jit(solution)/shard_map/ppermute | solution.py:148
  27.8 1.8 collective-permute-done.1
  29.6 3.1 %collective-permute-start.2 = (bf16[2,2,64,128]{3,2,1,0:T(8,128)(2,1)S(1)}, bf16[2,2,64,128]{3,2,1,0:T(8,128)(2,1)S(1)}, u32[]{:S(2)}, u32[]{:S(2)}) collective-permute-start(bf16[2,2,64,128]{3,2,1,0:T(8,128)(2,1)S(1)} %maximum_select_fusion.4), channel_id=1, source_target_pairs={{0,16},{16,0},{32,48},{48,32},{1,17},{17,1},{33,49},{49,33},{2,18}... | collective-permute-start | bytes 196616 | tf_op jit(solution)/shard_map/ppermute | solution.py:148
  32.7 2.2 %collective-permute-done.2 = bf16[2,2,64,128]{3,2,1,0:T(8,128)(2,1)S(1)} collective-permute-done((bf16[2,2,64,128]{3,2,1,0:T(8,128)(2,1)S(1)}, bf16[2,2,64,128]{3,2,1,0:T(8,128)(2,1)S(1)}, u32[]{:S(2)}, u32[]{:S(2)}) %collective-permute-start.2) | collective-permute-done | bytes 65568 | tf_op jit(solution)/shard_map/ppermute | solution.py:148
  34.9 3.2 %collective-permute-start.3 = (bf16[2,2,2,64,128]{4,3,2,1,0:T(8,128)(2,1)S(1)}, bf16[2,2,2,64,128]{4,3,2,1,0:T(8,128)(2,1)S(1)}, u32[]{:S(2)}, u32[]{:S(2)}) collective-permute-start(bf16[2,2,2,64,128]{4,3,2,1,0:T(8,128)(2,1)S(1)} %maximum_select_fusion.2), channel_id=1, source_target_pairs={{0,64},{64,0},{1,65},{65,1},{2,66},{66,2},{3,67},{67,3},{4,68},{68... | collective-permute-start | bytes 393224 | tf_op jit(solution)/shard_map/ppermute | solution.py:148
  38.1 2.4 %collective-permute-done.3 = bf16[2,2,2,64,128]{4,3,2,1,0:T(8,128)(2,1)S(1)} collective-permute-done((bf16[2,2,2,64,128]{4,3,2,1,0:T(8,128)(2,1)S(1)}, bf16[2,2,2,64,128]{4,3,2,1,0:T(8,128)(2,1)S(1)}, u32[]{:S(2)}, u32[]{:S(2)}) %collective-permute-start.3) | collective-permute-done | bytes 131104 | tf_op jit(solution)/shard_map/ppermute | solution.py:148
  41.1 0.8 copy.50
  41.9 8.0 %all-to-all-start.1 = ((bf16[8,64,128]{2,1,0:T(8,128)(2,1)}), bf16[8,64,128]{2,1,0:T(8,128)(2,1)S(1)}, u32[]{:S(2)}, u32[]{:S(2)}) async-start(bf16[8,64,128]{2,1,0:T(8,128)(2,1)} %bitcast.16), calls=%async_computation.1 | async-start | bytes 262144 | tf_op jit(solution)/shard_map/all_to_all | solution.py:31
  50.0 5.1 %all-to-all-done.1 = bf16[8,64,128]{2,1,0:T(8,128)(2,1)S(1)} async-done(((bf16[8,64,128]{2,1,0:T(8,128)(2,1)}), bf16[8,64,128]{2,1,0:T(8,128)(2,1)S(1)}, u32[]{:S(2)}, u32[]{:S(2)}) %all-to-all-start.1) | async-done | bytes 131104 | tf_op jit(solution)/shard_map/all_to_all | solution.py:31
  55.5 4.2 %all_to_all.60 = bf16[2,1088,128]{2,1,0:T(8,128)(2,1)S(1)} all-to-all(bf16[2,1088,128]{2,1,0:T(8,128)(2,1)S(1)} %bitcast.102), channel_id=1, replica_groups=mesh['p'=4,'yl'=2,'zl'=4,'c'=2,'zh'=2,'x'=4] {'c'}, dimensions={0} | all-to-all | bytes 1114112 | tf_op jit(solution)/shard_map/all_to_all | solution.py:31
  59.8 14.3 %all_to_all.61 = bf16[8,152,128]{2,1,0:T(8,128)(2,1)S(1)} all-to-all(bf16[8,152,128]{2,1,0:T(8,128)(2,1)S(1)} %pad_maximum_fusion.1), channel_id=1, replica_groups=mesh['p'=4,'yl'=2,'zl'=4,'c'=2,'zh'=2,'x'=4] {'zl','zh'}, dimensions={0} | all-to-all | bytes 622592 | tf_op jit(solution)/shard_map/all_to_all | solution.py:31
  74.2 7.3 %all_to_all.62 = bf16[4,120,128]{2,1,0:T(8,128)(2,1)S(1)} all-to-all(bf16[4,120,128]{2,1,0:T(8,128)(2,1)S(1)} %broadcast_in_dim.20), channel_id=1, replica_groups=mesh['p'=4,'yl'=2,'zl'=4,'c'=2,'zh'=2,'x'=4] {'x'}, dimensions={0} | all-to-all | bytes 245760 | tf_op jit(solution)/shard_map/all_to_all | solution.py:31
  82.2 6.8 %all-to-all-start.5 = ((bf16[8,120,128]{2,1,0:T(8,128)(2,1)}), bf16[8,120,128]{2,1,0:T(8,128)(2,1)S(1)}, u32[]{:S(2)}, u32[]{:S(2)}) async-start(bf16[8,120,128]{2,1,0:T(8,128)(2,1)} %broadcast_in_dim.21), calls=%async_computation.5 | async-start | bytes 491520 | tf_op jit(solution)/shard_map/all_to_all | solution.py:31
  89.0 9.3 %all-to-all-done.5 = bf16[8,120,128]{2,1,0:T(8,128)(2,1)S(1)} async-done(((bf16[8,120,128]{2,1,0:T(8,128)(2,1)}), bf16[8,120,128]{2,1,0:T(8,128)(2,1)S(1)}, u32[]{:S(2)}, u32[]{:S(2)}) %all-to-all-start.5) | async-done | bytes 245792 | tf_op jit(solution)/shard_map/all_to_all | solution.py:31
  98.9 1.7 shard_map.133
  100.6 0.9 fusion.49
  101.6 7.5 %collective-permute-start.4 = (bf16[128,128]{1,0:T(8,128)(2,1)S(1)}, bf16[128,128]{1,0:T(8,128)(2,1)S(1)}, u32[]{:S(2)}, u32[]{:S(2)}) collective-permute-start(bf16[128,128]{1,0:T(8,128)(2,1)S(1)} %get-tuple-element.14), channel_id=1, source_target_pairs={{0,8},{8,0},{1,9},{9,1},{2,10},{10,2},{3,11},{11,3},{4,12},{12,4},... | collective-permute-start | bytes 98312 | tf_op jit(solution)/shard_map/ppermute | solution.py:136
  109.1 0.8 collective-permute-done.4
  110.7 3.4 %all-to-all-start.6 = ((bf16[8,128,128]{2,1,0:T(8,128)(2,1)}), bf16[8,128,128]{2,1,0:T(8,128)(2,1)S(1)}, u32[]{:S(2)}, u32[]{:S(2)}) async-start(bf16[8,128,128]{2,1,0:T(8,128)(2,1)} %broadcast_in_dim.22), calls=%async_computation.6 | async-start | bytes 524288 | tf_op jit(solution)/shard_map/all_to_all | solution.py:31
  114.4 6.8 %all-to-all-done.6 = bf16[8,128,128]{2,1,0:T(8,128)(2,1)S(1)} async-done(((bf16[8,128,128]{2,1,0:T(8,128)(2,1)}), bf16[8,128,128]{2,1,0:T(8,128)(2,1)S(1)}, u32[]{:S(2)}, u32[]{:S(2)}) %all-to-all-start.6) | async-done | bytes 262176 | tf_op jit(solution)/shard_map/all_to_all | solution.py:31
  121.7 6.7 %all_to_all.63 = bf16[4,48,128]{2,1,0:T(8,128)(2,1)S(1)} all-to-all(bf16[4,48,128]{2,1,0:T(8,128)(2,1)S(1)} %bitcast.128), channel_id=1, replica_groups=mesh['p'=4,'yl'=2,'zl'=4,'c'=2,'zh'=2,'x'=4] {'x'}, dimensions={0} | all-to-all | bytes 98304 | tf_op jit(solution)/shard_map/all_to_all | solution.py:31
  128.5 10.0 %all_to_all.64 = bf16[8,48,128]{2,1,0:T(8,128)(2,1)S(1)} all-to-all(bf16[8,48,128]{2,1,0:T(8,128)(2,1)S(1)} %broadcast_in_dim.23), channel_id=1, replica_groups=mesh['p'=4,'yl'=2,'zl'=4,'c'=2,'zh'=2,'x'=4] {'p','yl'}, dimensions={0} | all-to-all | bytes 196608 | tf_op jit(solution)/shard_map/all_to_all | solution.py:31
  138.5 19.2 %all_to_all.65 = bf16[32,48,128]{2,1,0:T(8,128)(2,1)S(1)} all-to-all(bf16[32,48,128]{2,1,0:T(8,128)(2,1)S(1)} %broadcast_in_dim.24), channel_id=1, replica_groups=mesh['p'=4,'yl'=2,'zl'=4,'c'=2,'zh'=2,'x'=4] {'zl','zh','x'}, dimensions={0} | all-to-all | bytes 786432 | tf_op jit(solution)/shard_map/all_to_all | solution.py:31
  157.8 6.9 %collective-permute-start.5 = (bf16[32,48,128]{2,1,0:T(8,128)(2,1)S(1)}, bf16[32,48,128]{2,1,0:T(8,128)(2,1)S(1)}, u32[]{:S(2)}, u32[]{:S(2)}) collective-permute-start(bf16[32,48,128]{2,1,0:T(8,128)(2,1)S(1)} %all_to_all.65), channel_id=1, source_target_pairs={{0,8},{8,0},{1,9},{9,1},{2,10},{10,2},{3,11},{11,3},{4,12},{12,4},... | collective-permute-start | bytes 1179656 | tf_op jit(solution)/shard_map/ppermute | solution.py:136
  167.4 7.9 %all_to_all.66 = bf16[8,64,128]{2,1,0:T(8,128)(2,1)S(1)} all-to-all(bf16[8,64,128]{2,1,0:T(8,128)(2,1)S(1)} %broadcast_in_dim.25), channel_id=1, replica_groups=mesh['p'=4,'yl'=2,'zl'=4,'c'=2,'zh'=2,'x'=4] {'c','x'}, dimensions={0} | all-to-all | bytes 262144 | tf_op jit(solution)/shard_map/all_to_all | solution.py:31
  175.7 0.8 copy.62
  176.5 3.5 %all-to-all-start.11 = ((bf16[16,64,128]{2,1,0:T(8,128)(2,1)}), bf16[16,64,128]{2,1,0:T(8,128)(2,1)S(1)}, u32[]{:S(2)}, u32[]{:S(2)}) async-start(bf16[16,64,128]{2,1,0:T(8,128)(2,1)} %bitcast.55), calls=%async_computation.11 | async-start | bytes 524288 | tf_op jit(solution)/shard_map/all_to_all | solution.py:31
  180.7 9.6 %all-to-all-done.11 = bf16[16,64,128]{2,1,0:T(8,128)(2,1)S(1)} async-done(((bf16[16,64,128]{2,1,0:T(8,128)(2,1)}), bf16[16,64,128]{2,1,0:T(8,128)(2,1)S(1)}, u32[]{:S(2)}, u32[]{:S(2)}) %all-to-all-start.11) | async-done | bytes 262176 | tf_op jit(solution)/shard_map/all_to_all | solution.py:31
  (89 shorter events, 10.2 us)
Async XLA Ops:
  0.6 23.1 %collective-permute-start = (bf16[64,128]{1,0:T(8,128)(2,1)}, bf16[64,128]{1,0:T(8,128)(2,1)S(1)}, u32[]{:S(2)}, u32[]{:S(2)}) collective-permute-start(bf16[64,128]{1,0:T(8,128)(2,1)} %bitcast.129), channel_id=1, source_target_pairs={{0,4},{4,0},{1,5},{5,1},{2,6},{6,2},{3,7},{7,3},{8,12},{12,8},{9,1... | collective-permute-start | bytes 49160 | tf_op jit(solution)/shard_map/ppermute | solution.py:148
  14.7 5.5 %copy-start.7 = (f32[3]{0:T(128)S(1)}, f32[3]{0:T(128)}, u32[]{:S(2)}) copy-start(f32[3]{0:T(128)} %param.22) | copy-start | bytes 40
  14.7 5.5 %copy-start.8 = (s32[3]{0:T(128)S(1)}, s32[3]{0:T(128)}, u32[]{:S(2)}) copy-start(s32[3]{0:T(128)} %param.23) | copy-start | bytes 40
  14.7 5.7 %copy-start.6 = (f32[6]{0:T(128)S(1)}, f32[6]{0:T(128)}, u32[]{:S(2)}) copy-start(f32[6]{0:T(128)} %param.21) | copy-start | bytes 76
  14.7 6.0 %copy-start.1 = (bf16[1,1536,64]{1,2,0:T(8,128)(2,1)S(1)}, bf16[1,1536,64]{1,2,0:T(8,128)(2,1)}, u32[]{:S(2)}) copy-start(bf16[1,1536,64]{1,2,0:T(8,128)(2,1)} %param.14) | copy-start | bytes 589828
  14.8 25.9 %all-to-all-start = ((bf16[8,64,1024]{2,1,0:T(8,128)(2,1)}), bf16[8,64,1024]{2,1,0:T(8,128)(2,1)S(1)}, u32[]{:S(2)}, u32[]{:S(2)}) async-start(bf16[8,64,1024]{2,1,0:T(8,128)(2,1)} %shard_map.131), calls=%async_computation | async-start | bytes 2097152 | tf_op jit(solution)/shard_map/all_to_all | solution.py:31
  20.1 3.6 %copy-start.3 = (bf16[1,64,128]{2,1,0:T(8,128)(2,1)S(1)}, bf16[1,64,128]{2,1,0:T(8,128)(2,1)}, u32[]{:S(2)}) copy-start(bf16[1,64,128]{2,1,0:T(8,128)(2,1)} %param.12) | copy-start | bytes 49156
  23.7 5.8 %collective-permute-start.1 = (bf16[2,64,128]{2,1,0:T(8,128)(2,1)S(1)}, bf16[2,64,128]{2,1,0:T(8,128)(2,1)S(1)}, u32[]{:S(2)}, u32[]{:S(2)}) collective-permute-start(bf16[2,64,128]{2,1,0:T(8,128)(2,1)S(1)} %maximum_select_fusion.6), channel_id=1, source_target_pairs={{0,32},{16,48},{32,0},{48,16},{1,33},{17,49},{33,1},{49,17},{2,34}... | collective-permute-start | bytes 98312 | tf_op jit(solution)/shard_map/ppermute | solution.py:148
  29.6 5.3 %collective-permute-start.2 = (bf16[2,2,64,128]{3,2,1,0:T(8,128)(2,1)S(1)}, bf16[2,2,64,128]{3,2,1,0:T(8,128)(2,1)S(1)}, u32[]{:S(2)}, u32[]{:S(2)}) collective-permute-start(bf16[2,2,64,128]{3,2,1,0:T(8,128)(2,1)S(1)} %maximum_select_fusion.4), channel_id=1, source_target_pairs={{0,16},{16,0},{32,48},{48,32},{1,17},{17,1},{33,49},{49,33},{2,18}... | collective-permute-start | bytes 196616 | tf_op jit(solution)/shard_map/ppermute | solution.py:148
  34.9 5.7 %collective-permute-start.3 = (bf16[2,2,2,64,128]{4,3,2,1,0:T(8,128)(2,1)S(1)}, bf16[2,2,2,64,128]{4,3,2,1,0:T(8,128)(2,1)S(1)}, u32[]{:S(2)}, u32[]{:S(2)}) collective-permute-start(bf16[2,2,2,64,128]{4,3,2,1,0:T(8,128)(2,1)S(1)} %maximum_select_fusion.2), channel_id=1, source_target_pairs={{0,64},{64,0},{1,65},{65,1},{2,66},{66,2},{3,67},{67,3},{4,68},{68... | collective-permute-start | bytes 393224 | tf_op jit(solution)/shard_map/ppermute | solution.py:148
  41.1 14.0 %copy-start.4 = (bf16[6,128]{1,0:T(8,128)(2,1)S(1)}, bf16[6,128]{1,0:T(8,128)(2,1)}, u32[]{:S(2)}) copy-start(bf16[6,128]{1,0:T(8,128)(2,1)} %param.19) | copy-start | bytes 4612
  41.9 13.2 %all-to-all-start.1 = ((bf16[8,64,128]{2,1,0:T(8,128)(2,1)}), bf16[8,64,128]{2,1,0:T(8,128)(2,1)S(1)}, u32[]{:S(2)}, u32[]{:S(2)}) async-start(bf16[8,64,128]{2,1,0:T(8,128)(2,1)} %bitcast.16), calls=%async_computation.1 | async-start | bytes 262144 | tf_op jit(solution)/shard_map/all_to_all | solution.py:31
  49.9 5.5 %copy-start.2 = (bf16[16,2,8,128]{3,2,1,0:T(8,128)(2,1)S(1)}, bf16[16,2,8,128]{3,2,1,0:T(8,128)(2,1)}, u32[]{:S(2)}) copy-start(bf16[16,2,8,128]{3,2,1,0:T(8,128)(2,1)} %shard_map.132) | copy-start | bytes 196612
  82.2 16.1 %all-to-all-start.5 = ((bf16[8,120,128]{2,1,0:T(8,128)(2,1)}), bf16[8,120,128]{2,1,0:T(8,128)(2,1)S(1)}, u32[]{:S(2)}, u32[]{:S(2)}) async-start(bf16[8,120,128]{2,1,0:T(8,128)(2,1)} %broadcast_in_dim.21), calls=%async_computation.5 | async-start | bytes 491520 | tf_op jit(solution)/shard_map/all_to_all | solution.py:31
  98.2 0.7 copy-start
  101.6 8.4 %collective-permute-start.4 = (bf16[128,128]{1,0:T(8,128)(2,1)S(1)}, bf16[128,128]{1,0:T(8,128)(2,1)S(1)}, u32[]{:S(2)}, u32[]{:S(2)}) collective-permute-start(bf16[128,128]{1,0:T(8,128)(2,1)S(1)} %get-tuple-element.14), channel_id=1, source_target_pairs={{0,8},{8,0},{1,9},{9,1},{2,10},{10,2},{3,11},{11,3},{4,12},{12,4},... | collective-permute-start | bytes 98312 | tf_op jit(solution)/shard_map/ppermute | solution.py:136
  110.7 10.5 %all-to-all-start.6 = ((bf16[8,128,128]{2,1,0:T(8,128)(2,1)}), bf16[8,128,128]{2,1,0:T(8,128)(2,1)S(1)}, u32[]{:S(2)}, u32[]{:S(2)}) async-start(bf16[8,128,128]{2,1,0:T(8,128)(2,1)} %broadcast_in_dim.22), calls=%async_computation.6 | async-start | bytes 524288 | tf_op jit(solution)/shard_map/all_to_all | solution.py:31
  121.3 43.4 %copy-start.9 = (f32[1,32]{1,0:T(1,128)S(1)}, f32[1,32]{1,0:T(1,128)}, u32[]{:S(2)}) copy-start(f32[1,32]{1,0:T(1,128)} %param.17) | copy-start | bytes 388
  121.3 43.4 %copy-start.10 = (s32[1,32]{1,0:T(1,128)S(1)}, s32[1,32]{1,0:T(1,128)}, u32[]{:S(2)}) copy-start(s32[1,32]{1,0:T(1,128)} %param.18) | copy-start | bytes 388
  157.8 8.3 %collective-permute-start.5 = (bf16[32,48,128]{2,1,0:T(8,128)(2,1)S(1)}, bf16[32,48,128]{2,1,0:T(8,128)(2,1)S(1)}, u32[]{:S(2)}, u32[]{:S(2)}) collective-permute-start(bf16[32,48,128]{2,1,0:T(8,128)(2,1)S(1)} %all_to_all.65), channel_id=1, source_target_pairs={{0,8},{8,0},{1,9},{9,1},{2,10},{10,2},{3,11},{11,3},{4,12},{12,4},... | collective-permute-start | bytes 1179656 | tf_op jit(solution)/shard_map/ppermute | solution.py:136
  166.4 0.8 copy-start.5
  176.5 13.7 %all-to-all-start.11 = ((bf16[16,64,128]{2,1,0:T(8,128)(2,1)}), bf16[16,64,128]{2,1,0:T(8,128)(2,1)S(1)}, u32[]{:S(2)}, u32[]{:S(2)}) async-start(bf16[16,64,128]{2,1,0:T(8,128)(2,1)} %bitcast.55), calls=%async_computation.11 | async-start | bytes 524288 | tf_op jit(solution)/shard_map/all_to_all | solution.py:31

commit v6 on v5

--- a/solution.py
+++ b/solution.py
@@ -40,6 +40,10 @@
 
 def summed(blocks):
     return jnp.sum(blocks.astype(F32), axis=0)
+
+
+SCALARS = pl.BlockSpec(memory_space=pltpu.SMEM)
+VECTORS = pl.BlockSpec(memory_space=pltpu.VMEM)
 
 
 def split_columns_kernel(source_ref, out_ref):
@@ -66,38 +70,49 @@
     )(factor_rows)
 
 
-def combine_kernel(tiles_ref, terms_ref, out_ref, total_ref):
+def combine_kernel(tiles_ref, terms_ref, block_ref, wide_ref, narrow_ref, total_ref):
     for y in range(8):
         for j in range(3):
             total_ref[3 * y + j] = -terms_ref[15 * y + 12 + j].astype(F32)
+        total_ref[ROOT_TILES + y] = jnp.zeros((8, RHS), F32)
     for p in range(LEAVES):
         for k in range(LEAF_TILES):
             tile = tiles_ref[p, k]
             term = terms_ref[30 * p + k].astype(F32) + terms_ref[30 * p + 15 + k].astype(F32)
             total_ref[tile] = total_ref[tile] + term
-    out_ref[...] = (-total_ref[...]).astype(BF16)
-
-
-def combine(root_tiles, terms):
+    reduced = (-total_ref[...]).reshape(256, RHS).astype(BF16)
+    product = jnp.dot(block_ref[...], reduced, preferred_element_type=F32)
+    wide_ref[...] = product
+    narrow_ref[...] = product.astype(BF16)
+
+
+def combine(root_tiles, terms, block):
     return pl.pallas_call(
         combine_kernel,
-        out_shape=jax.ShapeDtypeStruct((ROOT_TILES, 8, RHS), BF16),
-        in_specs=[
-            pl.BlockSpec(memory_space=pltpu.SMEM),
-            pl.BlockSpec(memory_space=pltpu.VMEM),
-        ],
-        out_specs=pl.BlockSpec(memory_space=pltpu.VMEM),
-        scratch_shapes=[pltpu.VMEM((ROOT_TILES, 8, RHS), F32)],
-    )(root_tiles, terms)
-
-
-def granule_columns_kernel(source_ref, pivots_ref, out_ref):
+        out_shape=(
+            jax.ShapeDtypeStruct((TILE, RHS), F32),
+            jax.ShapeDtypeStruct((TILE, RHS), BF16),
+        ),
+        in_specs=[SCALARS, VECTORS, VECTORS],
+        out_specs=(VECTORS, VECTORS),
+        scratch_shapes=[pltpu.VMEM((ROOT_TILES + 8, 8, RHS), F32)],
+    )(root_tiles, terms, block)
+
+
+def granule_columns_kernel(dinv_ref, doff_ref, pairs_ref, source_ref, out_ref):
     lane = lax.broadcasted_iota(jnp.int32, (6, TILE), 1)
     slot = lane // 8
     tiles = [source_ref[:, t * TILE : (t + 1) * TILE].astype(F32) for t in range(ROOT_TILES)]
+    row = lax.broadcasted_iota(jnp.int32, (6, TILE), 0)
+    diagonal = jnp.zeros((6, TILE), F32)
+    joined = jnp.zeros((6, TILE), F32)
+    for i in range(6):
+        diagonal = jnp.where(row == i, dinv_ref[i], diagonal)
+        both = doff_ref[i // 2] * pairs_ref[i // 2].astype(F32)
+        joined = jnp.where(row == i, both, joined)
     spare = jnp.zeros((6, TILE), F32)
-    for j in range(6):
-        spare = jnp.where(lane == 64 + j, pivots_ref[:, j : j + 1], spare)
+    for j, part in enumerate(parts_of(diagonal) + parts_of(joined)):
+        spare = jnp.where(lane == 64 + j, part, spare)
     out_ref[...] = jnp.zeros_like(out_ref)
     for a in range(16):
         first = spare
@@ -110,18 +125,20 @@
         out_ref[a, 1, :6] = second.astype(BF16)
 
 
-def granule_columns(rows, pivots):
+def granule_columns(dinv, doff, pairs, rows):
     return pl.pallas_call(
         granule_columns_kernel,
         out_shape=jax.ShapeDtypeStruct((16, 2, 8, TILE), BF16),
-    )(rows, pivots)
+        in_specs=[SCALARS, SCALARS, SCALARS, VECTORS],
+        out_specs=VECTORS,
+    )(dinv, doff, pairs, rows)
 
 
 def parts_of(value):
-    high = lax.reduce_precision(value, 8, 7)
+    high = value.astype(BF16).astype(F32)
     rest = value - high
-    middle = lax.reduce_precision(rest, 8, 7)
-    low = lax.reduce_precision(rest - middle, 8, 7)
+    middle = rest.astype(BF16).astype(F32)
+    low = (rest - middle).astype(BF16).astype(F32)
     return [high, middle, low]
 
 
@@ -179,16 +196,15 @@
     blocks = exchange(split_columns(leaf_inverse[0]), CX).reshape(512, 1024)
     rhs_part = gather_leaf_rhs(leaf_rhs[0])
     partial = jnp.dot(blocks, rhs_part, preferred_element_type=F32).astype(BF16)
+    update = leaf_update[0]
+    at = jnp.arange(16 * 24, dtype=jnp.int32)
+    partial, late_update, at = lax.optimization_barrier((partial, update, at))
     partial = exchange(partial.reshape(8, 64, RHS), CX)
     leaf_forward = summed(partial).astype(BF16)
 
-    joined = jnp.repeat(root_doff * root_pairs.astype(F32), 2)
-    pivots = jnp.stack(parts_of(root_dinv) + parts_of(joined), axis=1)
-    root_block = granule_columns(root_inverse, pivots)
-
-    update = leaf_update[0]
-    ordered = update.reshape(12, 16, 8, 64).transpose(1, 0, 2, 3).reshape(16, 96, 64)
-    at = jnp.arange(16 * 24, dtype=jnp.int32)
+    root_block = granule_columns(root_dinv, root_doff, root_pairs, root_inverse)
+
+    ordered = late_update.reshape(12, 16, 8, 64).transpose(1, 0, 2, 3).reshape(16, 96, 64)
     row = TILE * (3 * lax.axis_index(YALL) + at // 8 % 3) + 8 * (at // 24) + at % 8
     row = row - 6 * lax.axis_index(AXES)
     select = (row[:, None] == jnp.arange(8, dtype=jnp.int32)[None, :]) & (row < 6)[:, None]
@@ -207,16 +223,15 @@
     pivots = root_block[:, 192:198].astype(F32)
     dinv_rows = pivots[:, 0:1] + pivots[:, 1:2] + pivots[:, 2:3]
     joined_rows = pivots[:, 3:4] + pivots[:, 4:5] + pivots[:, 5:6]
-    root_block = root_block[:, :192]
     term = summed(term[:, :120]).astype(BF16)
     term = summed(gather(term, ("x",))).astype(BF16)
-    reduced = combine(root_tiles, gather(term, YALL).reshape(120, 8, RHS)).reshape(192, RHS)
-
-    forward = jnp.dot(root_block, reduced, preferred_element_type=F32)
-    forward = forward + other_core(forward.astype(BF16)).astype(F32)
+    term = gather(term, YALL).reshape(120, 8, RHS)
+
+    wide, narrow = combine(root_tiles, term, root_block)
+    forward = wide + other_core(narrow).astype(F32)
     forward = summed(gather(forward.astype(BF16), Z))
     root_scaled = pivot_solve(forward, dinv_rows, joined_rows).astype(BF16)
-    back = transposed_product(root_block, root_scaled).astype(BF16)
+    back = transposed_product(root_block[:, :192], root_scaled).astype(BF16)
     back = summed(exchange(back.reshape(4, 48, RHS), ("x",))).astype(BF16)
     root_part = summed(gather(back, YALL)).astype(BF16)
     root_full = both_cores(gather(root_part, ZX)).reshape(16, ROOT_TILES, 8, RHS)

time: 192 us -> 191 us (level)
  no operation moved by 1% of the time
where the time goes in v6:
time: 191 us; the launch traced here: 190 us
  blocking collectives  69.7 us (36%)
  starting transfers between devices  63.4 us (33%)
  waiting for transfers between devices  37.9 us (20%)
  local copies, waits for them, and re-layouts  6.95 us (4%)
  Pallas kernels  6.25 us (3%)
  other arithmetic  2.78 us (1%)
  matrix products  2.19 us (1%)
    all_to_all x7, blocking collectives, exchange(): return lax.all_to_all(blocks, axes, 0, 0)  69.7 us
    all_to_all x5, waiting for transfers between devices, exchange(): return lax.all_to_all(blocks, axes, 0, 0)  30.1 us
    all_to_all x5, starting transfers between devices, exchange(): return lax.all_to_all(blocks, axes, 0, 0)  27.2 us
    ppermute x4, starting transfers between devices, doubled(): other = lax.ppermute(held, axis, pairs)  21.8 us
    ppermute x2, starting transfers between devices, other_core(): return lax.ppermute(value, 'c', [(0, 1), (1, 0)])  14.4 us
    ppermute x4, waiting for transfers between devices, doubled(): other = lax.ppermute(held, axis, pairs)  6.41 us
  transfers between devices with their start and end apart: 11, of which 9 were waited for; matrix products, arithmetic and copies ran while one was open for 2% of the time, Pallas kernels for 2%

profile of v6, /device:TPU:1, one launch (start us, length us, event | category | flops | bytes accessed | tf_op | source)
XLA Modules:
  0.0 190.1 jit_solution(1948754508497442024)
XLA Ops:
  0.6 11.5 %collective-permute-start = (bf16[64,128]{1,0:T(8,128)(2,1)}, bf16[64,128]{1,0:T(8,128)(2,1)S(1)}, u32[]{:S(2)}, u32[]{:S(2)}) collective-permute-start(bf16[64,128]{1,0:T(8,128)(2,1)} %bitcast.119), channel_id=1, source_target_pairs={{0,4},{4,0},{1,5},{5,1},{2,6},{6,2},{3,7},{7,3},{8,12},{12,8},{9,1... | collective-permute-start | bytes 49160 | tf_op jit(solution)/shard_map/ppermute | solution.py:165
  12.1 2.7 %shard_map.131 = bf16[8,64,1024]{2,1,0:T(8,128)(2,1)} custom-call(bf16[64,8192]{1,0:T(8,128)(2,1)} %bitcast.101), custom_call_target="tpu_custom_call" | custom-call | tf_op jit(solution)/shard_map/pallas_call | solution.py:67
  14.8 5.4 %all-to-all-start = ((bf16[8,64,1024]{2,1,0:T(8,128)(2,1)}), bf16[8,64,1024]{2,1,0:T(8,128)(2,1)S(1)}, u32[]{:S(2)}, u32[]{:S(2)}) async-start(bf16[8,64,1024]{2,1,0:T(8,128)(2,1)} %shard_map.131), calls=%async_computation | async-start | bytes 2097152 | tf_op jit(solution)/shard_map/all_to_all | solution.py:31
  20.4 1.7 shard_map.132
  22.1 4.0 %collective-permute-start.1 = (bf16[2,64,128]{2,1,0:T(8,128)(2,1)S(1)}, bf16[2,64,128]{2,1,0:T(8,128)(2,1)S(1)}, u32[]{:S(2)}, u32[]{:S(2)}) collective-permute-start(bf16[2,64,128]{2,1,0:T(8,128)(2,1)S(1)} %maximum_select_fusion.6), channel_id=1, source_target_pairs={{0,32},{16,48},{32,0},{48,16},{1,33},{17,49},{33,1},{49,17},{2,34}... | collective-permute-start | bytes 98312 | tf_op jit(solution)/shard_map/ppermute | solution.py:165
  26.2 1.8 collective-permute-done.1
  28.0 3.1 %collective-permute-start.2 = (bf16[2,2,64,128]{3,2,1,0:T(8,128)(2,1)S(1)}, bf16[2,2,64,128]{3,2,1,0:T(8,128)(2,1)S(1)}, u32[]{:S(2)}, u32[]{:S(2)}) collective-permute-start(bf16[2,2,64,128]{3,2,1,0:T(8,128)(2,1)S(1)} %maximum_select_fusion.4), channel_id=1, source_target_pairs={{0,16},{16,0},{32,48},{48,32},{1,17},{17,1},{33,49},{49,33},{2,18}... | collective-permute-start | bytes 196616 | tf_op jit(solution)/shard_map/ppermute | solution.py:165
  31.1 2.2 %collective-permute-done.2 = bf16[2,2,64,128]{3,2,1,0:T(8,128)(2,1)S(1)} collective-permute-done((bf16[2,2,64,128]{3,2,1,0:T(8,128)(2,1)S(1)}, bf16[2,2,64,128]{3,2,1,0:T(8,128)(2,1)S(1)}, u32[]{:S(2)}, u32[]{:S(2)}) %collective-permute-start.2) | collective-permute-done | bytes 65568 | tf_op jit(solution)/shard_map/ppermute | solution.py:165
  33.3 3.2 %collective-permute-start.3 = (bf16[2,2,2,64,128]{4,3,2,1,0:T(8,128)(2,1)S(1)}, bf16[2,2,2,64,128]{4,3,2,1,0:T(8,128)(2,1)S(1)}, u32[]{:S(2)}, u32[]{:S(2)}) collective-permute-start(bf16[2,2,2,64,128]{4,3,2,1,0:T(8,128)(2,1)S(1)} %maximum_select_fusion.2), channel_id=1, source_target_pairs={{0,64},{64,0},{1,65},{65,1},{2,66},{66,2},{3,67},{67,3},{4,68},{68... | collective-permute-start | bytes 393224 | tf_op jit(solution)/shard_map/ppermute | solution.py:165
  36.6 2.4 %collective-permute-done.3 = bf16[2,2,2,64,128]{4,3,2,1,0:T(8,128)(2,1)S(1)} collective-permute-done((bf16[2,2,2,64,128]{4,3,2,1,0:T(8,128)(2,1)S(1)}, bf16[2,2,2,64,128]{4,3,2,1,0:T(8,128)(2,1)S(1)}, u32[]{:S(2)}, u32[]{:S(2)}) %collective-permute-start.3) | collective-permute-done | bytes 131104 | tf_op jit(solution)/shard_map/ppermute | solution.py:165
  40.2 0.7 copy.38
  40.9 8.0 %all-to-all-start.1 = ((bf16[8,64,128]{2,1,0:T(8,128)(2,1)}), bf16[8,64,128]{2,1,0:T(8,128)(2,1)S(1)}, u32[]{:S(2)}, u32[]{:S(2)}) async-start(bf16[8,64,128]{2,1,0:T(8,128)(2,1)} %bitcast.17), calls=%async_computation.1 | async-start | bytes 262144 | tf_op jit(solution)/shard_map/all_to_all | solution.py:31
  49.0 5.1 %all-to-all-done.1 = bf16[8,64,128]{2,1,0:T(8,128)(2,1)S(1)} async-done(((bf16[8,64,128]{2,1,0:T(8,128)(2,1)}), bf16[8,64,128]{2,1,0:T(8,128)(2,1)S(1)}, u32[]{:S(2)}, u32[]{:S(2)}) %all-to-all-start.1) | async-done | bytes 131104 | tf_op jit(solution)/shard_map/all_to_all | solution.py:31
  54.5 4.2 %all_to_all.60 = bf16[2,1088,128]{2,1,0:T(8,128)(2,1)S(1)} all-to-all(bf16[2,1088,128]{2,1,0:T(8,128)(2,1)S(1)} %bitcast.92), channel_id=1, replica_groups=mesh['p'=4,'yl'=2,'zl'=4,'c'=2,'zh'=2,'x'=4] {'c'}, dimensions={0} | all-to-all | bytes 1114112 | tf_op jit(solution)/shard_map/all_to_all | solution.py:31
  58.8 14.3 %all_to_all.61 = bf16[8,152,128]{2,1,0:T(8,128)(2,1)S(1)} all-to-all(bf16[8,152,128]{2,1,0:T(8,128)(2,1)S(1)} %pad_maximum_fusion.1), channel_id=1, replica_groups=mesh['p'=4,'yl'=2,'zl'=4,'c'=2,'zh'=2,'x'=4] {'zl','zh'}, dimensions={0} | all-to-all | bytes 622592 | tf_op jit(solution)/shard_map/all_to_all | solution.py:31
  73.2 7.3 %all_to_all.62 = bf16[4,120,128]{2,1,0:T(8,128)(2,1)S(1)} all-to-all(bf16[4,120,128]{2,1,0:T(8,128)(2,1)S(1)} %broadcast_in_dim.17), channel_id=1, replica_groups=mesh['p'=4,'yl'=2,'zl'=4,'c'=2,'zh'=2,'x'=4] {'x'}, dimensions={0} | all-to-all | bytes 245760 | tf_op jit(solution)/shard_map/all_to_all | solution.py:31
  81.2 6.8 %all-to-all-start.5 = ((bf16[8,120,128]{2,1,0:T(8,128)(2,1)}), bf16[8,120,128]{2,1,0:T(8,128)(2,1)S(1)}, u32[]{:S(2)}, u32[]{:S(2)}) async-start(bf16[8,120,128]{2,1,0:T(8,128)(2,1)} %broadcast_in_dim.18), calls=%async_computation.5 | async-start | bytes 491520 | tf_op jit(solution)/shard_map/all_to_all | solution.py:31
  88.6 8.6 %all-to-all-done.5 = bf16[8,120,128]{2,1,0:T(8,128)(2,1)S(1)} async-done(((bf16[8,120,128]{2,1,0:T(8,128)(2,1)}), bf16[8,120,128]{2,1,0:T(8,128)(2,1)S(1)}, u32[]{:S(2)}, u32[]{:S(2)}) %all-to-all-start.5) | async-done | bytes 245792 | tf_op jit(solution)/shard_map/all_to_all | solution.py:31
  97.9 1.9 shard_map.133
  99.8 7.5 %collective-permute-start.4 = (bf16[128,128]{1,0:T(8,128)(2,1)}, bf16[128,128]{1,0:T(8,128)(2,1)S(1)}, u32[]{:S(2)}, u32[]{:S(2)}) collective-permute-start(bf16[128,128]{1,0:T(8,128)(2,1)} %get-tuple-element.11), channel_id=1, source_target_pairs={{0,8},{8,0},{1,9},{9,1},{2,10},{10,2},{3,11},{11,3},{4,12},{12,4},... | collective-permute-start | bytes 98312 | tf_op jit(solution)/shard_map/ppermute | solution.py:153
  107.3 1.0 collective-permute-done.4
  108.4 0.8 add_convert_fusion.1
  110.0 3.4 %all-to-all-start.6 = ((bf16[8,128,128]{2,1,0:T(8,128)(2,1)}), bf16[8,128,128]{2,1,0:T(8,128)(2,1)S(1)}, u32[]{:S(2)}, u32[]{:S(2)}) async-start(bf16[8,128,128]{2,1,0:T(8,128)(2,1)} %broadcast_in_dim.19), calls=%async_computation.6 | async-start | bytes 524288 | tf_op jit(solution)/shard_map/all_to_all | solution.py:31
  113.7 6.8 %all-to-all-done.6 = bf16[8,128,128]{2,1,0:T(8,128)(2,1)S(1)} async-done(((bf16[8,128,128]{2,1,0:T(8,128)(2,1)}), bf16[8,128,128]{2,1,0:T(8,128)(2,1)S(1)}, u32[]{:S(2)}, u32[]{:S(2)}) %all-to-all-start.6) | async-done | bytes 262176 | tf_op jit(solution)/shard_map/all_to_all | solution.py:31
  121.0 6.7 %all_to_all.63 = bf16[4,48,128]{2,1,0:T(8,128)(2,1)S(1)} all-to-all(bf16[4,48,128]{2,1,0:T(8,128)(2,1)S(1)} %bitcast.118), channel_id=1, replica_groups=mesh['p'=4,'yl'=2,'zl'=4,'c'=2,'zh'=2,'x'=4] {'x'}, dimensions={0} | all-to-all | bytes 98304 | tf_op jit(solution)/shard_map/all_to_all | solution.py:31
  127.7 10.0 %all_to_all.64 = bf16[8,48,128]{2,1,0:T(8,128)(2,1)S(1)} all-to-all(bf16[8,48,128]{2,1,0:T(8,128)(2,1)S(1)} %broadcast_in_dim.20), channel_id=1, replica_groups=mesh['p'=4,'yl'=2,'zl'=4,'c'=2,'zh'=2,'x'=4] {'p','yl'}, dimensions={0} | all-to-all | bytes 196608 | tf_op jit(solution)/shard_map/all_to_all | solution.py:31
  137.8 19.2 %all_to_all.65 = bf16[32,48,128]{2,1,0:T(8,128)(2,1)S(1)} all-to-all(bf16[32,48,128]{2,1,0:T(8,128)(2,1)S(1)} %broadcast_in_dim.21), channel_id=1, replica_groups=mesh['p'=4,'yl'=2,'zl'=4,'c'=2,'zh'=2,'x'=4] {'zl','zh','x'}, dimensions={0} | all-to-all | bytes 786432 | tf_op jit(solution)/shard_map/all_to_all | solution.py:31
  157.0 6.9 %collective-permute-start.5 = (bf16[32,48,128]{2,1,0:T(8,128)(2,1)S(1)}, bf16[32,48,128]{2,1,0:T(8,128)(2,1)S(1)}, u32[]{:S(2)}, u32[]{:S(2)}) collective-permute-start(bf16[32,48,128]{2,1,0:T(8,128)(2,1)S(1)} %all_to_all.65), channel_id=1, source_target_pairs={{0,8},{8,0},{1,9},{9,1},{2,10},{10,2},{3,11},{11,3},{4,12},{12,4},... | collective-permute-start | bytes 1179656 | tf_op jit(solution)/shard_map/ppermute | solution.py:153
  166.7 7.9 %all_to_all.66 = bf16[8,64,128]{2,1,0:T(8,128)(2,1)S(1)} all-to-all(bf16[8,64,128]{2,1,0:T(8,128)(2,1)S(1)} %broadcast_in_dim.22), channel_id=1, replica_groups=mesh['p'=4,'yl'=2,'zl'=4,'c'=2,'zh'=2,'x'=4] {'c','x'}, dimensions={0} | all-to-all | bytes 262144 | tf_op jit(solution)/shard_map/all_to_all | solution.py:31
  175.0 0.8 copy.44
  175.8 3.5 %all-to-all-start.11 = ((bf16[16,64,128]{2,1,0:T(8,128)(2,1)}), bf16[16,64,128]{2,1,0:T(8,128)(2,1)S(1)}, u32[]{:S(2)}, u32[]{:S(2)}) async-start(bf16[16,64,128]{2,1,0:T(8,128)(2,1)} %bitcast.51), calls=%async_computation.11 | async-start | bytes 524288 | tf_op jit(solution)/shard_map/all_to_all | solution.py:31
  179.9 9.6 %all-to-all-done.11 = bf16[16,64,128]{2,1,0:T(8,128)(2,1)S(1)} async-done(((bf16[16,64,128]{2,1,0:T(8,128)(2,1)}), bf16[16,64,128]{2,1,0:T(8,128)(2,1)S(1)}, u32[]{:S(2)}, u32[]{:S(2)}) %all-to-all-start.11) | async-done | bytes 262176 | tf_op jit(solution)/shard_map/all_to_all | solution.py:31
  (77 shorter events, 9.8 us)
Async XLA Ops:
  0.6 21.5 %collective-permute-start = (bf16[64,128]{1,0:T(8,128)(2,1)}, bf16[64,128]{1,0:T(8,128)(2,1)S(1)}, u32[]{:S(2)}, u32[]{:S(2)}) collective-permute-start(bf16[64,128]{1,0:T(8,128)(2,1)} %bitcast.119), channel_id=1, source_target_pairs={{0,4},{4,0},{1,5},{5,1},{2,6},{6,2},{3,7},{7,3},{8,12},{12,8},{9,1... | collective-permute-start | bytes 49160 | tf_op jit(solution)/shard_map/ppermute | solution.py:165
  14.8 5.4 %copy-start.2 = (bf16[1,1536,64]{1,2,0:T(8,128)(2,1)S(1)}, bf16[1,1536,64]{1,2,0:T(8,128)(2,1)}, u32[]{:S(2)}) copy-start(bf16[1,1536,64]{1,2,0:T(8,128)(2,1)} %param.14) | copy-start | bytes 589828
  14.8 7.3 %copy-start.4 = (bf16[1,64,128]{2,1,0:T(8,128)(2,1)S(1)}, bf16[1,64,128]{2,1,0:T(8,128)(2,1)}, u32[]{:S(2)}) copy-start(bf16[1,64,128]{2,1,0:T(8,128)(2,1)} %param.12) | copy-start | bytes 49156
  14.8 24.3 %all-to-all-start = ((bf16[8,64,1024]{2,1,0:T(8,128)(2,1)}), bf16[8,64,1024]{2,1,0:T(8,128)(2,1)S(1)}, u32[]{:S(2)}, u32[]{:S(2)}) async-start(bf16[8,64,1024]{2,1,0:T(8,128)(2,1)} %shard_map.131), calls=%async_computation | async-start | bytes 2097152 | tf_op jit(solution)/shard_map/all_to_all | solution.py:31
  22.1 5.9 %collective-permute-start.1 = (bf16[2,64,128]{2,1,0:T(8,128)(2,1)S(1)}, bf16[2,64,128]{2,1,0:T(8,128)(2,1)S(1)}, u32[]{:S(2)}, u32[]{:S(2)}) collective-permute-start(bf16[2,64,128]{2,1,0:T(8,128)(2,1)S(1)} %maximum_select_fusion.6), channel_id=1, source_target_pairs={{0,32},{16,48},{32,0},{48,16},{1,33},{17,49},{33,1},{49,17},{2,34}... | collective-permute-start | bytes 98312 | tf_op jit(solution)/shard_map/ppermute | solution.py:165
  28.0 5.3 %collective-permute-start.2 = (bf16[2,2,64,128]{3,2,1,0:T(8,128)(2,1)S(1)}, bf16[2,2,64,128]{3,2,1,0:T(8,128)(2,1)S(1)}, u32[]{:S(2)}, u32[]{:S(2)}) collective-permute-start(bf16[2,2,64,128]{3,2,1,0:T(8,128)(2,1)S(1)} %maximum_select_fusion.4), channel_id=1, source_target_pairs={{0,16},{16,0},{32,48},{48,32},{1,17},{17,1},{33,49},{49,33},{2,18}... | collective-permute-start | bytes 196616 | tf_op jit(solution)/shard_map/ppermute | solution.py:165
  33.3 5.7 %collective-permute-start.3 = (bf16[2,2,2,64,128]{4,3,2,1,0:T(8,128)(2,1)S(1)}, bf16[2,2,2,64,128]{4,3,2,1,0:T(8,128)(2,1)S(1)}, u32[]{:S(2)}, u32[]{:S(2)}) collective-permute-start(bf16[2,2,2,64,128]{4,3,2,1,0:T(8,128)(2,1)S(1)} %maximum_select_fusion.2), channel_id=1, source_target_pairs={{0,64},{64,0},{1,65},{65,1},{2,66},{66,2},{3,67},{67,3},{4,68},{68... | collective-permute-start | bytes 393224 | tf_op jit(solution)/shard_map/ppermute | solution.py:165
  40.1 14.1 %copy-start.5 = (bf16[6,128]{1,0:T(8,128)(2,1)S(1)}, bf16[6,128]{1,0:T(8,128)(2,1)}, u32[]{:S(2)}) copy-start(bf16[6,128]{1,0:T(8,128)(2,1)} %param.19) | copy-start | bytes 4612
  40.9 13.2 %all-to-all-start.1 = ((bf16[8,64,128]{2,1,0:T(8,128)(2,1)}), bf16[8,64,128]{2,1,0:T(8,128)(2,1)S(1)}, u32[]{:S(2)}, u32[]{:S(2)}) async-start(bf16[8,64,128]{2,1,0:T(8,128)(2,1)} %bitcast.17), calls=%async_computation.1 | async-start | bytes 262144 | tf_op jit(solution)/shard_map/all_to_all | solution.py:31
  48.9 5.5 %copy-start.3 = (bf16[16,2,8,128]{3,2,1,0:T(8,128)(2,1)S(1)}, bf16[16,2,8,128]{3,2,1,0:T(8,128)(2,1)}, u32[]{:S(2)}) copy-start(bf16[16,2,8,128]{3,2,1,0:T(8,128)(2,1)} %shard_map.132) | copy-start | bytes 196612
  81.2 16.1 %all-to-all-start.5 = ((bf16[8,120,128]{2,1,0:T(8,128)(2,1)}), bf16[8,120,128]{2,1,0:T(8,128)(2,1)S(1)}, u32[]{:S(2)}, u32[]{:S(2)}) async-start(bf16[8,120,128]{2,1,0:T(8,128)(2,1)} %broadcast_in_dim.18), calls=%async_computation.5 | async-start | bytes 491520 | tf_op jit(solution)/shard_map/all_to_all | solution.py:31
  88.6 24.8 %copy-start.1 = (bf16[8,32,128]{2,1,0:T(8,128)(2,1)S(1)}, bf16[8,32,128]{2,1,0:T(8,128)(2,1)}, u32[]{:S(2)}) copy-start(bf16[8,32,128]{2,1,0:T(8,128)(2,1)} %slice.50) | copy-start | bytes 196612
  97.3 0.7 copy-start
  99.8 8.6 %collective-permute-start.4 = (bf16[128,128]{1,0:T(8,128)(2,1)}, bf16[128,128]{1,0:T(8,128)(2,1)S(1)}, u32[]{:S(2)}, u32[]{:S(2)}) collective-permute-start(bf16[128,128]{1,0:T(8,128)(2,1)} %get-tuple-element.11), channel_id=1, source_target_pairs={{0,8},{8,0},{1,9},{9,1},{2,10},{10,2},{3,11},{11,3},{4,12},{12,4},... | collective-permute-start | bytes 98312 | tf_op jit(solution)/shard_map/ppermute | solution.py:153
  110.0 10.5 %all-to-all-start.6 = ((bf16[8,128,128]{2,1,0:T(8,128)(2,1)}), bf16[8,128,128]{2,1,0:T(8,128)(2,1)S(1)}, u32[]{:S(2)}, u32[]{:S(2)}) async-start(bf16[8,128,128]{2,1,0:T(8,128)(2,1)} %broadcast_in_dim.19), calls=%async_computation.6 | async-start | bytes 524288 | tf_op jit(solution)/shard_map/all_to_all | solution.py:31
  120.5 43.4 %copy-start.7 = (f32[1,32]{1,0:T(1,128)S(1)}, f32[1,32]{1,0:T(1,128)}, u32[]{:S(2)}) copy-start(f32[1,32]{1,0:T(1,128)} %param.17) | copy-start | bytes 388
  120.6 43.4 %copy-start.8 = (s32[1,32]{1,0:T(1,128)S(1)}, s32[1,32]{1,0:T(1,128)}, u32[]{:S(2)}) copy-start(s32[1,32]{1,0:T(1,128)} %param.18) | copy-start | bytes 388
  157.0 8.3 %collective-permute-start.5 = (bf16[32,48,128]{2,1,0:T(8,128)(2,1)S(1)}, bf16[32,48,128]{2,1,0:T(8,128)(2,1)S(1)}, u32[]{:S(2)}, u32[]{:S(2)}) collective-permute-start(bf16[32,48,128]{2,1,0:T(8,128)(2,1)S(1)} %all_to_all.65), channel_id=1, source_target_pairs={{0,8},{8,0},{1,9},{9,1},{2,10},{10,2},{3,11},{11,3},{4,12},{12,4},... | collective-permute-start | bytes 1179656 | tf_op jit(solution)/shard_map/ppermute | solution.py:153
  165.6 0.8 copy-start.6
  175.8 13.7 %all-to-all-start.11 = ((bf16[16,64,128]{2,1,0:T(8,128)(2,1)}), bf16[16,64,128]{2,1,0:T(8,128)(2,1)S(1)}, u32[]{:S(2)}, u32[]{:S(2)}) async-start(bf16[16,64,128]{2,1,0:T(8,128)(2,1)} %bitcast.51), calls=%async_computation.11 | async-start | bytes 524288 | tf_op jit(solution)/shard_map/all_to_all | solution.py:31

commit v7 on v6

--- a/solution.py
+++ b/solution.py
@@ -3,6 +3,7 @@
 from jax import lax
 from jax.experimental import pallas as pl
 from jax.experimental.pallas import tpu as pltpu
+from jax.experimental.layout import Layout, with_layout_constraint
 from jax.sharding import Mesh
 from jax.sharding import PartitionSpec as P
 
@@ -70,31 +71,29 @@
     )(factor_rows)
 
 
-def combine_kernel(tiles_ref, terms_ref, block_ref, wide_ref, narrow_ref, total_ref):
+def combine_kernel(tiles_ref, terms_ref, block_ref, out_ref, total_ref):
     for y in range(8):
-        for j in range(3):
-            total_ref[3 * y + j] = -terms_ref[15 * y + 12 + j].astype(F32)
+        for x in range(3):
+            total_ref[3 * y + x] = -terms_ref[(x * 8 + y) * 4 + 3].astype(F32)
         total_ref[ROOT_TILES + y] = jnp.zeros((8, RHS), F32)
     for p in range(LEAVES):
-        for k in range(LEAF_TILES):
-            tile = tiles_ref[p, k]
-            term = terms_ref[30 * p + k].astype(F32) + terms_ref[30 * p + 15 + k].astype(F32)
-            total_ref[tile] = total_ref[tile] + term
+        for x in range(4):
+            for k in range(3):
+                tile = tiles_ref[p, 3 * x + k]
+                first = (x * 8 + 2 * p) * 4 + k
+                term = terms_ref[first].astype(F32) + terms_ref[first + 4].astype(F32)
+                total_ref[tile] = total_ref[tile] + term
     reduced = (-total_ref[...]).reshape(256, RHS).astype(BF16)
     product = jnp.dot(block_ref[...], reduced, preferred_element_type=F32)
-    wide_ref[...] = product
-    narrow_ref[...] = product.astype(BF16)
+    out_ref[...] = product.astype(BF16)
 
 
 def combine(root_tiles, terms, block):
     return pl.pallas_call(
         combine_kernel,
-        out_shape=(
-            jax.ShapeDtypeStruct((TILE, RHS), F32),
-            jax.ShapeDtypeStruct((TILE, RHS), BF16),
-        ),
+        out_shape=jax.ShapeDtypeStruct((TILE, RHS), BF16),
         in_specs=[SCALARS, VECTORS, VECTORS],
-        out_specs=(VECTORS, VECTORS),
+        out_specs=VECTORS,
         scratch_shapes=[pltpu.VMEM((ROOT_TILES + 8, 8, RHS), F32)],
     )(root_tiles, terms, block)
 
@@ -195,40 +194,43 @@
 ):
     blocks = exchange(split_columns(leaf_inverse[0]), CX).reshape(512, 1024)
     rhs_part = gather_leaf_rhs(leaf_rhs[0])
-    partial = jnp.dot(blocks, rhs_part, preferred_element_type=F32).astype(BF16)
+    partial = jnp.dot(blocks, rhs_part, preferred_element_type=F32)
+    partial = with_layout_constraint(partial, Layout(major_to_minor=(0, 1))).astype(BF16)
     update = leaf_update[0]
-    at = jnp.arange(16 * 24, dtype=jnp.int32)
+    at = jnp.arange(512, dtype=jnp.int32)
     partial, late_update, at = lax.optimization_barrier((partial, update, at))
     partial = exchange(partial.reshape(8, 64, RHS), CX)
     leaf_forward = summed(partial).astype(BF16)
 
     root_block = granule_columns(root_dinv, root_doff, root_pairs, root_inverse)
 
-    ordered = late_update.reshape(12, 16, 8, 64).transpose(1, 0, 2, 3).reshape(16, 96, 64)
-    row = TILE * (3 * lax.axis_index(YALL) + at // 8 % 3) + 8 * (at // 24) + at % 8
-    row = row - 6 * lax.axis_index(AXES)
+    ordered = late_update.reshape(4, 3, 2, 8, 8, 64).transpose(2, 0, 3, 1, 4, 5)
+    ordered = ordered.reshape(64, 24, 64)
+    x_of = at // 64 % 4
+    row = TILE * (3 * lax.axis_index(YALL) + x_of) + 8 * (at // 256 * 8 + at // 8 % 8) + at % 8
+    row = jnp.where(x_of < 3, row, -1) - 6 * lax.axis_index(AXES)
     select = (row[:, None] == jnp.arange(8, dtype=jnp.int32)[None, :]) & (row < 6)[:, None]
-    select = select.astype(BF16).reshape(16, 24, 8)
+    select = select.astype(BF16).reshape(64, 8, 8)
     left = jnp.concatenate(
         [jnp.pad(ordered, ((0, 0), (0, 0), (0, 8))), jnp.pad(select, ((0, 0), (0, 0), (64, 0)))], 1
-    ).reshape(1920, 72)
+    ).reshape(2048, 72)
     right = jnp.concatenate([leaf_forward, jnp.pad(root_rhs, ((0, 2), (0, 0)))], 0)
     term = jnp.dot(left, right, preferred_element_type=F32).astype(BF16)
-    term = jnp.concatenate([term.reshape(2, 8, 120, RHS), root_block.reshape(2, 8, 16, RHS)], 2)
-    term = exchange(term.reshape(2, 1088, RHS), ("c",)).reshape(2, 8, 136, RHS)
-    root_block = term[:, :, 120:].transpose(1, 0, 2, 3).reshape(8, 32, RHS)
-    term = summed(term[:, :, :120]).astype(BF16)
-    term = exchange(jnp.concatenate([term, root_block], 1), Z)
-    root_block = term[:, 120:].reshape(8, 2, 2, 8, RHS).transpose(0, 1, 3, 2, 4).reshape(128, 2 * TILE)
+    term = jnp.concatenate([term.reshape(2, 1024, RHS), root_block.reshape(2, 128, RHS)], 1)
+    term = exchange(term, ("c",))
+    root_block = term[:, 1024:].reshape(2, 8, 16, RHS).transpose(1, 0, 2, 3).reshape(8, 32, RHS)
+    term = summed(term[:, :1024]).astype(BF16)
+    term = summed(exchange(term.reshape(4, 256, RHS), ("x",))).astype(BF16)
+    term = exchange(jnp.concatenate([term.reshape(8, 32, RHS), root_block], 1), Z)
+    root_block = term[:, 32:].reshape(8, 2, 2, 8, RHS).transpose(0, 1, 3, 2, 4).reshape(128, 2 * TILE)
     pivots = root_block[:, 192:198].astype(F32)
     dinv_rows = pivots[:, 0:1] + pivots[:, 1:2] + pivots[:, 2:3]
     joined_rows = pivots[:, 3:4] + pivots[:, 4:5] + pivots[:, 5:6]
-    term = summed(term[:, :120]).astype(BF16)
-    term = summed(gather(term, ("x",))).astype(BF16)
-    term = gather(term, YALL).reshape(120, 8, RHS)
-
-    wide, narrow = combine(root_tiles, term, root_block)
-    forward = wide + other_core(narrow).astype(F32)
+    term = summed(term[:, :32]).astype(BF16)
+    term = gather(gather(term, YALL).reshape(256, RHS), ("x",)).reshape(128, 8, RHS)
+
+    narrow = combine(root_tiles, term, root_block)
+    forward = narrow.astype(F32) + other_core(narrow).astype(F32)
     forward = summed(gather(forward.astype(BF16), Z))
     root_scaled = pivot_solve(forward, dinv_rows, joined_rows).astype(BF16)
     back = transposed_product(root_block[:, :192], root_scaled).astype(BF16)
@@ -249,7 +251,8 @@
     scaled = pivot_solve(leaf_forward.astype(F32), leaf_dinv[0][:, None], leaf_joined)
     leaf_vector = (scaled - coupling).astype(BF16)
     vector = gather(leaf_vector, CX).reshape(512, RHS)
-    back_leaf = transposed_product(blocks, vector).astype(BF16)
+    back_leaf = transposed_product(blocks, vector)
+    back_leaf = with_layout_constraint(back_leaf, Layout(major_to_minor=(0, 1))).astype(BF16)
     leaf_solution = summed(exchange(back_leaf.reshape(16, 64, RHS), YZ)).astype(BF16)
     return (leaf_solution[None], root_own)
 

time: 191 us -> 196 us (1.026)
  blocking collectives: 69.7 us -> 81.4 us
  starting transfers between devices: 63.4 us -> 59.8 us
  local copies, waits for them, and re-layouts: 6.95 us -> 3.39 us
  waiting for transfers between devices: 37.9 us -> 35.3 us
    all_to_all x7 -> x8, blocking collectives: 69.7 us -> 81.4 us  [exchange(): return lax.all_to_all(blocks, axes, 0, 0)]
    all_to_all x5, starting transfers between devices: 27.2 us -> 23.8 us  [exchange(): return lax.all_to_all(blocks, axes, 0, 0)]
    all_to_all x5, waiting for transfers between devices: 30.1 us -> 27.5 us  [exchange(): return lax.all_to_all(blocks, axes, 0, 0)]
  transfers between devices with their start and end apart: 11 -> 11, of which waited for: 9 -> 9; matrix products, arithmetic and copies ran while one was open for 2% -> 1% of each run, Pallas kernels for 2% -> 2%
where the time goes in v7:
time: 196 us; the launch traced here: 195 us
  blocking collectives  81.4 us (42%)
  starting transfers between devices  59.8 us (31%)
  waiting for transfers between devices  35.3 us (18%)
  Pallas kernels  6.21 us (3%)
  other arithmetic  4.05 us (2%)
  matrix products  3.72 us (2%)
  local copies, waits for them, and re-layouts  3.39 us (2%)
    all_to_all x8, blocking collectives, exchange(): return lax.all_to_all(blocks, axes, 0, 0)  81.4 us
    all_to_all x5, waiting for transfers between devices, exchange(): return lax.all_to_all(blocks, axes, 0, 0)  27.5 us
    all_to_all x5, starting transfers between devices, exchange(): return lax.all_to_all(blocks, axes, 0, 0)  23.8 us
    ppermute x4, starting transfers between devices, doubled(): other = lax.ppermute(held, axis, pairs)  21.8 us
    ppermute x2, starting transfers between devices, other_core(): return lax.ppermute(value, 'c', [(0, 1), (1, 0)])  14.3 us
    ppermute x4, waiting for transfers between devices, doubled(): other = lax.ppermute(held, axis, pairs)  6.41 us
  transfers between devices with their start and end apart: 11, of which 9 were waited for; matrix products, arithmetic and copies ran while one was open for 1% of the time, Pallas kernels for 2%

profile of v7, /device:TPU:1, one launch (start us, length us, event | category | flops | bytes accessed | tf_op | source)
XLA Modules:
  0.0 194.9 jit_solution(18384451007457276555)
XLA Ops:
  0.6 11.5 %collective-permute-start = (bf16[64,128]{1,0:T(8,128)(2,1)}, bf16[64,128]{1,0:T(8,128)(2,1)S(1)}, u32[]{:S(2)}, u32[]{:S(2)}) collective-permute-start(bf16[64,128]{1,0:T(8,128)(2,1)} %bitcast.119), channel_id=1, source_target_pairs={{0,4},{4,0},{1,5},{5,1},{2,6},{6,2},{3,7},{7,3},{8,12},{12,8},{9,1... | collective-permute-start | bytes 49160 | tf_op jit(solution)/shard_map/ppermute | solution.py:164
  12.1 2.7 %shard_map.131 = bf16[8,64,1024]{2,1,0:T(8,128)(2,1)} custom-call(bf16[64,8192]{1,0:T(8,128)(2,1)} %bitcast.98), custom_call_target="tpu_custom_call" | custom-call | tf_op jit(solution)/shard_map/pallas_call | solution.py:68
  14.8 5.4 %all-to-all-start = ((bf16[8,64,1024]{2,1,0:T(8,128)(2,1)}), bf16[8,64,1024]{2,1,0:T(8,128)(2,1)S(1)}, u32[]{:S(2)}, u32[]{:S(2)}) async-start(bf16[8,64,1024]{2,1,0:T(8,128)(2,1)} %shard_map.131), calls=%async_computation | async-start | bytes 2097152 | tf_op jit(solution)/shard_map/all_to_all | solution.py:32
  20.4 1.7 shard_map.132
  22.1 4.0 %collective-permute-start.1 = (bf16[2,64,128]{2,1,0:T(8,128)(2,1)S(1)}, bf16[2,64,128]{2,1,0:T(8,128)(2,1)S(1)}, u32[]{:S(2)}, u32[]{:S(2)}) collective-permute-start(bf16[2,64,128]{2,1,0:T(8,128)(2,1)S(1)} %maximum_select_fusion.6), channel_id=1, source_target_pairs={{0,32},{16,48},{32,0},{48,16},{1,33},{17,49},{33,1},{49,17},{2,34}... | collective-permute-start | bytes 98312 | tf_op jit(solution)/shard_map/ppermute | solution.py:164
  26.2 1.8 collective-permute-done.1
  28.0 3.1 %collective-permute-start.2 = (bf16[2,2,64,128]{3,2,1,0:T(8,128)(2,1)S(1)}, bf16[2,2,64,128]{3,2,1,0:T(8,128)(2,1)S(1)}, u32[]{:S(2)}, u32[]{:S(2)}) collective-permute-start(bf16[2,2,64,128]{3,2,1,0:T(8,128)(2,1)S(1)} %maximum_select_fusion.4), channel_id=1, source_target_pairs={{0,16},{16,0},{32,48},{48,32},{1,17},{17,1},{33,49},{49,33},{2,18}... | collective-permute-start | bytes 196616 | tf_op jit(solution)/shard_map/ppermute | solution.py:164
  31.1 2.2 %collective-permute-done.2 = bf16[2,2,64,128]{3,2,1,0:T(8,128)(2,1)S(1)} collective-permute-done((bf16[2,2,64,128]{3,2,1,0:T(8,128)(2,1)S(1)}, bf16[2,2,64,128]{3,2,1,0:T(8,128)(2,1)S(1)}, u32[]{:S(2)}, u32[]{:S(2)}) %collective-permute-start.2) | collective-permute-done | bytes 65568 | tf_op jit(solution)/shard_map/ppermute | solution.py:164
  33.3 3.2 %collective-permute-start.3 = (bf16[2,2,2,64,128]{4,3,2,1,0:T(8,128)(2,1)S(1)}, bf16[2,2,2,64,128]{4,3,2,1,0:T(8,128)(2,1)S(1)}, u32[]{:S(2)}, u32[]{:S(2)}) collective-permute-start(bf16[2,2,2,64,128]{4,3,2,1,0:T(8,128)(2,1)S(1)} %maximum_select_fusion.2), channel_id=1, source_target_pairs={{0,64},{64,0},{1,65},{65,1},{2,66},{66,2},{3,67},{67,3},{4,68},{68... | collective-permute-start | bytes 393224 | tf_op jit(solution)/shard_map/ppermute | solution.py:164
  36.6 2.4 %collective-permute-done.3 = bf16[2,2,2,64,128]{4,3,2,1,0:T(8,128)(2,1)S(1)} collective-permute-done((bf16[2,2,2,64,128]{4,3,2,1,0:T(8,128)(2,1)S(1)}, bf16[2,2,2,64,128]{4,3,2,1,0:T(8,128)(2,1)S(1)}, u32[]{:S(2)}, u32[]{:S(2)}) %collective-permute-start.3) | collective-permute-done | bytes 131104 | tf_op jit(solution)/shard_map/ppermute | solution.py:164
  39.1 1.1 fusion.1
  40.8 8.0 %all-to-all-start.1 = ((bf16[8,64,128]{2,1,0:T(8,128)(2,1)}), bf16[8,64,128]{2,1,0:T(8,128)(2,1)S(1)}, u32[]{:S(2)}, u32[]{:S(2)}) async-start(bf16[8,64,128]{2,1,0:T(8,128)(2,1)} %bitcast.17), calls=%async_computation.1 | async-start | bytes 262144 | tf_op jit(solution)/shard_map/all_to_all | solution.py:32
  48.9 5.1 %all-to-all-done.1 = bf16[8,64,128]{2,1,0:T(8,128)(2,1)S(1)} async-done(((bf16[8,64,128]{2,1,0:T(8,128)(2,1)}), bf16[8,64,128]{2,1,0:T(8,128)(2,1)S(1)}, u32[]{:S(2)}, u32[]{:S(2)}) %all-to-all-start.1) | async-done | bytes 131104 | tf_op jit(solution)/shard_map/all_to_all | solution.py:32
  54.4 4.2 %all_to_all.65 = bf16[2,1152,128]{2,1,0:T(8,128)(2,1)S(1)} all-to-all(bf16[2,1152,128]{2,1,0:T(8,128)(2,1)S(1)} %pad_maximum_fusion), channel_id=1, replica_groups=mesh['p'=4,'yl'=2,'zl'=4,'c'=2,'zh'=2,'x'=4] {'c'}, dimensions={0} | all-to-all | bytes 1179648 | tf_op jit(solution)/shard_map/all_to_all | solution.py:32
  59.4 3.4 %all-to-all-start.3 = ((bf16[4,256,128]{2,1,0:T(8,128)(2,1)}), bf16[4,256,128]{2,1,0:T(8,128)(2,1)S(1)}, u32[]{:S(2)}, u32[]{:S(2)}) async-start(bf16[4,256,128]{2,1,0:T(8,128)(2,1)} %bitcast.29), calls=%async_computation.3 | async-start | bytes 524288 | tf_op jit(solution)/shard_map/all_to_all | solution.py:32
  62.8 6.0 %all-to-all-done.3 = bf16[4,256,128]{2,1,0:T(8,128)(2,1)S(1)} async-done(((bf16[4,256,128]{2,1,0:T(8,128)(2,1)}), bf16[4,256,128]{2,1,0:T(8,128)(2,1)S(1)}, u32[]{:S(2)}, u32[]{:S(2)}) %all-to-all-start.3) | async-done | bytes 262176 | tf_op jit(solution)/shard_map/all_to_all | solution.py:32
  68.9 10.9 %all_to_all.66 = bf16[8,64,128]{2,1,0:T(8,128)(2,1)S(1)} all-to-all(bf16[8,64,128]{2,1,0:T(8,128)(2,1)S(1)} %pad_maximum_fusion.3), channel_id=1, replica_groups=mesh['p'=4,'yl'=2,'zl'=4,'c'=2,'zh'=2,'x'=4] {'zl','zh'}, dimensions={0} | all-to-all | bytes 262144 | tf_op jit(solution)/shard_map/all_to_all | solution.py:32
  80.4 13.8 %all_to_all.67 = bf16[8,32,128]{2,1,0:T(8,128)(2,1)S(1)} all-to-all(bf16[8,32,128]{2,1,0:T(8,128)(2,1)S(1)} %broadcast_in_dim.21), channel_id=1, replica_groups=mesh['p'=4,'yl'=2,'zl'=4,'c'=2,'zh'=2,'x'=4] {'p','yl'}, dimensions={0} | all-to-all | bytes 131072 | tf_op jit(solution)/shard_map/all_to_all | solution.py:32
  94.3 8.6 %all_to_all.68 = bf16[4,256,128]{2,1,0:T(8,128)(2,1)} all-to-all(bf16[4,256,128]{2,1,0:T(8,128)(2,1)S(1)} %broadcast_in_dim.23), channel_id=1, replica_groups=mesh['p'=4,'yl'=2,'zl'=4,'c'=2,'zh'=2,'x'=4] {'x'}, dimensions={0} | all-to-all | bytes 524288 | tf_op jit(solution)/shard_map/all_to_all | solution.py:32
  102.9 1.9 shard_map.133
  104.8 7.4 %collective-permute-start.4 = (bf16[128,128]{1,0:T(8,128)(2,1)}, bf16[128,128]{1,0:T(8,128)(2,1)S(1)}, u32[]{:S(2)}, u32[]{:S(2)}) collective-permute-start(bf16[128,128]{1,0:T(8,128)(2,1)} %shard_map.133), channel_id=1, source_target_pairs={{0,8},{8,0},{1,9},{9,1},{2,10},{10,2},{3,11},{11,3},{4,12},{12,4},... | collective-permute-start | bytes 98312 | tf_op jit(solution)/shard_map/ppermute | solution.py:152
  112.1 1.0 collective-permute-done.4
  114.7 3.4 %all-to-all-start.7 = ((bf16[8,128,128]{2,1,0:T(8,128)(2,1)}), bf16[8,128,128]{2,1,0:T(8,128)(2,1)S(1)}, u32[]{:S(2)}, u32[]{:S(2)}) async-start(bf16[8,128,128]{2,1,0:T(8,128)(2,1)} %broadcast_in_dim.24), calls=%async_computation.7 | async-start | bytes 524288 | tf_op jit(solution)/shard_map/all_to_all | solution.py:32
  118.4 6.8 %all-to-all-done.7 = bf16[8,128,128]{2,1,0:T(8,128)(2,1)S(1)} async-done(((bf16[8,128,128]{2,1,0:T(8,128)(2,1)}), bf16[8,128,128]{2,1,0:T(8,128)(2,1)S(1)}, u32[]{:S(2)}, u32[]{:S(2)}) %all-to-all-start.7) | async-done | bytes 262176 | tf_op jit(solution)/shard_map/all_to_all | solution.py:32
  125.7 6.7 %all_to_all.69 = bf16[4,48,128]{2,1,0:T(8,128)(2,1)S(1)} all-to-all(bf16[4,48,128]{2,1,0:T(8,128)(2,1)S(1)} %bitcast.118), channel_id=1, replica_groups=mesh['p'=4,'yl'=2,'zl'=4,'c'=2,'zh'=2,'x'=4] {'x'}, dimensions={0} | all-to-all | bytes 98304 | tf_op jit(solution)/shard_map/all_to_all | solution.py:32
  132.5 10.0 %all_to_all.70 = bf16[8,48,128]{2,1,0:T(8,128)(2,1)S(1)} all-to-all(bf16[8,48,128]{2,1,0:T(8,128)(2,1)S(1)} %broadcast_in_dim.25), channel_id=1, replica_groups=mesh['p'=4,'yl'=2,'zl'=4,'c'=2,'zh'=2,'x'=4] {'p','yl'}, dimensions={0} | all-to-all | bytes 196608 | tf_op jit(solution)/shard_map/all_to_all | solution.py:32
  142.5 19.2 %all_to_all.71 = bf16[32,48,128]{2,1,0:T(8,128)(2,1)S(1)} all-to-all(bf16[32,48,128]{2,1,0:T(8,128)(2,1)S(1)} %broadcast_in_dim.26), channel_id=1, replica_groups=mesh['p'=4,'yl'=2,'zl'=4,'c'=2,'zh'=2,'x'=4] {'zl','zh','x'}, dimensions={0} | all-to-all | bytes 786432 | tf_op jit(solution)/shard_map/all_to_all | solution.py:32
  161.7 6.9 %collective-permute-start.5 = (bf16[32,48,128]{2,1,0:T(8,128)(2,1)S(1)}, bf16[32,48,128]{2,1,0:T(8,128)(2,1)S(1)}, u32[]{:S(2)}, u32[]{:S(2)}) collective-permute-start(bf16[32,48,128]{2,1,0:T(8,128)(2,1)S(1)} %all_to_all.71), channel_id=1, source_target_pairs={{0,8},{8,0},{1,9},{9,1},{2,10},{10,2},{3,11},{11,3},{4,12},{12,4},... | collective-permute-start | bytes 1179656 | tf_op jit(solution)/shard_map/ppermute | solution.py:152
  171.4 7.9 %all_to_all.72 = bf16[8,64,128]{2,1,0:T(8,128)(2,1)S(1)} all-to-all(bf16[8,64,128]{2,1,0:T(8,128)(2,1)S(1)} %broadcast_in_dim.27), channel_id=1, replica_groups=mesh['p'=4,'yl'=2,'zl'=4,'c'=2,'zh'=2,'x'=4] {'c','x'}, dimensions={0} | all-to-all | bytes 262144 | tf_op jit(solution)/shard_map/all_to_all | solution.py:32
  179.3 1.2 fusion
  180.6 3.5 %all-to-all-start.12 = ((bf16[16,64,128]{2,1,0:T(8,128)(2,1)}), bf16[16,64,128]{2,1,0:T(8,128)(2,1)S(1)}, u32[]{:S(2)}, u32[]{:S(2)}) async-start(bf16[16,64,128]{2,1,0:T(8,128)(2,1)} %bitcast.53), calls=%async_computation.12 | async-start | bytes 524288 | tf_op jit(solution)/shard_map/all_to_all | solution.py:32
  184.7 9.5 %all-to-all-done.12 = bf16[16,64,128]{2,1,0:T(8,128)(2,1)S(1)} async-done(((bf16[16,64,128]{2,1,0:T(8,128)(2,1)}), bf16[16,64,128]{2,1,0:T(8,128)(2,1)S(1)}, u32[]{:S(2)}, u32[]{:S(2)}) %all-to-all-start.12) | async-done | bytes 262176 | tf_op jit(solution)/shard_map/all_to_all | solution.py:32
  (73 shorter events, 9.2 us)
Async XLA Ops:
  0.6 21.5 %collective-permute-start = (bf16[64,128]{1,0:T(8,128)(2,1)}, bf16[64,128]{1,0:T(8,128)(2,1)S(1)}, u32[]{:S(2)}, u32[]{:S(2)}) collective-permute-start(bf16[64,128]{1,0:T(8,128)(2,1)} %bitcast.119), channel_id=1, source_target_pairs={{0,4},{4,0},{1,5},{5,1},{2,6},{6,2},{3,7},{7,3},{8,12},{12,8},{9,1... | collective-permute-start | bytes 49160 | tf_op jit(solution)/shard_map/ppermute | solution.py:164
  14.8 5.4 %copy-start.1 = (bf16[1,1536,64]{1,2,0:T(8,128)(2,1)S(1)}, bf16[1,1536,64]{1,2,0:T(8,128)(2,1)}, u32[]{:S(2)}) copy-start(bf16[1,1536,64]{1,2,0:T(8,128)(2,1)} %param.14) | copy-start | bytes 589828
  14.8 7.3 %copy-start.3 = (bf16[1,64,128]{2,1,0:T(8,128)(2,1)S(1)}, bf16[1,64,128]{2,1,0:T(8,128)(2,1)}, u32[]{:S(2)}) copy-start(bf16[1,64,128]{2,1,0:T(8,128)(2,1)} %param.12) | copy-start | bytes 49156
  14.8 24.3 %all-to-all-start = ((bf16[8,64,1024]{2,1,0:T(8,128)(2,1)}), bf16[8,64,1024]{2,1,0:T(8,128)(2,1)S(1)}, u32[]{:S(2)}, u32[]{:S(2)}) async-start(bf16[8,64,1024]{2,1,0:T(8,128)(2,1)} %shard_map.131), calls=%async_computation | async-start | bytes 2097152 | tf_op jit(solution)/shard_map/all_to_all | solution.py:32
  22.1 5.9 %collective-permute-start.1 = (bf16[2,64,128]{2,1,0:T(8,128)(2,1)S(1)}, bf16[2,64,128]{2,1,0:T(8,128)(2,1)S(1)}, u32[]{:S(2)}, u32[]{:S(2)}) collective-permute-start(bf16[2,64,128]{2,1,0:T(8,128)(2,1)S(1)} %maximum_select_fusion.6), channel_id=1, source_target_pairs={{0,32},{16,48},{32,0},{48,16},{1,33},{17,49},{33,1},{49,17},{2,34}... | collective-permute-start | bytes 98312 | tf_op jit(solution)/shard_map/ppermute | solution.py:164
  28.0 5.3 %collective-permute-start.2 = (bf16[2,2,64,128]{3,2,1,0:T(8,128)(2,1)S(1)}, bf16[2,2,64,128]{3,2,1,0:T(8,128)(2,1)S(1)}, u32[]{:S(2)}, u32[]{:S(2)}) collective-permute-start(bf16[2,2,64,128]{3,2,1,0:T(8,128)(2,1)S(1)} %maximum_select_fusion.4), channel_id=1, source_target_pairs={{0,16},{16,0},{32,48},{48,32},{1,17},{17,1},{33,49},{49,33},{2,18}... | collective-permute-start | bytes 196616 | tf_op jit(solution)/shard_map/ppermute | solution.py:164
  33.3 5.7 %collective-permute-start.3 = (bf16[2,2,2,64,128]{4,3,2,1,0:T(8,128)(2,1)S(1)}, bf16[2,2,2,64,128]{4,3,2,1,0:T(8,128)(2,1)S(1)}, u32[]{:S(2)}, u32[]{:S(2)}) collective-permute-start(bf16[2,2,2,64,128]{4,3,2,1,0:T(8,128)(2,1)S(1)} %maximum_select_fusion.2), channel_id=1, source_target_pairs={{0,64},{64,0},{1,65},{65,1},{2,66},{66,2},{3,67},{67,3},{4,68},{68... | collective-permute-start | bytes 393224 | tf_op jit(solution)/shard_map/ppermute | solution.py:164
  40.7 13.3 %copy-start.4 = (bf16[6,128]{1,0:T(8,128)(2,1)S(1)}, bf16[6,128]{1,0:T(8,128)(2,1)}, u32[]{:S(2)}) copy-start(bf16[6,128]{1,0:T(8,128)(2,1)} %param.19) | copy-start | bytes 4612
  40.8 13.2 %all-to-all-start.1 = ((bf16[8,64,128]{2,1,0:T(8,128)(2,1)}), bf16[8,64,128]{2,1,0:T(8,128)(2,1)S(1)}, u32[]{:S(2)}, u32[]{:S(2)}) async-start(bf16[8,64,128]{2,1,0:T(8,128)(2,1)} %bitcast.17), calls=%async_computation.1 | async-start | bytes 262144 | tf_op jit(solution)/shard_map/all_to_all | solution.py:32
  48.8 5.5 %copy-start.2 = (bf16[16,2,8,128]{3,2,1,0:T(8,128)(2,1)S(1)}, bf16[16,2,8,128]{3,2,1,0:T(8,128)(2,1)}, u32[]{:S(2)}) copy-start(bf16[16,2,8,128]{3,2,1,0:T(8,128)(2,1)} %shard_map.132) | copy-start | bytes 196612
  59.4 9.5 %all-to-all-start.3 = ((bf16[4,256,128]{2,1,0:T(8,128)(2,1)}), bf16[4,256,128]{2,1,0:T(8,128)(2,1)S(1)}, u32[]{:S(2)}, u32[]{:S(2)}) async-start(bf16[4,256,128]{2,1,0:T(8,128)(2,1)} %bitcast.29), calls=%async_computation.3 | async-start | bytes 524288 | tf_op jit(solution)/shard_map/all_to_all | solution.py:32
  94.3 23.8 %copy-start = (bf16[8,32,128]{2,1,0:T(8,128)(2,1)S(1)}, bf16[8,32,128]{2,1,0:T(8,128)(2,1)}, u32[]{:S(2)}) copy-start(bf16[8,32,128]{2,1,0:T(8,128)(2,1)} %get-tuple-element.15) | copy-start | bytes 196612
  104.8 8.4 %collective-permute-start.4 = (bf16[128,128]{1,0:T(8,128)(2,1)}, bf16[128,128]{1,0:T(8,128)(2,1)S(1)}, u32[]{:S(2)}, u32[]{:S(2)}) collective-permute-start(bf16[128,128]{1,0:T(8,128)(2,1)} %shard_map.133), channel_id=1, source_target_pairs={{0,8},{8,0},{1,9},{9,1},{2,10},{10,2},{3,11},{11,3},{4,12},{12,4},... | collective-permute-start | bytes 98312 | tf_op jit(solution)/shard_map/ppermute | solution.py:152
  114.7 10.5 %all-to-all-start.7 = ((bf16[8,128,128]{2,1,0:T(8,128)(2,1)}), bf16[8,128,128]{2,1,0:T(8,128)(2,1)S(1)}, u32[]{:S(2)}, u32[]{:S(2)}) async-start(bf16[8,128,128]{2,1,0:T(8,128)(2,1)} %broadcast_in_dim.24), calls=%async_computation.7 | async-start | bytes 524288 | tf_op jit(solution)/shard_map/all_to_all | solution.py:32
  125.2 43.4 %copy-start.6 = (f32[1,32]{1,0:T(1,128)S(1)}, f32[1,32]{1,0:T(1,128)}, u32[]{:S(2)}) copy-start(f32[1,32]{1,0:T(1,128)} %param.17) | copy-start | bytes 388
  125.3 43.4 %copy-start.7 = (s32[1,32]{1,0:T(1,128)S(1)}, s32[1,32]{1,0:T(1,128)}, u32[]{:S(2)}) copy-start(s32[1,32]{1,0:T(1,128)} %param.18) | copy-start | bytes 388
  161.7 8.3 %collective-permute-start.5 = (bf16[32,48,128]{2,1,0:T(8,128)(2,1)S(1)}, bf16[32,48,128]{2,1,0:T(8,128)(2,1)S(1)}, u32[]{:S(2)}, u32[]{:S(2)}) collective-permute-start(bf16[32,48,128]{2,1,0:T(8,128)(2,1)S(1)} %all_to_all.71), channel_id=1, source_target_pairs={{0,8},{8,0},{1,9},{9,1},{2,10},{10,2},{3,11},{11,3},{4,12},{12,4},... | collective-permute-start | bytes 1179656 | tf_op jit(solution)/shard_map/ppermute | solution.py:152
  170.3 0.8 copy-start.5
  180.6 13.7 %all-to-all-start.12 = ((bf16[16,64,128]{2,1,0:T(8,128)(2,1)}), bf16[16,64,128]{2,1,0:T(8,128)(2,1)S(1)}, u32[]{:S(2)}, u32[]{:S(2)}) async-start(bf16[16,64,128]{2,1,0:T(8,128)(2,1)} %bitcast.53), calls=%async_computation.12 | async-start | bytes 524288 | tf_op jit(solution)/shard_map/all_to_all | solution.py:32

commit v8 on v6

--- a/solution.py
+++ b/solution.py
@@ -179,6 +179,10 @@
     )
 
 
+def xred(term):
+    return gather(term, ("x",))
+
+
 def on_device(
     leaf_rhs,
     leaf_inverse,
@@ -224,7 +228,10 @@
     dinv_rows = pivots[:, 0:1] + pivots[:, 1:2] + pivots[:, 2:3]
     joined_rows = pivots[:, 3:4] + pivots[:, 4:5] + pivots[:, 5:6]
     term = summed(term[:, :120]).astype(BF16)
-    term = summed(gather(term, ("x",))).astype(BF16)
+    term, root_block, dinv_rows, joined_rows = lax.optimization_barrier(
+        (xred(term), root_block, dinv_rows, joined_rows)
+    )
+    term = summed(term).astype(BF16)
     term = gather(term, YALL).reshape(120, 8, RHS)
 
     wide, narrow = combine(root_tiles, term, root_block)

time: 191 us -> 191 us (level)
  blocking collectives: 69.7 us -> 78.3 us
  waiting for transfers between devices: 37.9 us -> 33.9 us
  starting transfers between devices: 63.4 us -> 59.7 us
    all_to_all x7, blocking collectives: 69.7 us -> 78.3 us  [exchange(): return lax.all_to_all(blocks, axes, 0, 0)]
    all_to_all x5, waiting for transfers between devices: 30.1 us -> 26.1 us  [exchange(): return lax.all_to_all(blocks, axes, 0, 0)]
    all_to_all x5, starting transfers between devices: 27.2 us -> 23.7 us  [exchange(): return lax.all_to_all(blocks, axes, 0, 0)]
  transfers between devices with their start and end apart: 11 -> 11, of which waited for: 9 -> 9; matrix products, arithmetic and copies ran while one was open for 2% -> 1% of each run, Pallas kernels for 2% -> 2%
where the time goes in v8:
time: 191 us; the launch traced here: 190 us
  blocking collectives  78.3 us (41%)
  starting transfers between devices  59.7 us (31%)
  waiting for transfers between devices  33.9 us (18%)
  Pallas kernels  6.28 us (3%)
  local copies, waits for them, and re-layouts  5.61 us (3%)
  other arithmetic  2.91 us (2%)
  matrix products  2.19 us (1%)
    all_to_all x7, blocking collectives, exchange(): return lax.all_to_all(blocks, axes, 0, 0)  78.3 us
    all_to_all x5, waiting for transfers between devices, exchange(): return lax.all_to_all(blocks, axes, 0, 0)  26.1 us
    all_to_all x5, starting transfers between devices, exchange(): return lax.all_to_all(blocks, axes, 0, 0)  23.7 us
    ppermute x4, starting transfers between devices, doubled(): other = lax.ppermute(held, axis, pairs)  21.8 us
    ppermute x2, starting transfers between devices, other_core(): return lax.ppermute(value, 'c', [(0, 1), (1, 0)])  14.2 us
    ppermute x4, waiting for transfers between devices, doubled(): other = lax.ppermute(held, axis, pairs)  6.41 us
  transfers between devices with their start and end apart: 11, of which 9 were waited for; matrix products, arithmetic and copies ran while one was open for 1% of the time, Pallas kernels for 2%

profile of v8, /device:TPU:1, one launch (start us, length us, event | category | flops | bytes accessed | tf_op | source)
XLA Modules:
  0.0 190.0 jit_solution(4464077603186523323)
XLA Ops:
  0.6 11.5 %collective-permute-start = (bf16[64,128]{1,0:T(8,128)(2,1)}, bf16[64,128]{1,0:T(8,128)(2,1)S(1)}, u32[]{:S(2)}, u32[]{:S(2)}) collective-permute-start(bf16[64,128]{1,0:T(8,128)(2,1)} %bitcast.119), channel_id=1, source_target_pairs={{0,4},{4,0},{1,5},{5,1},{2,6},{6,2},{3,7},{7,3},{8,12},{12,8},{9,1... | collective-permute-start | bytes 49160 | tf_op jit(solution)/shard_map/ppermute | solution.py:165
  12.1 2.7 %shard_map.131 = bf16[8,64,1024]{2,1,0:T(8,128)(2,1)} custom-call(bf16[64,8192]{1,0:T(8,128)(2,1)} %bitcast.101), custom_call_target="tpu_custom_call" | custom-call | tf_op jit(solution)/shard_map/pallas_call | solution.py:67
  14.8 5.4 %all-to-all-start = ((bf16[8,64,1024]{2,1,0:T(8,128)(2,1)}), bf16[8,64,1024]{2,1,0:T(8,128)(2,1)S(1)}, u32[]{:S(2)}, u32[]{:S(2)}) async-start(bf16[8,64,1024]{2,1,0:T(8,128)(2,1)} %shard_map.131), calls=%async_computation | async-start | bytes 2097152 | tf_op jit(solution)/shard_map/all_to_all | solution.py:31
  20.4 1.7 shard_map.132
  22.1 4.0 %collective-permute-start.1 = (bf16[2,64,128]{2,1,0:T(8,128)(2,1)S(1)}, bf16[2,64,128]{2,1,0:T(8,128)(2,1)S(1)}, u32[]{:S(2)}, u32[]{:S(2)}) collective-permute-start(bf16[2,64,128]{2,1,0:T(8,128)(2,1)S(1)} %maximum_select_fusion.6), channel_id=1, source_target_pairs={{0,32},{16,48},{32,0},{48,16},{1,33},{17,49},{33,1},{49,17},{2,34}... | collective-permute-start | bytes 98312 | tf_op jit(solution)/shard_map/ppermute | solution.py:165
  26.2 1.8 collective-permute-done.1
  28.0 3.1 %collective-permute-start.2 = (bf16[2,2,64,128]{3,2,1,0:T(8,128)(2,1)S(1)}, bf16[2,2,64,128]{3,2,1,0:T(8,128)(2,1)S(1)}, u32[]{:S(2)}, u32[]{:S(2)}) collective-permute-start(bf16[2,2,64,128]{3,2,1,0:T(8,128)(2,1)S(1)} %maximum_select_fusion.4), channel_id=1, source_target_pairs={{0,16},{16,0},{32,48},{48,32},{1,17},{17,1},{33,49},{49,33},{2,18}... | collective-permute-start | bytes 196616 | tf_op jit(solution)/shard_map/ppermute | solution.py:165
  31.1 2.2 %collective-permute-done.2 = bf16[2,2,64,128]{3,2,1,0:T(8,128)(2,1)S(1)} collective-permute-done((bf16[2,2,64,128]{3,2,1,0:T(8,128)(2,1)S(1)}, bf16[2,2,64,128]{3,2,1,0:T(8,128)(2,1)S(1)}, u32[]{:S(2)}, u32[]{:S(2)}) %collective-permute-start.2) | collective-permute-done | bytes 65568 | tf_op jit(solution)/shard_map/ppermute | solution.py:165
  33.3 3.2 %collective-permute-start.3 = (bf16[2,2,2,64,128]{4,3,2,1,0:T(8,128)(2,1)S(1)}, bf16[2,2,2,64,128]{4,3,2,1,0:T(8,128)(2,1)S(1)}, u32[]{:S(2)}, u32[]{:S(2)}) collective-permute-start(bf16[2,2,2,64,128]{4,3,2,1,0:T(8,128)(2,1)S(1)} %maximum_select_fusion.2), channel_id=1, source_target_pairs={{0,64},{64,0},{1,65},{65,1},{2,66},{66,2},{3,67},{67,3},{4,68},{68... | collective-permute-start | bytes 393224 | tf_op jit(solution)/shard_map/ppermute | solution.py:165
  36.6 2.4 %collective-permute-done.3 = bf16[2,2,2,64,128]{4,3,2,1,0:T(8,128)(2,1)S(1)} collective-permute-done((bf16[2,2,2,64,128]{4,3,2,1,0:T(8,128)(2,1)S(1)}, bf16[2,2,2,64,128]{4,3,2,1,0:T(8,128)(2,1)S(1)}, u32[]{:S(2)}, u32[]{:S(2)}) %collective-permute-start.3) | collective-permute-done | bytes 131104 | tf_op jit(solution)/shard_map/ppermute | solution.py:165
  40.2 0.7 copy.38
  40.9 8.0 %all-to-all-start.1 = ((bf16[8,64,128]{2,1,0:T(8,128)(2,1)}), bf16[8,64,128]{2,1,0:T(8,128)(2,1)S(1)}, u32[]{:S(2)}, u32[]{:S(2)}) async-start(bf16[8,64,128]{2,1,0:T(8,128)(2,1)} %bitcast.17), calls=%async_computation.1 | async-start | bytes 262144 | tf_op jit(solution)/shard_map/all_to_all | solution.py:31
  49.0 5.1 %all-to-all-done.1 = bf16[8,64,128]{2,1,0:T(8,128)(2,1)S(1)} async-done(((bf16[8,64,128]{2,1,0:T(8,128)(2,1)}), bf16[8,64,128]{2,1,0:T(8,128)(2,1)S(1)}, u32[]{:S(2)}, u32[]{:S(2)}) %all-to-all-start.1) | async-done | bytes 131104 | tf_op jit(solution)/shard_map/all_to_all | solution.py:31
  54.5 4.2 %all_to_all.60 = bf16[2,1088,128]{2,1,0:T(8,128)(2,1)S(1)} all-to-all(bf16[2,1088,128]{2,1,0:T(8,128)(2,1)S(1)} %bitcast.92), channel_id=1, replica_groups=mesh['p'=4,'yl'=2,'zl'=4,'c'=2,'zh'=2,'x'=4] {'c'}, dimensions={0} | all-to-all | bytes 1114112 | tf_op jit(solution)/shard_map/all_to_all | solution.py:31
  58.8 14.3 %all_to_all.61 = bf16[8,152,128]{2,1,0:T(8,128)(2,1)S(1)} all-to-all(bf16[8,152,128]{2,1,0:T(8,128)(2,1)S(1)} %pad_maximum_fusion.1), channel_id=1, replica_groups=mesh['p'=4,'yl'=2,'zl'=4,'c'=2,'zh'=2,'x'=4] {'zl','zh'}, dimensions={0} | all-to-all | bytes 622592 | tf_op jit(solution)/shard_map/all_to_all | solution.py:31
  73.9 3.3 %all-to-all-start.4 = ((bf16[4,120,128]{2,1,0:T(8,128)(2,1)}), bf16[4,120,128]{2,1,0:T(8,128)(2,1)S(1)}, u32[]{:S(2)}, u32[]{:S(2)}) async-start(bf16[4,120,128]{2,1,0:T(8,128)(2,1)} %broadcast_in_dim.17), calls=%async_computation.4 | async-start | bytes 245760 | tf_op jit(solution)/shard_map/all_to_all | solution.py:31
  77.4 4.6 %all-to-all-done.4 = bf16[4,120,128]{2,1,0:T(8,128)(2,1)S(1)} async-done(((bf16[4,120,128]{2,1,0:T(8,128)(2,1)}), bf16[4,120,128]{2,1,0:T(8,128)(2,1)S(1)}, u32[]{:S(2)}, u32[]{:S(2)}) %all-to-all-start.4) | async-done | bytes 122912 | tf_op jit(solution)/shard_map/all_to_all | solution.py:31
  82.0 15.9 %all_to_all.62 = bf16[8,120,128]{2,1,0:T(8,128)(2,1)} all-to-all(bf16[8,120,128]{2,1,0:T(8,128)(2,1)S(1)} %broadcast_in_dim.18), channel_id=1, replica_groups=mesh['p'=4,'yl'=2,'zl'=4,'c'=2,'zh'=2,'x'=4] {'p','yl'}, dimensions={0} | all-to-all | bytes 491520 | tf_op jit(solution)/shard_map/all_to_all | solution.py:31
  97.9 1.9 %shard_map.133 = (f32[128,128]{1,0:T(8,128)}, bf16[128,128]{1,0:T(8,128)(2,1)}) custom-call(s32[4,12]{1,0:T(4,128)} %tiles_ref.1, bf16[120,8,128]{2,1,0:T(8,128)(2,1)} %bitcast.103, bf16[128,256]{1,0:T(8,128)(2,1)} %bitcast.105), custom_call_target="tpu_custom_call" | custom-call | tf_op jit(solution)/shard_map/pallas_call | solution.py:90
  99.8 7.3 %collective-permute-start.4 = (bf16[128,128]{1,0:T(8,128)(2,1)}, bf16[128,128]{1,0:T(8,128)(2,1)S(1)}, u32[]{:S(2)}, u32[]{:S(2)}) collective-permute-start(bf16[128,128]{1,0:T(8,128)(2,1)} %get-tuple-element.18), channel_id=1, source_target_pairs={{0,8},{8,0},{1,9},{9,1},{2,10},{10,2},{3,11},{11,3},{4,12},{12,4},... | collective-permute-start | bytes 98312 | tf_op jit(solution)/shard_map/ppermute | solution.py:153
  107.2 1.0 collective-permute-done.4
  108.2 0.8 add_convert_fusion.1
  109.8 3.4 %all-to-all-start.6 = ((bf16[8,128,128]{2,1,0:T(8,128)(2,1)}), bf16[8,128,128]{2,1,0:T(8,128)(2,1)S(1)}, u32[]{:S(2)}, u32[]{:S(2)}) async-start(bf16[8,128,128]{2,1,0:T(8,128)(2,1)} %broadcast_in_dim.19), calls=%async_computation.6 | async-start | bytes 524288 | tf_op jit(solution)/shard_map/all_to_all | solution.py:31
  113.4 6.9 %all-to-all-done.6 = bf16[8,128,128]{2,1,0:T(8,128)(2,1)S(1)} async-done(((bf16[8,128,128]{2,1,0:T(8,128)(2,1)}), bf16[8,128,128]{2,1,0:T(8,128)(2,1)S(1)}, u32[]{:S(2)}, u32[]{:S(2)}) %all-to-all-start.6) | async-done | bytes 262176 | tf_op jit(solution)/shard_map/all_to_all | solution.py:31
  120.8 6.7 %all_to_all.63 = bf16[4,48,128]{2,1,0:T(8,128)(2,1)S(1)} all-to-all(bf16[4,48,128]{2,1,0:T(8,128)(2,1)S(1)} %bitcast.118), channel_id=1, replica_groups=mesh['p'=4,'yl'=2,'zl'=4,'c'=2,'zh'=2,'x'=4] {'x'}, dimensions={0} | all-to-all | bytes 98304 | tf_op jit(solution)/shard_map/all_to_all | solution.py:31
  127.6 10.0 %all_to_all.64 = bf16[8,48,128]{2,1,0:T(8,128)(2,1)S(1)} all-to-all(bf16[8,48,128]{2,1,0:T(8,128)(2,1)S(1)} %broadcast_in_dim.20), channel_id=1, replica_groups=mesh['p'=4,'yl'=2,'zl'=4,'c'=2,'zh'=2,'x'=4] {'p','yl'}, dimensions={0} | all-to-all | bytes 196608 | tf_op jit(solution)/shard_map/all_to_all | solution.py:31
  137.6 19.2 %all_to_all.65 = bf16[32,48,128]{2,1,0:T(8,128)(2,1)S(1)} all-to-all(bf16[32,48,128]{2,1,0:T(8,128)(2,1)S(1)} %broadcast_in_dim.21), channel_id=1, replica_groups=mesh['p'=4,'yl'=2,'zl'=4,'c'=2,'zh'=2,'x'=4] {'zl','zh','x'}, dimensions={0} | all-to-all | bytes 786432 | tf_op jit(solution)/shard_map/all_to_all | solution.py:31
  156.9 6.9 %collective-permute-start.5 = (bf16[32,48,128]{2,1,0:T(8,128)(2,1)S(1)}, bf16[32,48,128]{2,1,0:T(8,128)(2,1)S(1)}, u32[]{:S(2)}, u32[]{:S(2)}) collective-permute-start(bf16[32,48,128]{2,1,0:T(8,128)(2,1)S(1)} %all_to_all.65), channel_id=1, source_target_pairs={{0,8},{8,0},{1,9},{9,1},{2,10},{10,2},{3,11},{11,3},{4,12},{12,4},... | collective-permute-start | bytes 1179656 | tf_op jit(solution)/shard_map/ppermute | solution.py:153
  166.5 7.9 %all_to_all.66 = bf16[8,64,128]{2,1,0:T(8,128)(2,1)S(1)} all-to-all(bf16[8,64,128]{2,1,0:T(8,128)(2,1)S(1)} %broadcast_in_dim.22), channel_id=1, replica_groups=mesh['p'=4,'yl'=2,'zl'=4,'c'=2,'zh'=2,'x'=4] {'c','x'}, dimensions={0} | all-to-all | bytes 262144 | tf_op jit(solution)/shard_map/all_to_all | solution.py:31
  174.8 0.8 copy.44
  175.6 3.5 %all-to-all-start.11 = ((bf16[16,64,128]{2,1,0:T(8,128)(2,1)}), bf16[16,64,128]{2,1,0:T(8,128)(2,1)S(1)}, u32[]{:S(2)}, u32[]{:S(2)}) async-start(bf16[16,64,128]{2,1,0:T(8,128)(2,1)} %bitcast.51), calls=%async_computation.11 | async-start | bytes 524288 | tf_op jit(solution)/shard_map/all_to_all | solution.py:31
  179.8 9.6 %all-to-all-done.11 = bf16[16,64,128]{2,1,0:T(8,128)(2,1)S(1)} async-done(((bf16[16,64,128]{2,1,0:T(8,128)(2,1)}), bf16[16,64,128]{2,1,0:T(8,128)(2,1)S(1)}, u32[]{:S(2)}, u32[]{:S(2)}) %all-to-all-start.11) | async-done | bytes 262176 | tf_op jit(solution)/shard_map/all_to_all | solution.py:31
  (79 shorter events, 8.6 us)
Async XLA Ops:
  0.6 21.5 %collective-permute-start = (bf16[64,128]{1,0:T(8,128)(2,1)}, bf16[64,128]{1,0:T(8,128)(2,1)S(1)}, u32[]{:S(2)}, u32[]{:S(2)}) collective-permute-start(bf16[64,128]{1,0:T(8,128)(2,1)} %bitcast.119), channel_id=1, source_target_pairs={{0,4},{4,0},{1,5},{5,1},{2,6},{6,2},{3,7},{7,3},{8,12},{12,8},{9,1... | collective-permute-start | bytes 49160 | tf_op jit(solution)/shard_map/ppermute | solution.py:165
  14.8 5.4 %copy-start.2 = (bf16[1,1536,64]{1,2,0:T(8,128)(2,1)S(1)}, bf16[1,1536,64]{1,2,0:T(8,128)(2,1)}, u32[]{:S(2)}) copy-start(bf16[1,1536,64]{1,2,0:T(8,128)(2,1)} %param.14) | copy-start | bytes 589828
  14.8 7.3 %copy-start.4 = (bf16[1,64,128]{2,1,0:T(8,128)(2,1)S(1)}, bf16[1,64,128]{2,1,0:T(8,128)(2,1)}, u32[]{:S(2)}) copy-start(bf16[1,64,128]{2,1,0:T(8,128)(2,1)} %param.12) | copy-start | bytes 49156
  14.8 24.3 %all-to-all-start = ((bf16[8,64,1024]{2,1,0:T(8,128)(2,1)}), bf16[8,64,1024]{2,1,0:T(8,128)(2,1)S(1)}, u32[]{:S(2)}, u32[]{:S(2)}) async-start(bf16[8,64,1024]{2,1,0:T(8,128)(2,1)} %shard_map.131), calls=%async_computation | async-start | bytes 2097152 | tf_op jit(solution)/shard_map/all_to_all | solution.py:31
  22.1 5.9 %collective-permute-start.1 = (bf16[2,64,128]{2,1,0:T(8,128)(2,1)S(1)}, bf16[2,64,128]{2,1,0:T(8,128)(2,1)S(1)}, u32[]{:S(2)}, u32[]{:S(2)}) collective-permute-start(bf16[2,64,128]{2,1,0:T(8,128)(2,1)S(1)} %maximum_select_fusion.6), channel_id=1, source_target_pairs={{0,32},{16,48},{32,0},{48,16},{1,33},{17,49},{33,1},{49,17},{2,34}... | collective-permute-start | bytes 98312 | tf_op jit(solution)/shard_map/ppermute | solution.py:165
  28.0 5.3 %collective-permute-start.2 = (bf16[2,2,64,128]{3,2,1,0:T(8,128)(2,1)S(1)}, bf16[2,2,64,128]{3,2,1,0:T(8,128)(2,1)S(1)}, u32[]{:S(2)}, u32[]{:S(2)}) collective-permute-start(bf16[2,2,64,128]{3,2,1,0:T(8,128)(2,1)S(1)} %maximum_select_fusion.4), channel_id=1, source_target_pairs={{0,16},{16,0},{32,48},{48,32},{1,17},{17,1},{33,49},{49,33},{2,18}... | collective-permute-start | bytes 196616 | tf_op jit(solution)/shard_map/ppermute | solution.py:165
  33.3 5.7 %collective-permute-start.3 = (bf16[2,2,2,64,128]{4,3,2,1,0:T(8,128)(2,1)S(1)}, bf16[2,2,2,64,128]{4,3,2,1,0:T(8,128)(2,1)S(1)}, u32[]{:S(2)}, u32[]{:S(2)}) collective-permute-start(bf16[2,2,2,64,128]{4,3,2,1,0:T(8,128)(2,1)S(1)} %maximum_select_fusion.2), channel_id=1, source_target_pairs={{0,64},{64,0},{1,65},{65,1},{2,66},{66,2},{3,67},{67,3},{4,68},{68... | collective-permute-start | bytes 393224 | tf_op jit(solution)/shard_map/ppermute | solution.py:165
  40.1 14.1 %copy-start.5 = (bf16[6,128]{1,0:T(8,128)(2,1)S(1)}, bf16[6,128]{1,0:T(8,128)(2,1)}, u32[]{:S(2)}) copy-start(bf16[6,128]{1,0:T(8,128)(2,1)} %param.19) | copy-start | bytes 4612
  40.9 13.2 %all-to-all-start.1 = ((bf16[8,64,128]{2,1,0:T(8,128)(2,1)}), bf16[8,64,128]{2,1,0:T(8,128)(2,1)S(1)}, u32[]{:S(2)}, u32[]{:S(2)}) async-start(bf16[8,64,128]{2,1,0:T(8,128)(2,1)} %bitcast.17), calls=%async_computation.1 | async-start | bytes 262144 | tf_op jit(solution)/shard_map/all_to_all | solution.py:31
  48.9 5.5 %copy-start.3 = (bf16[16,2,8,128]{3,2,1,0:T(8,128)(2,1)S(1)}, bf16[16,2,8,128]{3,2,1,0:T(8,128)(2,1)}, u32[]{:S(2)}) copy-start(bf16[16,2,8,128]{3,2,1,0:T(8,128)(2,1)} %shard_map.132) | copy-start | bytes 196612
  73.1 24.8 %copy-start = (bf16[8,32,128]{2,1,0:T(8,128)(2,1)}, bf16[8,32,128]{2,1,0:T(8,128)(2,1)S(1)}, u32[]{:S(2)}) copy-start(bf16[8,32,128]{2,1,0:T(8,128)(2,1)S(1)} %slice.51) | copy-start | bytes 196612
  73.9 8.1 %all-to-all-start.4 = ((bf16[4,120,128]{2,1,0:T(8,128)(2,1)}), bf16[4,120,128]{2,1,0:T(8,128)(2,1)S(1)}, u32[]{:S(2)}, u32[]{:S(2)}) async-start(bf16[4,120,128]{2,1,0:T(8,128)(2,1)} %broadcast_in_dim.17), calls=%async_computation.4 | async-start | bytes 245760 | tf_op jit(solution)/shard_map/all_to_all | solution.py:31
  97.9 22.6 %copy-start.1 = (bf16[8,32,128]{2,1,0:T(8,128)(2,1)S(1)}, bf16[8,32,128]{2,1,0:T(8,128)(2,1)}, u32[]{:S(2)}) copy-start(bf16[8,32,128]{2,1,0:T(8,128)(2,1)} %copy-done) | copy-start | bytes 196612
  99.8 8.4 %collective-permute-start.4 = (bf16[128,128]{1,0:T(8,128)(2,1)}, bf16[128,128]{1,0:T(8,128)(2,1)S(1)}, u32[]{:S(2)}, u32[]{:S(2)}) collective-permute-start(bf16[128,128]{1,0:T(8,128)(2,1)} %get-tuple-element.18), channel_id=1, source_target_pairs={{0,8},{8,0},{1,9},{9,1},{2,10},{10,2},{3,11},{11,3},{4,12},{12,4},... | collective-permute-start | bytes 98312 | tf_op jit(solution)/shard_map/ppermute | solution.py:153
  109.8 10.5 %all-to-all-start.6 = ((bf16[8,128,128]{2,1,0:T(8,128)(2,1)}), bf16[8,128,128]{2,1,0:T(8,128)(2,1)S(1)}, u32[]{:S(2)}, u32[]{:S(2)}) async-start(bf16[8,128,128]{2,1,0:T(8,128)(2,1)} %broadcast_in_dim.19), calls=%async_computation.6 | async-start | bytes 524288 | tf_op jit(solution)/shard_map/all_to_all | solution.py:31
  120.4 43.4 %copy-start.7 = (f32[1,32]{1,0:T(1,128)S(1)}, f32[1,32]{1,0:T(1,128)}, u32[]{:S(2)}) copy-start(f32[1,32]{1,0:T(1,128)} %param.17) | copy-start | bytes 388
  120.4 43.4 %copy-start.8 = (s32[1,32]{1,0:T(1,128)S(1)}, s32[1,32]{1,0:T(1,128)}, u32[]{:S(2)}) copy-start(s32[1,32]{1,0:T(1,128)} %param.18) | copy-start | bytes 388
  156.9 8.3 %collective-permute-start.5 = (bf16[32,48,128]{2,1,0:T(8,128)(2,1)S(1)}, bf16[32,48,128]{2,1,0:T(8,128)(2,1)S(1)}, u32[]{:S(2)}, u32[]{:S(2)}) collective-permute-start(bf16[32,48,128]{2,1,0:T(8,128)(2,1)S(1)} %all_to_all.65), channel_id=1, source_target_pairs={{0,8},{8,0},{1,9},{9,1},{2,10},{10,2},{3,11},{11,3},{4,12},{12,4},... | collective-permute-start | bytes 1179656 | tf_op jit(solution)/shard_map/ppermute | solution.py:153
  165.5 0.8 copy-start.6
  175.6 13.7 %all-to-all-start.11 = ((bf16[16,64,128]{2,1,0:T(8,128)(2,1)}), bf16[16,64,128]{2,1,0:T(8,128)(2,1)S(1)}, u32[]{:S(2)}, u32[]{:S(2)}) async-start(bf16[16,64,128]{2,1,0:T(8,128)(2,1)} %bitcast.51), calls=%async_computation.11 | async-start | bytes 524288 | tf_op jit(solution)/shard_map/all_to_all | solution.py:31

commit v9 on v8

--- a/solution.py
+++ b/solution.py
@@ -70,7 +70,7 @@
     )(factor_rows)
 
 
-def combine_kernel(tiles_ref, terms_ref, block_ref, wide_ref, narrow_ref, total_ref):
+def combine_kernel(tiles_ref, terms_ref, block_ref, out_ref, total_ref):
     for y in range(8):
         for j in range(3):
             total_ref[3 * y + j] = -terms_ref[15 * y + 12 + j].astype(F32)
@@ -82,19 +82,15 @@
             total_ref[tile] = total_ref[tile] + term
     reduced = (-total_ref[...]).reshape(256, RHS).astype(BF16)
     product = jnp.dot(block_ref[...], reduced, preferred_element_type=F32)
-    wide_ref[...] = product
-    narrow_ref[...] = product.astype(BF16)
+    out_ref[...] = product.astype(BF16)
 
 
 def combine(root_tiles, terms, block):
     return pl.pallas_call(
         combine_kernel,
-        out_shape=(
-            jax.ShapeDtypeStruct((TILE, RHS), F32),
-            jax.ShapeDtypeStruct((TILE, RHS), BF16),
-        ),
+        out_shape=jax.ShapeDtypeStruct((TILE, RHS), BF16),
         in_specs=[SCALARS, VECTORS, VECTORS],
-        out_specs=(VECTORS, VECTORS),
+        out_specs=VECTORS,
         scratch_shapes=[pltpu.VMEM((ROOT_TILES + 8, 8, RHS), F32)],
     )(root_tiles, terms, block)
 
@@ -234,8 +230,8 @@
     term = summed(term).astype(BF16)
     term = gather(term, YALL).reshape(120, 8, RHS)
 
-    wide, narrow = combine(root_tiles, term, root_block)
-    forward = wide + other_core(narrow).astype(F32)
+    narrow = combine(root_tiles, term, root_block)
+    forward = narrow.astype(F32) + other_core(narrow).astype(F32)
     forward = summed(gather(forward.astype(BF16), Z))
     root_scaled = pivot_solve(forward, dinv_rows, joined_rows).astype(BF16)
     back = transposed_product(root_block[:, :192], root_scaled).astype(BF16)

time: 191 us -> 191 us (level)
  no operation moved by 1% of the time
where the time goes in v9:
time: 191 us; the launch traced here: 190 us
  blocking collectives  78.3 us (41%)
  starting transfers between devices  59.7 us (31%)
  waiting for transfers between devices  33.9 us (18%)
  Pallas kernels  6.26 us (3%)
  local copies, waits for them, and re-layouts  5.61 us (3%)
  other arithmetic  2.84 us (1%)
  matrix products  2.2 us (1%)
    all_to_all x7, blocking collectives, exchange(): return lax.all_to_all(blocks, axes, 0, 0)  78.3 us
    all_to_all x5, waiting for transfers between devices, exchange(): return lax.all_to_all(blocks, axes, 0, 0)  26.1 us
    all_to_all x5, starting transfers between devices, exchange(): return lax.all_to_all(blocks, axes, 0, 0)  23.7 us
    ppermute x4, starting transfers between devices, doubled(): other = lax.ppermute(held, axis, pairs)  21.8 us
    ppermute x2, starting transfers between devices, other_core(): return lax.ppermute(value, 'c', [(0, 1), (1, 0)])  14.2 us
    ppermute x4, waiting for transfers between devices, doubled(): other = lax.ppermute(held, axis, pairs)  6.41 us
  transfers between devices with their start and end apart: 11, of which 9 were waited for; matrix products, arithmetic and copies ran while one was open for 1% of the time, Pallas kernels for 2%

profile of v9, /device:TPU:1, one launch (start us, length us, event | category | flops | bytes accessed | tf_op | source)
XLA Modules:
  0.0 189.9 jit_solution(10338540053052836388)
XLA Ops:
  0.6 11.5 %collective-permute-start = (bf16[64,128]{1,0:T(8,128)(2,1)}, bf16[64,128]{1,0:T(8,128)(2,1)S(1)}, u32[]{:S(2)}, u32[]{:S(2)}) collective-permute-start(bf16[64,128]{1,0:T(8,128)(2,1)} %bitcast.119), channel_id=1, source_target_pairs={{0,4},{4,0},{1,5},{5,1},{2,6},{6,2},{3,7},{7,3},{8,12},{12,8},{9,1... | collective-permute-start | bytes 49160 | tf_op jit(solution)/shard_map/ppermute | solution.py:161
  12.1 2.7 %shard_map.131 = bf16[8,64,1024]{2,1,0:T(8,128)(2,1)} custom-call(bf16[64,8192]{1,0:T(8,128)(2,1)} %bitcast.101), custom_call_target="tpu_custom_call" | custom-call | tf_op jit(solution)/shard_map/pallas_call | solution.py:67
  14.8 5.4 %all-to-all-start = ((bf16[8,64,1024]{2,1,0:T(8,128)(2,1)}), bf16[8,64,1024]{2,1,0:T(8,128)(2,1)S(1)}, u32[]{:S(2)}, u32[]{:S(2)}) async-start(bf16[8,64,1024]{2,1,0:T(8,128)(2,1)} %shard_map.131), calls=%async_computation | async-start | bytes 2097152 | tf_op jit(solution)/shard_map/all_to_all | solution.py:31
  20.4 1.7 shard_map.132
  22.1 4.0 %collective-permute-start.1 = (bf16[2,64,128]{2,1,0:T(8,128)(2,1)S(1)}, bf16[2,64,128]{2,1,0:T(8,128)(2,1)S(1)}, u32[]{:S(2)}, u32[]{:S(2)}) collective-permute-start(bf16[2,64,128]{2,1,0:T(8,128)(2,1)S(1)} %maximum_select_fusion.6), channel_id=1, source_target_pairs={{0,32},{16,48},{32,0},{48,16},{1,33},{17,49},{33,1},{49,17},{2,34}... | collective-permute-start | bytes 98312 | tf_op jit(solution)/shard_map/ppermute | solution.py:161
  26.2 1.8 collective-permute-done.1
  28.0 3.1 %collective-permute-start.2 = (bf16[2,2,64,128]{3,2,1,0:T(8,128)(2,1)S(1)}, bf16[2,2,64,128]{3,2,1,0:T(8,128)(2,1)S(1)}, u32[]{:S(2)}, u32[]{:S(2)}) collective-permute-start(bf16[2,2,64,128]{3,2,1,0:T(8,128)(2,1)S(1)} %maximum_select_fusion.4), channel_id=1, source_target_pairs={{0,16},{16,0},{32,48},{48,32},{1,17},{17,1},{33,49},{49,33},{2,18}... | collective-permute-start | bytes 196616 | tf_op jit(solution)/shard_map/ppermute | solution.py:161
  31.1 2.2 %collective-permute-done.2 = bf16[2,2,64,128]{3,2,1,0:T(8,128)(2,1)S(1)} collective-permute-done((bf16[2,2,64,128]{3,2,1,0:T(8,128)(2,1)S(1)}, bf16[2,2,64,128]{3,2,1,0:T(8,128)(2,1)S(1)}, u32[]{:S(2)}, u32[]{:S(2)}) %collective-permute-start.2) | collective-permute-done | bytes 65568 | tf_op jit(solution)/shard_map/ppermute | solution.py:161
  33.3 3.2 %collective-permute-start.3 = (bf16[2,2,2,64,128]{4,3,2,1,0:T(8,128)(2,1)S(1)}, bf16[2,2,2,64,128]{4,3,2,1,0:T(8,128)(2,1)S(1)}, u32[]{:S(2)}, u32[]{:S(2)}) collective-permute-start(bf16[2,2,2,64,128]{4,3,2,1,0:T(8,128)(2,1)S(1)} %maximum_select_fusion.2), channel_id=1, source_target_pairs={{0,64},{64,0},{1,65},{65,1},{2,66},{66,2},{3,67},{67,3},{4,68},{68... | collective-permute-start | bytes 393224 | tf_op jit(solution)/shard_map/ppermute | solution.py:161
  36.6 2.4 %collective-permute-done.3 = bf16[2,2,2,64,128]{4,3,2,1,0:T(8,128)(2,1)S(1)} collective-permute-done((bf16[2,2,2,64,128]{4,3,2,1,0:T(8,128)(2,1)S(1)}, bf16[2,2,2,64,128]{4,3,2,1,0:T(8,128)(2,1)S(1)}, u32[]{:S(2)}, u32[]{:S(2)}) %collective-permute-start.3) | collective-permute-done | bytes 131104 | tf_op jit(solution)/shard_map/ppermute | solution.py:161
  40.2 0.7 copy.38
  40.9 8.0 %all-to-all-start.1 = ((bf16[8,64,128]{2,1,0:T(8,128)(2,1)}), bf16[8,64,128]{2,1,0:T(8,128)(2,1)S(1)}, u32[]{:S(2)}, u32[]{:S(2)}) async-start(bf16[8,64,128]{2,1,0:T(8,128)(2,1)} %bitcast.17), calls=%async_computation.1 | async-start | bytes 262144 | tf_op jit(solution)/shard_map/all_to_all | solution.py:31
  49.0 5.1 %all-to-all-done.1 = bf16[8,64,128]{2,1,0:T(8,128)(2,1)S(1)} async-done(((bf16[8,64,128]{2,1,0:T(8,128)(2,1)}), bf16[8,64,128]{2,1,0:T(8,128)(2,1)S(1)}, u32[]{:S(2)}, u32[]{:S(2)}) %all-to-all-start.1) | async-done | bytes 131104 | tf_op jit(solution)/shard_map/all_to_all | solution.py:31
  54.5 4.2 %all_to_all.60 = bf16[2,1088,128]{2,1,0:T(8,128)(2,1)S(1)} all-to-all(bf16[2,1088,128]{2,1,0:T(8,128)(2,1)S(1)} %bitcast.92), channel_id=1, replica_groups=mesh['p'=4,'yl'=2,'zl'=4,'c'=2,'zh'=2,'x'=4] {'c'}, dimensions={0} | all-to-all | bytes 1114112 | tf_op jit(solution)/shard_map/all_to_all | solution.py:31
  58.8 14.3 %all_to_all.61 = bf16[8,152,128]{2,1,0:T(8,128)(2,1)S(1)} all-to-all(bf16[8,152,128]{2,1,0:T(8,128)(2,1)S(1)} %pad_maximum_fusion.1), channel_id=1, replica_groups=mesh['p'=4,'yl'=2,'zl'=4,'c'=2,'zh'=2,'x'=4] {'zl','zh'}, dimensions={0} | all-to-all | bytes 622592 | tf_op jit(solution)/shard_map/all_to_all | solution.py:31
  73.9 3.3 %all-to-all-start.4 = ((bf16[4,120,128]{2,1,0:T(8,128)(2,1)}), bf16[4,120,128]{2,1,0:T(8,128)(2,1)S(1)}, u32[]{:S(2)}, u32[]{:S(2)}) async-start(bf16[4,120,128]{2,1,0:T(8,128)(2,1)} %broadcast_in_dim.17), calls=%async_computation.4 | async-start | bytes 245760 | tf_op jit(solution)/shard_map/all_to_all | solution.py:31
  77.4 4.6 %all-to-all-done.4 = bf16[4,120,128]{2,1,0:T(8,128)(2,1)S(1)} async-done(((bf16[4,120,128]{2,1,0:T(8,128)(2,1)}), bf16[4,120,128]{2,1,0:T(8,128)(2,1)S(1)}, u32[]{:S(2)}, u32[]{:S(2)}) %all-to-all-start.4) | async-done | bytes 122912 | tf_op jit(solution)/shard_map/all_to_all | solution.py:31
  82.0 15.9 %all_to_all.62 = bf16[8,120,128]{2,1,0:T(8,128)(2,1)} all-to-all(bf16[8,120,128]{2,1,0:T(8,128)(2,1)S(1)} %broadcast_in_dim.18), channel_id=1, replica_groups=mesh['p'=4,'yl'=2,'zl'=4,'c'=2,'zh'=2,'x'=4] {'p','yl'}, dimensions={0} | all-to-all | bytes 491520 | tf_op jit(solution)/shard_map/all_to_all | solution.py:31
  97.9 1.9 shard_map.133
  99.8 7.3 %collective-permute-start.4 = (bf16[128,128]{1,0:T(8,128)(2,1)}, bf16[128,128]{1,0:T(8,128)(2,1)S(1)}, u32[]{:S(2)}, u32[]{:S(2)}) collective-permute-start(bf16[128,128]{1,0:T(8,128)(2,1)} %shard_map.133), channel_id=1, source_target_pairs={{0,8},{8,0},{1,9},{9,1},{2,10},{10,2},{3,11},{11,3},{4,12},{12,4},... | collective-permute-start | bytes 98312 | tf_op jit(solution)/shard_map/ppermute | solution.py:149
  107.2 1.0 collective-permute-done.4
  108.2 0.8 add_convert_fusion.1
  109.7 3.4 %all-to-all-start.6 = ((bf16[8,128,128]{2,1,0:T(8,128)(2,1)}), bf16[8,128,128]{2,1,0:T(8,128)(2,1)S(1)}, u32[]{:S(2)}, u32[]{:S(2)}) async-start(bf16[8,128,128]{2,1,0:T(8,128)(2,1)} %broadcast_in_dim.19), calls=%async_computation.6 | async-start | bytes 524288 | tf_op jit(solution)/shard_map/all_to_all | solution.py:31
  113.3 6.9 %all-to-all-done.6 = bf16[8,128,128]{2,1,0:T(8,128)(2,1)S(1)} async-done(((bf16[8,128,128]{2,1,0:T(8,128)(2,1)}), bf16[8,128,128]{2,1,0:T(8,128)(2,1)S(1)}, u32[]{:S(2)}, u32[]{:S(2)}) %all-to-all-start.6) | async-done | bytes 262176 | tf_op jit(solution)/shard_map/all_to_all | solution.py:31
  120.7 6.7 %all_to_all.63 = bf16[4,48,128]{2,1,0:T(8,128)(2,1)S(1)} all-to-all(bf16[4,48,128]{2,1,0:T(8,128)(2,1)S(1)} %bitcast.118), channel_id=1, replica_groups=mesh['p'=4,'yl'=2,'zl'=4,'c'=2,'zh'=2,'x'=4] {'x'}, dimensions={0} | all-to-all | bytes 98304 | tf_op jit(solution)/shard_map/all_to_all | solution.py:31
  127.5 10.0 %all_to_all.64 = bf16[8,48,128]{2,1,0:T(8,128)(2,1)S(1)} all-to-all(bf16[8,48,128]{2,1,0:T(8,128)(2,1)S(1)} %broadcast_in_dim.20), channel_id=1, replica_groups=mesh['p'=4,'yl'=2,'zl'=4,'c'=2,'zh'=2,'x'=4] {'p','yl'}, dimensions={0} | all-to-all | bytes 196608 | tf_op jit(solution)/shard_map/all_to_all | solution.py:31
  137.5 19.2 %all_to_all.65 = bf16[32,48,128]{2,1,0:T(8,128)(2,1)S(1)} all-to-all(bf16[32,48,128]{2,1,0:T(8,128)(2,1)S(1)} %broadcast_in_dim.21), channel_id=1, replica_groups=mesh['p'=4,'yl'=2,'zl'=4,'c'=2,'zh'=2,'x'=4] {'zl','zh','x'}, dimensions={0} | all-to-all | bytes 786432 | tf_op jit(solution)/shard_map/all_to_all | solution.py:31
  156.8 6.9 %collective-permute-start.5 = (bf16[32,48,128]{2,1,0:T(8,128)(2,1)S(1)}, bf16[32,48,128]{2,1,0:T(8,128)(2,1)S(1)}, u32[]{:S(2)}, u32[]{:S(2)}) collective-permute-start(bf16[32,48,128]{2,1,0:T(8,128)(2,1)S(1)} %all_to_all.65), channel_id=1, source_target_pairs={{0,8},{8,0},{1,9},{9,1},{2,10},{10,2},{3,11},{11,3},{4,12},{12,4},... | collective-permute-start | bytes 1179656 | tf_op jit(solution)/shard_map/ppermute | solution.py:149
  166.4 7.9 %all_to_all.66 = bf16[8,64,128]{2,1,0:T(8,128)(2,1)S(1)} all-to-all(bf16[8,64,128]{2,1,0:T(8,128)(2,1)S(1)} %broadcast_in_dim.22), channel_id=1, replica_groups=mesh['p'=4,'yl'=2,'zl'=4,'c'=2,'zh'=2,'x'=4] {'c','x'}, dimensions={0} | all-to-all | bytes 262144 | tf_op jit(solution)/shard_map/all_to_all | solution.py:31
  174.7 0.8 copy.44
  175.6 3.5 %all-to-all-start.11 = ((bf16[16,64,128]{2,1,0:T(8,128)(2,1)}), bf16[16,64,128]{2,1,0:T(8,128)(2,1)S(1)}, u32[]{:S(2)}, u32[]{:S(2)}) async-start(bf16[16,64,128]{2,1,0:T(8,128)(2,1)} %bitcast.51), calls=%async_computation.11 | async-start | bytes 524288 | tf_op jit(solution)/shard_map/all_to_all | solution.py:31
  179.7 9.6 %all-to-all-done.11 = bf16[16,64,128]{2,1,0:T(8,128)(2,1)S(1)} async-done(((bf16[16,64,128]{2,1,0:T(8,128)(2,1)}), bf16[16,64,128]{2,1,0:T(8,128)(2,1)S(1)}, u32[]{:S(2)}, u32[]{:S(2)}) %all-to-all-start.11) | async-done | bytes 262176 | tf_op jit(solution)/shard_map/all_to_all | solution.py:31
  (79 shorter events, 8.6 us)
Async XLA Ops:
  0.6 21.5 %collective-permute-start = (bf16[64,128]{1,0:T(8,128)(2,1)}, bf16[64,128]{1,0:T(8,128)(2,1)S(1)}, u32[]{:S(2)}, u32[]{:S(2)}) collective-permute-start(bf16[64,128]{1,0:T(8,128)(2,1)} %bitcast.119), channel_id=1, source_target_pairs={{0,4},{4,0},{1,5},{5,1},{2,6},{6,2},{3,7},{7,3},{8,12},{12,8},{9,1... | collective-permute-start | bytes 49160 | tf_op jit(solution)/shard_map/ppermute | solution.py:161
  14.8 5.4 %copy-start.2 = (bf16[1,1536,64]{1,2,0:T(8,128)(2,1)S(1)}, bf16[1,1536,64]{1,2,0:T(8,128)(2,1)}, u32[]{:S(2)}) copy-start(bf16[1,1536,64]{1,2,0:T(8,128)(2,1)} %param.14) | copy-start | bytes 589828
  14.8 7.3 %copy-start.4 = (bf16[1,64,128]{2,1,0:T(8,128)(2,1)S(1)}, bf16[1,64,128]{2,1,0:T(8,128)(2,1)}, u32[]{:S(2)}) copy-start(bf16[1,64,128]{2,1,0:T(8,128)(2,1)} %param.12) | copy-start | bytes 49156
  14.8 24.3 %all-to-all-start = ((bf16[8,64,1024]{2,1,0:T(8,128)(2,1)}), bf16[8,64,1024]{2,1,0:T(8,128)(2,1)S(1)}, u32[]{:S(2)}, u32[]{:S(2)}) async-start(bf16[8,64,1024]{2,1,0:T(8,128)(2,1)} %shard_map.131), calls=%async_computation | async-start | bytes 2097152 | tf_op jit(solution)/shard_map/all_to_all | solution.py:31
  22.1 5.9 %collective-permute-start.1 = (bf16[2,64,128]{2,1,0:T(8,128)(2,1)S(1)}, bf16[2,64,128]{2,1,0:T(8,128)(2,1)S(1)}, u32[]{:S(2)}, u32[]{:S(2)}) collective-permute-start(bf16[2,64,128]{2,1,0:T(8,128)(2,1)S(1)} %maximum_select_fusion.6), channel_id=1, source_target_pairs={{0,32},{16,48},{32,0},{48,16},{1,33},{17,49},{33,1},{49,17},{2,34}... | collective-permute-start | bytes 98312 | tf_op jit(solution)/shard_map/ppermute | solution.py:161
  28.0 5.3 %collective-permute-start.2 = (bf16[2,2,64,128]{3,2,1,0:T(8,128)(2,1)S(1)}, bf16[2,2,64,128]{3,2,1,0:T(8,128)(2,1)S(1)}, u32[]{:S(2)}, u32[]{:S(2)}) collective-permute-start(bf16[2,2,64,128]{3,2,1,0:T(8,128)(2,1)S(1)} %maximum_select_fusion.4), channel_id=1, source_target_pairs={{0,16},{16,0},{32,48},{48,32},{1,17},{17,1},{33,49},{49,33},{2,18}... | collective-permute-start | bytes 196616 | tf_op jit(solution)/shard_map/ppermute | solution.py:161
  33.3 5.7 %collective-permute-start.3 = (bf16[2,2,2,64,128]{4,3,2,1,0:T(8,128)(2,1)S(1)}, bf16[2,2,2,64,128]{4,3,2,1,0:T(8,128)(2,1)S(1)}, u32[]{:S(2)}, u32[]{:S(2)}) collective-permute-start(bf16[2,2,2,64,128]{4,3,2,1,0:T(8,128)(2,1)S(1)} %maximum_select_fusion.2), channel_id=1, source_target_pairs={{0,64},{64,0},{1,65},{65,1},{2,66},{66,2},{3,67},{67,3},{4,68},{68... | collective-permute-start | bytes 393224 | tf_op jit(solution)/shard_map/ppermute | solution.py:161
  40.1 14.1 %copy-start.5 = (bf16[6,128]{1,0:T(8,128)(2,1)S(1)}, bf16[6,128]{1,0:T(8,128)(2,1)}, u32[]{:S(2)}) copy-start(bf16[6,128]{1,0:T(8,128)(2,1)} %param.19) | copy-start | bytes 4612
  40.9 13.2 %all-to-all-start.1 = ((bf16[8,64,128]{2,1,0:T(8,128)(2,1)}), bf16[8,64,128]{2,1,0:T(8,128)(2,1)S(1)}, u32[]{:S(2)}, u32[]{:S(2)}) async-start(bf16[8,64,128]{2,1,0:T(8,128)(2,1)} %bitcast.17), calls=%async_computation.1 | async-start | bytes 262144 | tf_op jit(solution)/shard_map/all_to_all | solution.py:31
  48.9 5.5 %copy-start.3 = (bf16[16,2,8,128]{3,2,1,0:T(8,128)(2,1)S(1)}, bf16[16,2,8,128]{3,2,1,0:T(8,128)(2,1)}, u32[]{:S(2)}) copy-start(bf16[16,2,8,128]{3,2,1,0:T(8,128)(2,1)} %shard_map.132) | copy-start | bytes 196612
  73.1 24.8 %copy-start = (bf16[8,32,128]{2,1,0:T(8,128)(2,1)}, bf16[8,32,128]{2,1,0:T(8,128)(2,1)S(1)}, u32[]{:S(2)}) copy-start(bf16[8,32,128]{2,1,0:T(8,128)(2,1)S(1)} %slice.51) | copy-start | bytes 196612
  73.9 8.1 %all-to-all-start.4 = ((bf16[4,120,128]{2,1,0:T(8,128)(2,1)}), bf16[4,120,128]{2,1,0:T(8,128)(2,1)S(1)}, u32[]{:S(2)}, u32[]{:S(2)}) async-start(bf16[4,120,128]{2,1,0:T(8,128)(2,1)} %broadcast_in_dim.17), calls=%async_computation.4 | async-start | bytes 245760 | tf_op jit(solution)/shard_map/all_to_all | solution.py:31
  97.9 22.5 %copy-start.1 = (bf16[8,32,128]{2,1,0:T(8,128)(2,1)S(1)}, bf16[8,32,128]{2,1,0:T(8,128)(2,1)}, u32[]{:S(2)}) copy-start(bf16[8,32,128]{2,1,0:T(8,128)(2,1)} %copy-done) | copy-start | bytes 196612
  99.8 8.4 %collective-permute-start.4 = (bf16[128,128]{1,0:T(8,128)(2,1)}, bf16[128,128]{1,0:T(8,128)(2,1)S(1)}, u32[]{:S(2)}, u32[]{:S(2)}) collective-permute-start(bf16[128,128]{1,0:T(8,128)(2,1)} %shard_map.133), channel_id=1, source_target_pairs={{0,8},{8,0},{1,9},{9,1},{2,10},{10,2},{3,11},{11,3},{4,12},{12,4},... | collective-permute-start | bytes 98312 | tf_op jit(solution)/shard_map/ppermute | solution.py:149
  109.7 10.5 %all-to-all-start.6 = ((bf16[8,128,128]{2,1,0:T(8,128)(2,1)}), bf16[8,128,128]{2,1,0:T(8,128)(2,1)S(1)}, u32[]{:S(2)}, u32[]{:S(2)}) async-start(bf16[8,128,128]{2,1,0:T(8,128)(2,1)} %broadcast_in_dim.19), calls=%async_computation.6 | async-start | bytes 524288 | tf_op jit(solution)/shard_map/all_to_all | solution.py:31
  120.3 43.4 %copy-start.7 = (f32[1,32]{1,0:T(1,128)S(1)}, f32[1,32]{1,0:T(1,128)}, u32[]{:S(2)}) copy-start(f32[1,32]{1,0:T(1,128)} %param.17) | copy-start | bytes 388
  120.3 43.4 %copy-start.8 = (s32[1,32]{1,0:T(1,128)S(1)}, s32[1,32]{1,0:T(1,128)}, u32[]{:S(2)}) copy-start(s32[1,32]{1,0:T(1,128)} %param.18) | copy-start | bytes 388
  156.8 8.3 %collective-permute-start.5 = (bf16[32,48,128]{2,1,0:T(8,128)(2,1)S(1)}, bf16[32,48,128]{2,1,0:T(8,128)(2,1)S(1)}, u32[]{:S(2)}, u32[]{:S(2)}) collective-permute-start(bf16[32,48,128]{2,1,0:T(8,128)(2,1)S(1)} %all_to_all.65), channel_id=1, source_target_pairs={{0,8},{8,0},{1,9},{9,1},{2,10},{10,2},{3,11},{11,3},{4,12},{12,4},... | collective-permute-start | bytes 1179656 | tf_op jit(solution)/shard_map/ppermute | solution.py:149
  165.4 0.8 copy-start.6
  175.6 13.7 %all-to-all-start.11 = ((bf16[16,64,128]{2,1,0:T(8,128)(2,1)}), bf16[16,64,128]{2,1,0:T(8,128)(2,1)S(1)}, u32[]{:S(2)}, u32[]{:S(2)}) async-start(bf16[16,64,128]{2,1,0:T(8,128)(2,1)} %bitcast.51), calls=%async_computation.11 | async-start | bytes 524288 | tf_op jit(solution)/shard_map/all_to_all | solution.py:31
